TPU v7x, 32 devices: a whole 2x2x4 slice. The times are simulated.
32 devices in a mesh: seq: 4 (over y, x), fsdp: 8 (over z, core).
Axes of the slice: x: 2, y: 2, z: 4, core: 2. Of those that a mesh axis runs over, the one named last changes fastest.
Arguments:
- tokens: bfloat16 [8, 1280, 1536], P('fsdp', 'seq'), may hold values from -6 to 6
- conditioning: bfloat16 [8, 2, 130, 1536], P('fsdp'), may hold values from -6 to 6
- lengths: int32 [8, 2], P('fsdp'), may hold values from 1 to 1024, 1280 in all within a row
- grad_output: bfloat16 [8, 1280, 1536], P('fsdp', 'seq'), may hold values from -6 to 6
- norm_first: bfloat16 [1536], P(('seq', 'fsdp')), may hold values from 0.099609375 to 1.8984375
- proj_self: bfloat16 [1536, 4608], P(('seq', 'fsdp')), may hold values from -0.15625 to 0.15625
- out_self: bfloat16 [1536, 1536], P(('seq', 'fsdp')), may hold values from -2.5 to 2.5
- norm_second: bfloat16 [1536], P(('seq', 'fsdp')), may hold values from 0.099609375 to 1.8984375
- proj_query: bfloat16 [1536, 1536], P(('seq', 'fsdp')), may hold values from -0.15625 to 0.15625
- proj_keyval: bfloat16 [1536, 3072], P(('seq', 'fsdp')), may hold values from -0.15625 to 0.15625
- out_cross: bfloat16 [1536, 1536], P(('seq', 'fsdp')), may hold values from -1.25 to 1.25
- norm_third: bfloat16 [1536], P(('seq', 'fsdp')), may hold values from 0.099609375 to 1.8984375
- proj_gateup: bfloat16 [1536, 12288], P(('seq', 'fsdp')), may hold values from -0.15625 to 0.15625
- bias_gateup: bfloat16 [12288], P(('seq', 'fsdp')), may hold values from -3 to 3
- proj_down: bfloat16 [6144, 1536], P(('seq', 'fsdp')), may hold values from -0.078125 to 0.078125
- bias_down: bfloat16 [1536], P(('seq', 'fsdp')), may hold values from -3 to 3
Outputs:
- layer_out: bfloat16 [8, 1280, 1536], P('fsdp', 'seq')
- grad_tokens: float32 [8, 1280, 1536], P('fsdp', 'seq')
- grad_cond: float32 [8, 2, 130, 1536], P('fsdp')
- grad_norm_first: float32 [1536], P(('seq', 'fsdp'))
- grad_proj_self: float32 [1536, 4608], P(('seq', 'fsdp'))
- grad_out_self: float32 [1536, 1536], P(('seq', 'fsdp'))
- grad_norm_second: float32 [1536], P(('seq', 'fsdp'))
- grad_proj_query: float32 [1536, 1536], P(('seq', 'fsdp'))
- grad_proj_keyval: float32 [1536, 3072], P(('seq', 'fsdp'))
- grad_out_cross: float32 [1536, 1536], P(('seq', 'fsdp'))
- grad_norm_third: float32 [1536], P(('seq', 'fsdp'))
- grad_proj_gateup: float32 [1536, 12288], P(('seq', 'fsdp'))
- grad_bias_gateup: float32 [12288], P(('seq', 'fsdp'))
- grad_proj_down: float32 [6144, 1536], P(('seq', 'fsdp'))
- grad_bias_down: float32 [1536], P(('seq', 'fsdp'))
Inputs may be any that keep to these rules, and one draw needn't show every extreme that they name: Each row of lengths holds the lengths of the 2 sequences of one group, which sum to 1280; the largest in each row is at most 1024.
All inputs are finite; a program needn't handle non-finite values.
Results may differ from a plain program's by a relative error of at most 0.028.
Values may be sent and summed in bfloat16 or wider, within the bound.
No kernel may reach another device: no remote copies, remote signals or barrier semaphores. Data moves between devices by JAX's collectives and lax.ppermute only.
A program may use at most 576 MiB of HBM per device.

v0:
```python
import math

import jax
import jax.numpy as jnp
from jax import lax
from jax.sharding import PartitionSpec as P

D = 1536
HEADS = 24
HEAD = 64
FF = 6144
COND = 130
SEQS_GRP = 2


epsilon = 1e-05
masked_score = -1e30


def seq_info(global_rows, group_lengths):
    ends = jnp.cumsum(group_lengths)
    starts = ends - group_lengths
    ident = jnp.sum((global_rows[:, None] >= ends[None, :]).astype(jnp.int32), axis=1)
    onehot = ident[:, None] == jnp.arange(group_lengths.shape[0], dtype=jnp.int32)[None, :]
    begin = jnp.sum(jnp.where(onehot, starts[None, :], 0), axis=1)
    return (ident, (global_rows - begin).astype(jnp.float32))


def angles(positions):
    half = HEAD // 2
    inverse = jnp.power(10000.0, -jnp.arange(half, dtype=jnp.float32) / half)
    turned = positions[:, None] * inverse[None, :]
    return (jnp.cos(turned), jnp.sin(turned))


def rotate(vector, cosine, sine):
    half = vector.shape[-1] // 2
    first_half = vector[..., :half]
    second_half = vector[..., half:]
    cos_rows = cosine[:, None, :]
    sin_rows = sine[:, None, :]
    return jnp.concatenate(
        [
            first_half * cos_rows - second_half * sin_rows,
            second_half * cos_rows + first_half * sin_rows,
        ],
        axis=-1,
    )


def norm_rows(values, gain):
    centre = values - jnp.mean(values, axis=-1, keepdims=True)
    spread = jnp.mean(centre * centre, axis=-1, keepdims=True)
    scaled = lax.rsqrt(spread + epsilon)
    normal = centre * scaled
    return (normal, scaled, normal * gain)


def norm_back(grad_rows, normal, scaled, gain):
    weighted = grad_rows * gain
    mean_one = jnp.mean(weighted, axis=-1, keepdims=True)
    mean_two = jnp.mean(weighted * normal, axis=-1, keepdims=True)
    return (scaled * (weighted - mean_one - normal * mean_two), jnp.sum(grad_rows * normal, axis=0))


def outer_sum(left, right):
    return lax.dot_general(
        left, right, (((0,), (0,)), ((), ())), preferred_element_type=jnp.float32
    )


def back_prod(left, weight):
    return lax.dot_general(
        left, weight, (((1,), (1,)), ((), ())), preferred_element_type=jnp.float32
    )


def shards(
    tokens,
    conditioning,
    lengths,
    grad_output,
    norm_first,
    proj_self,
    out_self,
    norm_second,
    proj_query,
    proj_keyval,
    out_cross,
    norm_third,
    proj_gateup,
    bias_gateup,
    proj_down,
    bias_down,
):
    bf16 = jnp.bfloat16
    f32 = jnp.float32
    rows = tokens.shape[1]
    group = rows * lax.axis_size("seq")
    group_lengths = lengths[0]
    my_rows = lax.axis_index("seq") * rows + jnp.arange(rows, dtype=jnp.int32)
    my_ids, my_pos = seq_info(my_rows, group_lengths)
    cosine, sine = angles(my_pos)
    attn_set = (
        lax.all_gather(norm_first, ("seq", "fsdp"), axis=0, tiled=True),
        lax.all_gather(proj_self, ("seq", "fsdp"), axis=0, tiled=True),
        lax.all_gather(out_self, ("seq", "fsdp"), axis=0, tiled=True),
        lax.all_gather(norm_second, ("seq", "fsdp"), axis=0, tiled=True),
        lax.all_gather(proj_query, ("seq", "fsdp"), axis=0, tiled=True),
        lax.all_gather(proj_keyval, ("seq", "fsdp"), axis=0, tiled=True),
        lax.all_gather(out_cross, ("seq", "fsdp"), axis=0, tiled=True),
    )
    gain_one, w_self, w_out, gain_two, w_query, w_keyval, w_cross = attn_set
    inputs = tokens[0].astype(f32)
    normal_one, scaled_one, normed = norm_rows(inputs, gain_one.astype(f32))
    normed_one = normed.astype(bf16)
    packed = jnp.dot(normed_one, w_self, preferred_element_type=f32)
    queries = rotate(packed[:, :D].reshape(rows, HEADS, HEAD), cosine, sine).astype(bf16)
    keys = rotate(packed[:, D : 2 * D].reshape(rows, HEADS, HEAD), cosine, sine).astype(bf16)
    values = packed[:, 2 * D :].reshape(rows, HEADS, HEAD).astype(bf16)
    start_state = (
        jnp.full((HEADS, rows), masked_score, f32),
        jnp.zeros((HEADS, rows), f32),
        jnp.zeros((rows, HEADS, HEAD), f32),
    )
    carry = start_state
    key_piece = lax.all_gather(keys, "seq", axis=0, tiled=True)
    value_piece = lax.all_gather(values, "seq", axis=0, tiled=True)
    count = key_piece.shape[0]
    step = math.gcd(count, 512)

    def inner(state, index):
        running, total, accum = state
        key_block = lax.dynamic_slice_in_dim(key_piece, index * step, step, 0)
        value_block = lax.dynamic_slice_in_dim(value_piece, index * step, step, 0)
        key_ids, _ = seq_info(index * step + jnp.arange(step, dtype=jnp.int32), group_lengths)
        allowed = (my_ids[:, None] == key_ids[None, :])[None]
        scores = jnp.einsum("qhd,khd->hqk", queries, key_block, preferred_element_type=f32) * 0.125
        scores = jnp.where(allowed, scores, masked_score)
        newer = jnp.maximum(running, jnp.max(scores, axis=-1))
        expo = jnp.where(allowed, jnp.exp(scores - newer[..., None]), 0.0)
        factor = jnp.exp(running - newer)
        total = total * factor + jnp.sum(expo, axis=-1)
        accum = accum * factor.T[:, :, None] + jnp.einsum(
            "hqk,khd->qhd", expo.astype(bf16), value_block, preferred_element_type=f32
        )
        return ((newer, total, accum), None)

    carry, _ = lax.scan(inner, carry, jnp.arange(count // step))
    running, total, accum = carry
    attn_full = accum / total.T[:, :, None]
    mixed = attn_full.reshape(rows, D).astype(bf16)
    first = inputs + jnp.dot(mixed, w_out, preferred_element_type=f32)
    normal_two, scaled_two, normed = norm_rows(first, gain_two.astype(f32))
    normed_two = normed.astype(bf16)
    cross_query = (
        jnp.dot(normed_two, w_query, preferred_element_type=f32)
        .astype(bf16)
        .reshape(rows, HEADS, HEAD)
    )
    cond_rows = conditioning[0].reshape(SEQS_GRP * COND, D)
    count = SEQS_GRP * COND
    keyval = jnp.dot(cond_rows, w_keyval, preferred_element_type=f32).astype(bf16)
    cross_keys = keyval[:, :D].reshape(count, HEADS, HEAD)
    cross_values = keyval[:, D:].reshape(count, HEADS, HEAD)
    cond_ids = jnp.arange(count, dtype=jnp.int32) // COND
    cross_allowed = (my_ids[:, None] == cond_ids[None, :])[None]
    cross_scores = (
        jnp.einsum("qhd,khd->hqk", cross_query, cross_keys, preferred_element_type=f32) * 0.125
    )
    cross_scores = jnp.where(cross_allowed, cross_scores, masked_score)
    cross_top = jnp.max(cross_scores, axis=-1, keepdims=True)
    cross_expo = jnp.where(cross_allowed, jnp.exp(cross_scores - cross_top), 0.0)
    cross_probs = cross_expo / jnp.sum(cross_expo, axis=-1, keepdims=True)
    cross_low = cross_probs.astype(bf16)
    cross_mixed = (
        jnp.einsum("hqk,khd->qhd", cross_low, cross_values, preferred_element_type=f32)
        .reshape(rows, D)
        .astype(bf16)
    )
    second = first + jnp.dot(cross_mixed, w_cross, preferred_element_type=f32)
    mlp_set = (
        lax.all_gather(norm_third, ("seq", "fsdp"), axis=0, tiled=True),
        lax.all_gather(proj_gateup, ("seq", "fsdp"), axis=0, tiled=True),
        lax.all_gather(bias_gateup, ("seq", "fsdp"), axis=0, tiled=True),
        lax.all_gather(proj_down, ("seq", "fsdp"), axis=0, tiled=True),
        lax.all_gather(bias_down, ("seq", "fsdp"), axis=0, tiled=True),
    )
    gain_three, w_gateup, b_gateup, w_down, b_down = mlp_set
    normal_three, scaled_three, normed = norm_rows(second, gain_three.astype(f32))
    normed_three = normed.astype(bf16)
    gateup = jnp.dot(normed_three, w_gateup, preferred_element_type=f32) + b_gateup.astype(f32)
    gate = gateup[:, :FF]
    upper = gateup[:, FF:]
    sigma = jax.nn.sigmoid(gate)
    silu_gate = gate * sigma
    active = (silu_gate * upper).astype(bf16)
    result = second + jnp.dot(active, w_down, preferred_element_type=f32) + b_down.astype(f32)
    back_mlp = (
        lax.all_gather(norm_third, ("seq", "fsdp"), axis=0, tiled=True),
        lax.all_gather(proj_gateup, ("seq", "fsdp"), axis=0, tiled=True),
        lax.all_gather(proj_down, ("seq", "fsdp"), axis=0, tiled=True),
    )
    gain_three, w_gateup, w_down = back_mlp
    back_attn = (
        lax.all_gather(norm_first, ("seq", "fsdp"), axis=0, tiled=True),
        lax.all_gather(proj_self, ("seq", "fsdp"), axis=0, tiled=True),
        lax.all_gather(out_self, ("seq", "fsdp"), axis=0, tiled=True),
        lax.all_gather(norm_second, ("seq", "fsdp"), axis=0, tiled=True),
        lax.all_gather(proj_query, ("seq", "fsdp"), axis=0, tiled=True),
        lax.all_gather(proj_keyval, ("seq", "fsdp"), axis=0, tiled=True),
        lax.all_gather(out_cross, ("seq", "fsdp"), axis=0, tiled=True),
    )
    gain_one, w_self, w_out, gain_two, w_query, w_keyval, w_cross = back_attn
    grad_rows = grad_output[0].astype(f32)
    grad_low = grad_output[0]
    grad_b_down = jnp.sum(grad_low.astype(f32), axis=0)
    grad_w_down = outer_sum(active, grad_low)
    grad_active = back_prod(grad_low, w_down)
    grad_gate = grad_active * upper * sigma * (1.0 + gate * (1.0 - sigma))
    grad_upper = grad_active * silu_gate
    grad_gateup = jnp.concatenate([grad_gate, grad_upper], axis=1).astype(bf16)
    grad_b_gateup = jnp.sum(grad_gateup.astype(f32), axis=0)
    grad_w_gateup = outer_sum(normed_three, grad_gateup)
    through, grad_gain_three = norm_back(
        back_prod(grad_gateup, w_gateup), normal_three, scaled_three, gain_three.astype(f32)
    )
    grad_second = grad_rows + through
    mlp_grads = (
        lax.psum_scatter(grad_gain_three, ("seq", "fsdp"), scatter_dimension=0, tiled=True),
        lax.psum_scatter(grad_w_gateup, ("seq", "fsdp"), scatter_dimension=0, tiled=True),
        lax.psum_scatter(grad_b_gateup, ("seq", "fsdp"), scatter_dimension=0, tiled=True),
        lax.psum_scatter(grad_w_down, ("seq", "fsdp"), scatter_dimension=0, tiled=True),
        lax.psum_scatter(grad_b_down, ("seq", "fsdp"), scatter_dimension=0, tiled=True),
    )
    second_low = grad_second.astype(bf16)
    grad_w_cross = outer_sum(cross_mixed, second_low)
    grad_cmix = back_prod(second_low, w_cross).astype(bf16).reshape(rows, HEADS, HEAD)
    cross_dp = jnp.einsum("qhd,khd->hqk", grad_cmix, cross_values, preferred_element_type=f32)
    cross_dv = jnp.einsum("hqk,qhd->khd", cross_low, grad_cmix, preferred_element_type=f32)
    cross_ds = (
        cross_probs * (cross_dp - jnp.sum(cross_probs * cross_dp, axis=-1, keepdims=True))
    ).astype(bf16)
    grad_cquery = (
        (jnp.einsum("hqk,khd->qhd", cross_ds, cross_keys, preferred_element_type=f32) * 0.125)
        .astype(bf16)
        .reshape(rows, D)
    )
    cross_dk = jnp.einsum("hqk,qhd->khd", cross_ds, cross_query, preferred_element_type=f32) * 0.125
    partial_kv = jnp.concatenate([cross_dk.reshape(count, D), cross_dv.reshape(count, D)], axis=1)
    grad_keyval = lax.psum(partial_kv.astype(jnp.bfloat16), "seq").astype(jnp.float32).astype(bf16)
    grad_cond = back_prod(grad_keyval, w_keyval).reshape(1, SEQS_GRP, COND, D)
    columns = 2 * D // lax.axis_size("seq")
    column_start = lax.axis_index("seq") * columns
    keyval_part = lax.dynamic_slice_in_dim(grad_keyval, column_start, columns, 1)
    grad_w_keyval = lax.dynamic_update_slice_in_dim(
        jnp.zeros((D, 2 * D), f32), outer_sum(cond_rows, keyval_part), column_start, 1
    )
    grad_w_query = outer_sum(normed_two, grad_cquery)
    through, grad_gain_two = norm_back(
        back_prod(grad_cquery, w_query), normal_two, scaled_two, gain_two.astype(f32)
    )
    grad_first = grad_second + through
    first_low = grad_first.astype(bf16)
    grad_w_out = outer_sum(mixed, first_low)
    grad_mixed = back_prod(first_low, w_out).astype(bf16).reshape(rows, HEADS, HEAD)
    delta = jnp.sum(grad_mixed.astype(f32) * attn_full, axis=-1).T
    keys_all, values_all = (
        lax.all_gather(keys, "seq", axis=0, tiled=True),
        lax.all_gather(values, "seq", axis=0, tiled=True),
    )
    block = math.gcd(group, 512)

    def back_block(grad_query, index):
        key_block = lax.dynamic_slice_in_dim(keys_all, index * block, block, 0)
        value_block = lax.dynamic_slice_in_dim(values_all, index * block, block, 0)
        key_ids, _ = seq_info(index * block + jnp.arange(block, dtype=jnp.int32), group_lengths)
        allowed = (my_ids[:, None] == key_ids[None, :])[None]
        scores = jnp.einsum("qhd,khd->hqk", queries, key_block, preferred_element_type=f32) * 0.125
        probs = jnp.where(allowed, jnp.exp(scores - running[..., None]), 0.0) / total[..., None]
        grad_probs = jnp.einsum("qhd,khd->hqk", grad_mixed, value_block, preferred_element_type=f32)
        grad_values = jnp.einsum(
            "hqk,qhd->khd", probs.astype(bf16), grad_mixed, preferred_element_type=f32
        )
        grad_scores = (probs * (grad_probs - delta[..., None])).astype(bf16)
        grad_query = grad_query + jnp.einsum(
            "hqk,khd->qhd", grad_scores, key_block, preferred_element_type=f32
        )
        grad_keys = (
            jnp.einsum("hqk,qhd->khd", grad_scores, queries, preferred_element_type=f32) * 0.125
        )
        return (
            grad_query,
            jnp.concatenate([grad_keys.reshape(block, D), grad_values.reshape(block, D)], axis=1),
        )

    grad_query, grad_kv_all = lax.scan(
        back_block, jnp.zeros((rows, HEADS, HEAD), f32), jnp.arange(group // block)
    )
    grad_kv_mine = lax.psum_scatter(
        grad_kv_all.reshape(group, 2 * D).astype(jnp.bfloat16),
        "seq",
        scatter_dimension=0,
        tiled=True,
    ).astype(jnp.float32)
    grad_q_pre = rotate(grad_query * 0.125, cosine, -sine).reshape(rows, D)
    grad_k_pre = rotate(grad_kv_mine[:, :D].reshape(rows, HEADS, HEAD), cosine, -sine).reshape(
        rows, D
    )
    grad_packed = jnp.concatenate([grad_q_pre, grad_k_pre, grad_kv_mine[:, D:]], axis=1).astype(
        bf16
    )
    grad_w_self = outer_sum(normed_one, grad_packed)
    through, grad_gain_one = norm_back(
        back_prod(grad_packed, w_self), normal_one, scaled_one, gain_one.astype(f32)
    )
    grad_inputs = grad_first + through
    attn_grads = (
        lax.psum_scatter(grad_gain_one, ("seq", "fsdp"), scatter_dimension=0, tiled=True),
        lax.psum_scatter(grad_w_self, ("seq", "fsdp"), scatter_dimension=0, tiled=True),
        lax.psum_scatter(grad_w_out, ("seq", "fsdp"), scatter_dimension=0, tiled=True),
        lax.psum_scatter(grad_gain_two, ("seq", "fsdp"), scatter_dimension=0, tiled=True),
        lax.psum_scatter(grad_w_query, ("seq", "fsdp"), scatter_dimension=0, tiled=True),
        lax.psum_scatter(grad_w_keyval, ("seq", "fsdp"), scatter_dimension=0, tiled=True),
        lax.psum_scatter(grad_w_cross, ("seq", "fsdp"), scatter_dimension=0, tiled=True),
    )
    return (
        result.astype(bf16)[None],
        grad_inputs[None],
        grad_cond,
        attn_grads[0],
        attn_grads[1],
        attn_grads[2],
        attn_grads[3],
        attn_grads[4],
        attn_grads[5],
        attn_grads[6],
        mlp_grads[0],
        mlp_grads[1],
        mlp_grads[2],
        mlp_grads[3],
        mlp_grads[4],
    )


def solution(mesh):
    placed = (
        P("fsdp", "seq", None),
        P("fsdp", None, None, None),
        P("fsdp", None),
        P("fsdp", "seq", None),
        P(("seq", "fsdp")),
        P(("seq", "fsdp"), None),
        P(("seq", "fsdp"), None),
        P(("seq", "fsdp")),
        P(("seq", "fsdp"), None),
        P(("seq", "fsdp"), None),
        P(("seq", "fsdp"), None),
        P(("seq", "fsdp")),
        P(("seq", "fsdp"), None),
        P(("seq", "fsdp")),
        P(("seq", "fsdp"), None),
        P(("seq", "fsdp")),
    )
    return jax.shard_map(
        shards,
        mesh=mesh,
        in_specs=placed,
        out_specs=(
            P("fsdp", "seq", None),
            P("fsdp", "seq", None),
            P("fsdp", None, None, None),
            P(("seq", "fsdp")),
            P(("seq", "fsdp"), None),
            P(("seq", "fsdp"), None),
            P(("seq", "fsdp")),
            P(("seq", "fsdp"), None),
            P(("seq", "fsdp"), None),
            P(("seq", "fsdp"), None),
            P(("seq", "fsdp")),
            P(("seq", "fsdp"), None),
            P(("seq", "fsdp")),
            P(("seq", "fsdp"), None),
            P(("seq", "fsdp")),
        ),
        check_vma=False,
    )
```

profile of v0, /device:TPU:8, one launch (start us, length us, event | category | flops | bytes accessed | tf_op | source)
XLA Modules:
  0.0 3364.7 jit_solution(14988351149457536577)
XLA Ops:
  12.1 41.3 %all-reduce.10 = (bf16[1536]{0:T(1024)(128)(2,1)S(1)}, bf16[1536]{0:T(1024)(128)(2,1)S(1)}, bf16[1536]{0:T(1024)(128)(2,1)}, bf16[1536]{0:T(1024)(128)(2,1)}) all-reduce(bf16[1536]{0:T(1024)(128)(2,1)S(1)} %dynamic-update-slice, bf16[1536]{0:T(1024)(128)(2,1)S(1)} %dynamic-update-slice.1, ...), channel_id=1, replica_groups=mesh['seq'=4,'fsdp'=8] {'seq','fsdp'}, use_global_device_ids=true, to_apply=%add | all-reduce | flops 6144 | bytes 24576
  58.0 57.4 %all-gather.11.cloned.1.call-done = bf16[1536,4608]{1,0:T(8,128)(2,1)} async-done(((bf16[48,4608]{1,0:T(8,128)(2,1)}), bf16[1536,4608]{1,0:T(8,128)(2,1)}) %all-gather.11.cloned.1.call-update) | async-done | bytes 14155792 | tf_op jit(solution)/shard_map/all_gather | solution.py:106
  147.9 38.4 %all-gather = bf16[32,1,384]{2,1,0:T(2,128)(2,1)S(1)} all-gather(bf16[1,1,384]{2,1,0:T(2,128)(2,1)S(1)} %reshape.414), channel_id=1, replica_groups=mesh['seq'=4,'fsdp'=8] {'seq','fsdp'}, dimensions={0}, use_global_device_ids=true | all-gather | bytes 25344 | tf_op jit(solution)/shard_map/all_gather | solution.py:185
  209.4 74.6 %all-gather.13.cloned.1.call-done = bf16[1280,24,64]{2,1,0:T(8,128)(2,1)} async-done(((bf16[320,24,64]{2,1,0:T(8,128)(2,1)}), bf16[1280,24,64]{2,1,0:T(8,128)(2,1)}) %all-gather.13.cloned.1.call-update) | async-done | bytes 3932176 | tf_op jit(solution)/shard_map/all_gather | solution.py:127
  294.6 74.4 %all-gather.15.cloned.1.call-done = bf16[1280,24,64]{2,1,0:T(8,128)(2,1)} async-done(((bf16[320,24,64]{2,1,0:T(8,128)(2,1)}), bf16[1280,24,64]{2,1,0:T(8,128)(2,1)}) %all-gather.15.cloned.1.call-update) | async-done | bytes 3932176 | tf_op jit(solution)/shard_map/all_gather | solution.py:128
  379.6 92.6 %while.32 = (s32[]{:T(128)}, f32[24,320]{1,0:T(8,128)S(1)}, f32[24,320]{1,0:T(8,128)S(1)}, f32[320,24,64]{0,2,1:T(8,128)}, s32[320]{0:T(512)S(1)}, /*index=5*/s3...) while((s32[]{:T(128)}, f32[24,320]{1,0:T(8,128)S(1)}, ...), condition=%wide.region_10.11_spmd.clone, body=%wide.region_6.0_spmd.clone.sunk | while | flops 530479616 | bytes 62756472 | solution.py:149
  480.9 20.6 all-gather.21.cloned.1.call-done
  523.6 43.4 %all-gather.23.cloned.1.call-done = bf16[1536,1536]{1,0:T(8,128)(2,1)} async-done(((bf16[48,1536]{1,0:T(8,128)(2,1)}), bf16[1536,1536]{1,0:T(8,128)(2,1)}) %all-gather.23.cloned.1.call-update) | async-done | bytes 4718608 | tf_op jit(solution)/shard_map/all_gather | solution.py:111
  572.8 208.8 %all-gather.25.cloned.1.call-done = bf16[1536,12288]{1,0:T(8,128)(2,1)} async-done(((bf16[48,12288]{1,0:T(8,128)(2,1)}), bf16[1536,12288]{1,0:T(8,128)(2,1)}) %all-gather.25.cloned.1.call-update) | async-done | bytes 37748752 | tf_op jit(solution)/shard_map/all_gather | solution.py:184
  781.6 22.8 convolution_add_fusion
  804.4 103.7 %all-gather.27.cloned.1.call-done = bf16[6144,1536]{1,0:T(8,128)(2,1)} async-done(((bf16[192,1536]{1,0:T(8,128)(2,1)}), bf16[6144,1536]{1,0:T(8,128)(2,1)}) %all-gather.27.cloned.1.call-update) | async-done | bytes 18874384 | tf_op jit(solution)/shard_map/all_gather | solution.py:186
  908.1 23.7 multiply_convert_fusion.2
  931.8 25.0 multiply_reduce_fusion.2
  1007.7 131.2 %while.33 = (s32[]{:T(128)}, f32[320,24,64]{0,2,1:T(8,128)}, bf16[5,256,3072]{2,1,0:T(8,128)(2,1)}, s32[5]{0:T(128)S(1)}, bf16[1280,24,64]{0,2,1:T(8,128)(2,1)},...) while((s32[]{:T(128)}, f32[320,24,64]{0,2,1:T(8,128)}, ...), condition=%wide.region_25.26_spmd.clone, body=%wide.region_23.25_spmd.clone.sunk | while | flops 1279018496 | bytes 139853440 | solution.py:297
  1160.5 61.3 %reduce-scatter.9.cloned.1.call-done = bf16[320,3072]{1,0:T(8,128)(2,1)} async-done(((bf16[1280,3072]{1,0:T(8,128)(2,1)}), bf16[320,3072]{1,0:T(8,128)(2,1)}) %reduce-scatter.9.cloned.1.call-update) | async-done | bytes 1966096 | tf_op jit(solution)/shard_map/reduce_scatter | solution.py:300
  1270.6 28.4 all-reduce.14.cloned.1.call-done
  1357.8 32.7 fusion.50
  1437.8 135.5 %reduce-scatter.13.cloned.1.call-done = f32[48,1536]{1,0:T(8,128)} async-done(((f32[1536,1536]{1,0:T(8,128)}), f32[48,1536]{1,0:T(8,128)}) %reduce-scatter.13.cloned.1.call-update) | async-done | bytes 294928 | tf_op jit(solution)/shard_map/reduce_scatter | solution.py:321
  1573.3 140.9 %reduce-scatter.15.cloned.1.call-done = f32[48,1536]{1,0:T(8,128)} async-done(((f32[1536,1536]{1,0:T(8,128)}), f32[48,1536]{1,0:T(8,128)}) %reduce-scatter.15.cloned.1.call-update) | async-done | bytes 294928 | tf_op jit(solution)/shard_map/reduce_scatter | solution.py:323
  1714.2 142.0 %reduce-scatter.19.cloned.1.call-done = f32[48,1536]{1,0:T(8,128)} async-done(((f32[1536,1536]{1,0:T(8,128)}), f32[48,1536]{1,0:T(8,128)}) %reduce-scatter.19.cloned.1.call-update) | async-done | bytes 294928 | tf_op jit(solution)/shard_map/reduce_scatter | solution.py:325
  1856.2 212.0 %reduce-scatter.17.cloned.1.call-done = f32[48,3072]{1,0:T(8,128)} async-done(((f32[1536,3072]{1,0:T(8,128)}), f32[48,3072]{1,0:T(8,128)}) %reduce-scatter.17.cloned.1.call-update) | async-done | bytes 589840 | tf_op jit(solution)/shard_map/reduce_scatter | solution.py:324
  2068.2 354.7 %reduce-scatter.23.cloned.1.call-done = f32[192,1536]{1,0:T(8,128)} async-done(((f32[6144,1536]{1,0:T(8,128)}), f32[192,1536]{1,0:T(8,128)}) %reduce-scatter.23.cloned.1.call-update) | async-done | bytes 1179664 | tf_op jit(solution)/shard_map/reduce_scatter | solution.py:233
  2422.9 271.4 %reduce-scatter.11.cloned.1.call-done = f32[48,4608]{1,0:T(8,128)} async-done(((f32[1536,4608]{1,0:T(8,128)}), f32[48,4608]{1,0:T(8,128)}) %reduce-scatter.11.cloned.1.call-update) | async-done | bytes 884752 | tf_op jit(solution)/shard_map/reduce_scatter | solution.py:320
  2694.4 663.3 %reduce-scatter.21.cloned.1.call-done = f32[48,12288]{1,0:T(8,128)} async-done(((f32[1536,12288]{1,0:T(8,128)}), f32[48,12288]{1,0:T(8,128)}) %reduce-scatter.21.cloned.1.call-update) | async-done | bytes 2359312 | tf_op jit(solution)/shard_map/reduce_scatter | solution.py:231
  (478 shorter events, 565.2 us)
Async XLA Ops:
  7.2 108.2 %all-gather.11.cloned.1.call-start = ((), (), s32[]{:S(2)}) async-start(), calls=%async_computation.8 | async-start | bytes 14598144 | tf_op jit(solution)/shard_map/all_gather | solution.py:106
  7.9 191.8 %all-gather.19.cloned.1.call-start = ((), (), s32[]{:S(2)}) async-start(), calls=%async_computation.12 | async-start | bytes 9732096 | tf_op jit(solution)/shard_map/all_gather | solution.py:110
  8.7 275.4 %all-gather.13.cloned.1.call-start = ((), (), s32[]{:S(2)}) async-start(), calls=%async_computation.9 | async-start | bytes 9830400 | tf_op jit(solution)/shard_map/all_gather | solution.py:127
  138.2 230.8 %all-gather.15.cloned.1.call-start = ((), (), s32[]{:S(2)}) async-start(), calls=%async_computation.10 | async-start | bytes 9830400 | tf_op jit(solution)/shard_map/all_gather | solution.py:128
  143.3 332.3 %all-gather.17.cloned.1.call-start = ((), (), s32[]{:S(2)}) async-start(), calls=%async_computation.11 | async-start | bytes 4866048 | tf_op jit(solution)/shard_map/all_gather | solution.py:107
  143.9 357.6 %all-gather.21.cloned.1.call-start = ((), (), s32[]{:S(2)}) async-start(), calls=%async_computation.13 | async-start | bytes 4866048 | tf_op jit(solution)/shard_map/all_gather | solution.py:109
  144.5 422.5 %all-gather.23.cloned.1.call-start = ((), (), s32[]{:S(2)}) async-start(), calls=%async_computation.14 | async-start | bytes 4866048 | tf_op jit(solution)/shard_map/all_gather | solution.py:111
  145.2 636.4 %all-gather.25.cloned.1.call-start = ((), (), s32[]{:S(2)}) async-start(), calls=%async_computation.15 | async-start | bytes 38928384 | tf_op jit(solution)/shard_map/all_gather | solution.py:184
  146.0 762.1 %all-gather.27.cloned.1.call-start = ((), (), s32[]{:S(2)}) async-start(), calls=%async_computation.16 | async-start | bytes 19464192 | tf_op jit(solution)/shard_map/all_gather | solution.py:186
  146.7 1075.1 %reduce-scatter.9.cloned.1.call-start = ((), (), s32[]{:S(2)}) async-start(), calls=%async_computation.17 | async-start | bytes 9830400 | tf_op jit(solution)/shard_map/reduce_scatter | solution.py:300
  187.1 769.7 %copy-start.45 = (f32[1536]{0:T(1024)}, f32[1536]{0:T(1024)S(1)}, u32[]{:S(2)}) copy-start(f32[1536]{0:T(1024)S(1)} %convert_element_type.164) | copy-start | bytes 18436
  480.5 518.5 %copy-start.8 = (f32[320,1536]{1,0:T(8,128)}, f32[320,1536]{1,0:T(8,128)S(1)}, u32[]{:S(2)}) copy-start(f32[320,1536]{1,0:T(8,128)S(1)} %get-tuple-element.577) | copy-start | bytes 5898244
  480.5 518.5 %copy-start.66 = (f32[320]{0:T(512)}, f32[320]{0:T(512)S(1)}, u32[]{:S(2)}) copy-start(f32[320]{0:T(512)S(1)} %broadcast_multiply_fusion.8) | copy-start | bytes 3844
  480.9 518.1 %copy-start.69 = (f32[320]{0:T(512)}, f32[320]{0:T(512)S(1)}, u32[]{:S(2)}) copy-start(f32[320]{0:T(512)S(1)} %add_rsqrt_fusion.1) | copy-start | bytes 3844
  571.2 385.6 %copy-start.47 = (f32[320]{0:T(512)}, f32[320]{0:T(512)S(1)}, u32[]{:S(2)}) copy-start(f32[320]{0:T(512)S(1)} %broadcast_multiply_fusion.7) | copy-start | bytes 3844
  1138.9 160.2 %all-reduce.14.cloned.1.call-start = ((), (), s32[]{:S(2)}) async-start(), calls=%async_computation.18 | async-start | bytes 4718592 | tf_op jit(solution)/shard_map/psum | solution.py:251
  1160.5 270.9 %all-reduce.16.cloned.1.call-start = ((), (), s32[]{:S(2)}) async-start(), calls=%async_computation.26 | async-start | bytes 163840
  1247.8 325.5 %reduce-scatter.13.cloned.1.call-start = ((), (), s32[]{:S(2)}) async-start(), calls=%async_computation.20 | async-start | bytes 9732096 | tf_op jit(solution)/shard_map/reduce_scatter | solution.py:321
  1254.3 459.9 %reduce-scatter.15.cloned.1.call-start = ((), (), s32[]{:S(2)}) async-start(), calls=%async_computation.21 | async-start | bytes 9732096 | tf_op jit(solution)/shard_map/reduce_scatter | solution.py:323
  1262.6 593.6 %reduce-scatter.19.cloned.1.call-start = ((), (), s32[]{:S(2)}) async-start(), calls=%async_computation.23 | async-start | bytes 9732096 | tf_op jit(solution)/shard_map/reduce_scatter | solution.py:325
  1270.6 797.6 %reduce-scatter.17.cloned.1.call-start = ((), (), s32[]{:S(2)}) async-start(), calls=%async_computation.22 | async-start | bytes 19464192 | tf_op jit(solution)/shard_map/reduce_scatter | solution.py:324
  1321.4 1101.5 %reduce-scatter.23.cloned.1.call-start = ((), (), s32[]{:S(2)}) async-start(), calls=%async_computation.25 | async-start | bytes 38928384 | tf_op jit(solution)/shard_map/reduce_scatter | solution.py:233
  1341.0 1353.4 %reduce-scatter.11.cloned.1.call-start = ((), (), s32[]{:S(2)}) async-start(), calls=%async_computation.19 | async-start | bytes 29196288 | tf_op jit(solution)/shard_map/reduce_scatter | solution.py:320
  1356.3 2001.4 %reduce-scatter.21.cloned.1.call-start = ((), (), s32[]{:S(2)}) async-start(), calls=%async_computation.24 | async-start | bytes 77856768 | tf_op jit(solution)/shard_map/reduce_scatter | solution.py:231
  (100 other events, 1836.5 us)
Sparse Core Ops, SparseCore 0:
  11.0 104.3 all-gather.10
  118.4 81.2 all-gather.18
  202.2 81.8 all-gather.12
  285.8 83.2 all-gather.14
  371.9 64.0 all-gather.16
  438.9 62.4 all-gather.20
  504.5 62.4 all-gather.22
  570.0 211.5 all-gather.24
  784.6 123.4 all-gather.26
  1139.0 82.8 reduce-scatter.8
  1225.0 74.0 all-reduce.13
  1306.5 124.8 all-reduce.15
  1438.8 134.4 reduce-scatter.12
  1579.6 134.5 reduce-scatter.14
  1721.5 134.6 reduce-scatter.18
  1863.0 205.1 reduce-scatter.16
  2075.1 347.8 reduce-scatter.22
  2430.9 263.4 reduce-scatter.10
  2702.5 655.1 reduce-scatter.20
where the time goes:
time: 3380 us; the launch traced here: 3360 us
  waiting for transfers between devices  2620 us (78%)
  matrix products  409 us (12%)
  local copies, waits for them, and re-layouts  148 us (4%)
  other arithmetic  83.4 us (2%)
  blocking collectives  79.8 us (2%)
    reduce_scatter x1, waiting for transfers between devices, shards(): lax.psum_scatter(grad_w_gateup, ('seq', 'fsdp'), scatter_dimension=0, til...  663 us
    reduce_scatter x1, waiting for transfers between devices, shards(): lax.psum_scatter(grad_w_down, ('seq', 'fsdp'), scatter_dimension=0, tiled...  355 us
    reduce_scatter x1, waiting for transfers between devices, shards(): lax.psum_scatter(grad_w_self, ('seq', 'fsdp'), scatter_dimension=0, tiled...  271 us
    reduce_scatter x1, waiting for transfers between devices, shards(): lax.psum_scatter(grad_w_keyval, ('seq', 'fsdp'), scatter_dimension=0, til...  212 us
    all_gather x1, waiting for transfers between devices, shards(): lax.all_gather(proj_gateup, ('seq', 'fsdp'), axis=0, tiled=True)  209 us
    reduce_scatter x1, waiting for transfers between devices, shards(): lax.psum_scatter(grad_w_cross, ('seq', 'fsdp'), scatter_dimension=0, tile...  142 us
    reduce_scatter x1, waiting for transfers between devices, shards(): lax.psum_scatter(grad_w_query, ('seq', 'fsdp'), scatter_dimension=0, tile...  141 us
    reduce_scatter x1, waiting for transfers between devices, shards(): lax.psum_scatter(grad_w_out, ('seq', 'fsdp'), scatter_dimension=0, tiled=...  135 us
  transfers between devices with their start and end apart: 19, of which 18 were waited for; matrix products, arithmetic and copies ran while one was open for 12% of the time, Pallas kernels for 0%

commit v1 on v0

v1 whole, which is shorter than its diff:
```python
import functools

import jax
import jax.numpy as jnp
from jax import lax
from jax.experimental import pallas as pl
from jax.experimental.pallas import tpu as pltpu
from jax.sharding import PartitionSpec as P

D = 1536
HEADS = 24
HEAD = 64
FF = 6144
COND = 130
SEQS_GRP = 2
LANES = 128

epsilon = 1e-05
masked_score = -1e30
bf16 = jnp.bfloat16
f32 = jnp.float32
ALL = ("seq", "fsdp")


def seq_info(global_rows, group_lengths):
    ends = jnp.cumsum(group_lengths)
    starts = ends - group_lengths
    ident = jnp.sum((global_rows[:, None] >= ends[None, :]).astype(jnp.int32), axis=1)
    onehot = ident[:, None] == jnp.arange(group_lengths.shape[0], dtype=jnp.int32)[None, :]
    begin = jnp.sum(jnp.where(onehot, starts[None, :], 0), axis=1)
    return (ident, (global_rows - begin).astype(f32))


def angle_tables(positions):
    half = HEAD // 2
    inverse = jnp.power(10000.0, -jnp.arange(half, dtype=f32) / half)
    turned = positions[:, None] * inverse[None, :]
    cosine, sine = jnp.cos(turned), jnp.sin(turned)
    reps = LANES // HEAD
    return (
        jnp.concatenate([cosine, cosine] * reps, axis=1),
        jnp.concatenate([-sine, sine] * reps, axis=1),
    )


def norm_rows(values, gain):
    centre = values - jnp.mean(values, axis=-1, keepdims=True)
    spread = jnp.mean(centre * centre, axis=-1, keepdims=True)
    scaled = lax.rsqrt(spread + epsilon)
    normal = centre * scaled
    return (normal, scaled, normal * gain)


def norm_back(grad_rows, normal, scaled, gain):
    weighted = grad_rows * gain
    mean_one = jnp.mean(weighted, axis=-1, keepdims=True)
    mean_two = jnp.mean(weighted * normal, axis=-1, keepdims=True)
    return (scaled * (weighted - mean_one - normal * mean_two), jnp.sum(grad_rows * normal, axis=0))


def dot(left, right):
    return jnp.dot(left, right, preferred_element_type=f32)


def outer_sum(left, right):
    return lax.dot_general(left, right, (((0,), (0,)), ((), ())), preferred_element_type=f32)


def back_prod(left, weight):
    return lax.dot_general(left, weight, (((1,), (1,)), ((), ())), preferred_element_type=f32)


def hop(value, j):
    return lax.ppermute(value, "seq", [(i, i ^ j) for i in range(4)])


def block_ids(n):
    if n == 4:
        return lax.axis_index("seq") ^ jnp.arange(n, dtype=jnp.int32)
    return jnp.arange(n, dtype=jnp.int32)


def gather_rows(value, n):
    if n != 4:
        return lax.all_gather(value, "seq", axis=0, tiled=True)
    half = value.shape[0] // 2
    first, second = hop(value, 1), hop(value, 2)
    third, fourth = hop(second[:half], 1), hop(first[half:], 2)
    return jnp.concatenate([value, first, second, third, fourth], axis=0)


def scatter_rows(blocks, n):
    if n != 4:
        whole = jnp.concatenate([blocks(j) for j in range(n)], axis=0)
        return lax.psum_scatter(whole.astype(bf16), "seq", scatter_dimension=0, tiled=True).astype(f32)
    last = blocks(3).astype(bf16)
    half = last.shape[0] // 2
    to_first, to_second = hop(last[:half], 1), hop(last[half:], 2)
    one, two = blocks(1), blocks(2)
    plain_one, plain_two = hop(one[:half].astype(bf16), 1), hop(two[half:].astype(bf16), 2)
    sum_one = hop((one[half:] + to_second.astype(f32)).astype(bf16), 1)
    sum_two = hop((two[:half] + to_first.astype(f32)).astype(bf16), 2)
    own = blocks(0)
    return own + jnp.concatenate(
        [
            plain_one.astype(f32) + sum_two.astype(f32),
            sum_one.astype(f32) + plain_two.astype(f32),
        ],
        axis=0,
    )


def swap_halves(value):
    lane = lax.broadcasted_iota(jnp.int32, value.shape, 1)
    half = HEAD // 2
    return jnp.where(
        lane % HEAD < half, pltpu.roll(value, LANES - half, 1), pltpu.roll(value, half, 1)
    )


def head_rows(h):
    return slice(h * HEAD, (h + 1) * HEAD)


def lane_mask(value, h):
    lane = lax.broadcasted_iota(jnp.int32, value.shape, 1)
    return jnp.where(lane // HEAD == h, value, jnp.zeros_like(value))


def row_mask(value, h):
    row = lax.broadcasted_iota(jnp.int32, value.shape, 0)
    return jnp.where(row // HEAD == h, value, jnp.zeros_like(value))


def attend_kernel(rope, tile, *refs):
    if rope:
        q_ref, k_ref, v_ref, cos_ref, sin_ref, qid_ref, kid_ref = refs[:7]
        qo_ref, ko_ref, vo_ref, o_ref, lse_ref, qt, vt, ot, kb = refs[7:]
        q, k = q_ref[...], k_ref[...]
        q = (q * cos_ref[...] + swap_halves(q) * sin_ref[...]).astype(bf16)
        k = (k * cos_ref[...] + swap_halves(k) * sin_ref[...]).astype(bf16)
        v = v_ref[...].astype(bf16)
        qo_ref[...] = q
        ko_ref[...] = k
        vo_ref[...] = v
    else:
        q_ref, k_ref, v_ref, qid_ref, kid_ref, o_ref, lse_ref, qt, vt, ot, kb = refs
        q, k, v = q_ref[...], k_ref[...], v_ref[...]
    kb[...] = k
    qt[...] = q.astype(f32).T.astype(bf16)
    vt[...] = v.astype(f32).T.astype(bf16)

    def body(t, carry):
        at = pl.ds(pl.multiple_of(t * tile, tile), tile)
        queries = qt[:, at]
        allowed = kid_ref[...] == qid_ref[:, at]
        for h in range(LANES // HEAD):
            s = dot(kb[...], row_mask(queries, h)) * 0.125
            s = jnp.where(allowed, s, masked_score)
            top = jnp.max(s, axis=0, keepdims=True)
            e = jnp.exp(s - top)
            total = jnp.sum(e, axis=0, keepdims=True)
            p = (e * (1.0 / total)).astype(bf16)
            ot[head_rows(h), at] = dot(vt[head_rows(h), :], p)
            lse_ref[0, h : h + 1, at] = top + jnp.log(total)
        return carry

    lax.fori_loop(0, qt.shape[1] // tile, body, 0)
    o_ref[...] = ot[...].T.astype(bf16)


def attend_back_kernel(rope, tile, *refs):
    if rope:
        q_ref, k_ref, v_ref, do_ref, o_ref, lse_ref, cos_ref, sin_ref, qid_ref, kid_ref = refs[:10]
        dq_ref, dk_ref, dv_ref, qt, dot_t, kt, dqt, dk_acc, dv_acc, delta = refs[10:]
    else:
        q_ref, k_ref, v_ref, do_ref, o_ref, lse_ref, qid_ref, kid_ref = refs[:8]
        dq_ref, dk_ref, dv_ref, qt, dot_t, kt, dqt, dk_acc, dv_acc, delta = refs[8:]
    qt[...] = q_ref[...].astype(f32).T.astype(bf16)
    kt[...] = k_ref[...].astype(f32).T.astype(bf16)
    dof_t = do_ref[...].astype(f32).T
    dot_t[...] = dof_t.astype(bf16)
    product = dof_t * o_ref[...].astype(f32).T
    for h in range(LANES // HEAD):
        delta[h : h + 1, :] = jnp.sum(product[head_rows(h), :], axis=0, keepdims=True)
    dk_acc[...] = jnp.zeros_like(dk_acc)
    dv_acc[...] = jnp.zeros_like(dv_acc)

    def body(t, carry):
        at = pl.ds(pl.multiple_of(t * tile, tile), tile)
        allowed = kid_ref[...] == qid_ref[:, at]
        for h in range(LANES // HEAD):
            s = dot(k_ref[...], row_mask(qt[:, at], h)) * 0.125
            p = jnp.where(allowed, jnp.exp(s - lse_ref[0, h : h + 1, at]), 0.0)
            dp = dot(v_ref[...], row_mask(dot_t[:, at], h))
            dv_acc[...] += dot(p.astype(bf16), lane_mask(do_ref[at, :], h))
            ds = (p * (dp - delta[h : h + 1, at])).astype(bf16)
            dk_acc[...] += dot(ds, lane_mask(q_ref[at, :], h))
            dqt[head_rows(h), at] = dot(kt[head_rows(h), :], ds)
        return carry

    lax.fori_loop(0, qt.shape[1] // tile, body, 0)
    dq = dqt[...].T * 0.125
    dk = dk_acc[...] * 0.125
    if rope:
        dq = dq * cos_ref[...] - swap_halves(dq) * sin_ref[...]
        dk = dk * cos_ref[...] - swap_halves(dk) * sin_ref[...]
    dq_ref[...] = dq.astype(bf16)
    dk_ref[...] = dk.astype(bf16)
    dv_ref[...] = dv_acc[...].astype(bf16)


def query_tile(rows):
    for tile in (256, 128):
        if rows % tile == 0:
            return tile
    return rows


def spec(rows, offset=0):
    return pl.BlockSpec((rows, LANES), lambda i: (0, i + offset))


def whole(shape):
    return pl.BlockSpec(shape, lambda i: (0,) * len(shape), pipeline_mode=pl.Buffered(1))


LIMIT = 56 * 1024 * 1024


def attend(q, k, v, offsets, pairs, qid, kid, tables=None):
    nq, nk = q.shape[0], k.shape[0]
    rope = tables is not None
    tile = query_tile(nq)
    ins = [spec(nq, offsets[0]), spec(nk, offsets[1]), spec(nk, offsets[2])]
    args = [q, k, v]
    outs, shapes = [], []
    if rope:
        ins += [whole((nq, LANES)), whole((nq, LANES))]
        args += list(tables)
        outs += [spec(nq), spec(nk), spec(nk)]
        shapes += [jax.ShapeDtypeStruct((rows, pairs * LANES), bf16) for rows in (nq, nk, nk)]
    ins += [whole((1, nq)), whole((nk, 1))]
    args += [qid[None, :], kid[:, None]]
    outs += [spec(nq), pl.BlockSpec((1, 8, nq), lambda i: (i, 0, 0))]
    shapes += [
        jax.ShapeDtypeStruct((nq, pairs * LANES), bf16),
        jax.ShapeDtypeStruct((pairs, 8, nq), f32),
    ]
    return pl.pallas_call(
        functools.partial(attend_kernel, rope, tile),
        out_shape=shapes,
        grid=(pairs,),
        in_specs=ins,
        out_specs=outs,
        scratch_shapes=[
            pltpu.VMEM((LANES, nq), bf16),
            pltpu.VMEM((LANES, nk), bf16),
            pltpu.VMEM((LANES, nq), f32),
            pltpu.VMEM((nk, LANES), bf16),
        ],
        compiler_params=pltpu.CompilerParams(vmem_limit_bytes=LIMIT),
        cost_estimate=pl.CostEstimate(
            flops=2 * 2 * 2 * pairs * nq * nk * LANES,
            bytes_accessed=pairs * LANES * (nq + nk) * 12,
            transcendentals=2 * pairs * nq * nk,
        ),
        name="attend_self" if rope else "attend_cross",
    )(*args)


def attend_back(q, k, v, offsets, pairs, grad, mixed, lse, qid, kid, tables=None):
    nq, nk = q.shape[0], k.shape[0]
    rope = tables is not None
    tile = query_tile(nq)
    ins = [spec(nq, offsets[0]), spec(nk, offsets[1]), spec(nk, offsets[2]), spec(nq), spec(nq)]
    args = [q, k, v, grad, mixed]
    ins += [pl.BlockSpec((1, 8, nq), lambda i: (i, 0, 0))]
    args += [lse]
    if rope:
        ins += [whole((nq, LANES)), whole((nq, LANES))]
        args += list(tables)
    ins += [whole((1, nq)), whole((nk, 1))]
    args += [qid[None, :], kid[:, None]]
    return pl.pallas_call(
        functools.partial(attend_back_kernel, rope, tile),
        out_shape=[jax.ShapeDtypeStruct((rows, pairs * LANES), bf16) for rows in (nq, nk, nk)],
        grid=(pairs,),
        in_specs=ins,
        out_specs=[spec(nq), spec(nk), spec(nk)],
        scratch_shapes=[
            pltpu.VMEM((LANES, nq), bf16),
            pltpu.VMEM((LANES, nq), bf16),
            pltpu.VMEM((LANES, nk), bf16),
            pltpu.VMEM((LANES, nq), f32),
            pltpu.VMEM((nk, LANES), f32),
            pltpu.VMEM((nk, LANES), f32),
            pltpu.VMEM((8, nq), f32),
        ],
        compiler_params=pltpu.CompilerParams(vmem_limit_bytes=LIMIT),
        cost_estimate=pl.CostEstimate(
            flops=2 * 5 * 2 * pairs * nq * nk * LANES,
            bytes_accessed=pairs * LANES * (nq + nk) * 12,
            transcendentals=2 * pairs * nq * nk,
        ),
        name="back_self" if rope else "back_cross",
    )(*args)


def column_parts(shard, parts, n):
    r, columns = shard.shape
    c = columns // (parts * n)
    return shard.reshape(r, parts, n, c).transpose(2, 0, 1, 3).reshape(n, r, parts * c)


def natural_columns(pieces, parts, n):
    r, columns = pieces.shape[1:]
    c = columns // parts
    return pieces.reshape(n, r, parts, c).transpose(1, 2, 0, 3).reshape(r, parts * n * c)


def to_seq(pieces):
    return lax.all_to_all(pieces, "seq", 0, 0, tiled=True)


def gather_columns(pieces, n, nf):
    r, c = pieces.shape[1:]
    gathered = lax.all_gather(pieces.reshape(n * r, c), "fsdp", axis=0, tiled=True)
    return gathered.reshape(nf, n, r, c).transpose(1, 0, 2, 3).reshape(n * nf * r, c)


def scatter_columns(grad, n, nf):
    rows, c = grad.shape
    r = rows // (n * nf)
    ordered = grad.astype(bf16).reshape(n, nf, r, c).transpose(1, 0, 2, 3).reshape(rows, c)
    return lax.psum_scatter(ordered, "fsdp", scatter_dimension=0, tiled=True).reshape(n, r, c)


def scatter_plain(grad):
    return lax.psum_scatter(grad.astype(bf16), "fsdp", scatter_dimension=0, tiled=True)


def pad_heads(value, parts):
    rows, columns = value.shape
    c = columns // parts
    if c % LANES == 0:
        return value
    padded = -(-c // LANES) * LANES
    return jnp.pad(value.reshape(rows, parts, c), ((0, 0), (0, 0), (0, padded - c))).reshape(
        rows, parts * padded
    )


def shards(
    tokens,
    conditioning,
    lengths,
    grad_output,
    norm_first,
    proj_self,
    out_self,
    norm_second,
    proj_query,
    proj_keyval,
    out_cross,
    norm_third,
    proj_gateup,
    bias_gateup,
    proj_down,
    bias_down,
):
    rows = tokens.shape[1]
    n = lax.axis_size("seq")
    nf = lax.axis_size("fsdp")
    me = lax.axis_index("seq")
    group = rows * n
    wide = D // n
    pairs = -(-wide // LANES)
    hidden = FF // n
    r = norm_first.shape[0]

    small = jnp.concatenate(
        [v.reshape(r, -1) for v in (norm_first, norm_second, norm_third, bias_down, bias_gateup)],
        axis=1,
    )
    small = jnp.pad(small, ((0, 0), (0, LANES - small.shape[1])))
    self_in = jnp.concatenate(
        [column_parts(proj_self, 3, n), jnp.broadcast_to(small[None], (n, r, LANES))], axis=2
    )
    self_pieces = to_seq(self_in)
    rest_in = jnp.concatenate(
        [column_parts(proj_keyval, 2, n), column_parts(proj_query, 1, n), column_parts(proj_gateup, 2, n)],
        axis=2,
    )
    rest_pieces = to_seq(rest_in)
    self_all = gather_columns(self_pieces, n, nf)
    w_self = self_all[:, : 3 * wide]
    vectors = self_all[:, 3 * wide : 3 * wide + 12]
    gain_one, gain_two, gain_three, b_down = (vectors[:, j].astype(f32) for j in range(4))
    b_gateup = vectors[:, 4:12].reshape(2 * FF).astype(f32)
    b_gate = lax.dynamic_slice_in_dim(b_gateup, me * hidden, hidden, 0)
    b_upper = lax.dynamic_slice_in_dim(b_gateup, FF + me * hidden, hidden, 0)
    outs = lax.all_gather(jnp.concatenate([out_self, out_cross], axis=0), "fsdp", axis=0, tiled=True)
    outs = outs.reshape(nf, 2, r, D)
    w_out = outs[:, 0].reshape(nf * r, D)
    w_cross = outs[:, 1].reshape(nf * r, D)
    kvq = gather_columns(rest_pieces[:, :, : 3 * wide], n, nf)
    w_keyval, w_query = kvq[:, : 2 * wide], kvq[:, 2 * wide :]
    w_gateup = gather_columns(rest_pieces[:, :, 3 * wide :], n, nf)
    w_down = lax.all_gather(proj_down, "fsdp", axis=0, tiled=True)

    group_lengths = lengths[0]
    order = block_ids(n)
    all_rows = (order[:, None] * rows + jnp.arange(rows, dtype=jnp.int32)[None, :]).reshape(group)
    ids, positions = seq_info(all_rows, group_lengths)
    tables = angle_tables(positions)
    group_tokens = gather_rows(tokens[0], n)
    group_grad = gather_rows(grad_output[0], n)

    def block(value, j):
        return lax.slice_in_dim(value, j * rows, (j + 1) * rows, axis=0)

    inputs = tokens[0].astype(f32)
    normal_one, scaled_one, _ = norm_rows(inputs, gain_one)
    normed_one = norm_rows(group_tokens.astype(f32), gain_one)[2].astype(bf16)
    packed = pad_heads(dot(normed_one, w_self), 3)
    q, k, v, mixed, lse = attend(packed, packed, packed, (0, pairs, 2 * pairs), pairs, ids, ids, tables)
    mixed_in = mixed[:, :wide]
    first = inputs + scatter_rows(lambda j: dot(block(mixed_in, j), w_out), n)

    normal_two, scaled_two, normed = norm_rows(first, gain_two)
    normed_two = gather_rows(normed.astype(bf16), n)
    cq = pad_heads(dot(normed_two, w_query).astype(bf16), 1)
    cond_rows = conditioning[0].reshape(SEQS_GRP * COND, D)
    count = SEQS_GRP * COND
    count_pad = -(-count // 16) * 16
    keyval = pad_heads(dot(cond_rows, w_keyval).astype(bf16), 2)
    keyval = jnp.pad(keyval, ((0, count_pad - count), (0, 0)))
    index = jnp.arange(count_pad, dtype=jnp.int32)
    cond_ids = jnp.where(index < count, index // COND, -1)
    cmix, clse = attend(cq, keyval, keyval, (0, 0, pairs), pairs, ids, cond_ids)
    cmix_in = cmix[:, :wide]
    second = first + scatter_rows(lambda j: dot(block(cmix_in, j), w_cross), n)

    normal_three, scaled_three, normed = norm_rows(second, gain_three)
    normed_three = gather_rows(normed.astype(bf16), n)
    gate = dot(normed_three, w_gateup[:, :hidden]) + b_gate
    upper = dot(normed_three, w_gateup[:, hidden:]) + b_upper
    sigma = jax.nn.sigmoid(gate)
    silu_gate = gate * sigma
    active = (silu_gate * upper).astype(bf16)
    result = second + scatter_rows(lambda j: dot(block(active, j), w_down), n) + b_down

    grad_rows = grad_output[0].astype(f32)
    grad_b_down = jnp.sum(grad_rows, axis=0)
    grad_active = back_prod(group_grad, w_down)
    grad_gate = grad_active * upper * sigma * (1.0 + gate * (1.0 - sigma))
    grad_upper = grad_active * silu_gate
    grad_gateup = jnp.concatenate([grad_gate, grad_upper], axis=1).astype(bf16)
    grad_w_down = scatter_plain(outer_sum(active, group_grad))
    through = scatter_rows(lambda j: back_prod(block(grad_gateup, j), w_gateup), n)
    grad_w_gateup = scatter_columns(outer_sum(normed_three, grad_gateup), n, nf)
    grad_b_gateup = jnp.sum(grad_gateup.astype(f32), axis=0)
    through, grad_gain_three = norm_back(through, normal_three, scaled_three, gain_three)
    grad_second = grad_rows + through

    group_second = gather_rows(grad_second.astype(bf16), n)
    grad_cmix = pad_heads(back_prod(group_second, w_cross).astype(bf16), 1)
    dcq, dck, dcv = attend_back(
        cq, keyval, keyval, (0, 0, pairs), pairs, grad_cmix, cmix, clse, ids, cond_ids
    )
    dcq, dck, dcv = dcq[:, :wide], dck[:count, :wide], dcv[:count, :wide]
    through = scatter_rows(lambda j: back_prod(block(dcq, j), w_query), n)
    grad_keyval = jnp.concatenate([dck, dcv], axis=1)
    grad_w_cross = scatter_plain(outer_sum(cmix_in, group_second))
    grad_w_kvq = scatter_columns(
        jnp.concatenate([outer_sum(cond_rows, grad_keyval), outer_sum(normed_two, dcq)], axis=1), n, nf
    )
    grad_cond = lax.psum(back_prod(grad_keyval, w_keyval), "seq").reshape(1, SEQS_GRP, COND, D)
    through, grad_gain_two = norm_back(through, normal_two, scaled_two, gain_two)
    grad_first = grad_second + through

    group_first = gather_rows(grad_first.astype(bf16), n)
    grad_mixed = pad_heads(back_prod(group_first, w_out).astype(bf16), 1)
    dq, dk, dv = attend_back(q, k, v, (0, 0, 0), pairs, grad_mixed, mixed, lse, ids, ids, tables)
    grad_packed = jnp.concatenate([dq[:, :wide], dk[:, :wide], dv[:, :wide]], axis=1)
    through = scatter_rows(lambda j: back_prod(block(grad_packed, j), w_self), n)
    grad_w_out = scatter_plain(outer_sum(mixed_in, group_first))
    grad_w_self = scatter_columns(outer_sum(normed_one, grad_packed), n, nf)
    through, grad_gain_one = norm_back(through, normal_one, scaled_one, gain_one)
    grad_inputs = grad_first + through

    rest = to_seq(jnp.concatenate([grad_w_kvq, grad_w_gateup], axis=2))
    own_self = to_seq(grad_w_self)
    place = me * nf + lax.axis_index("fsdp")
    b_whole = jnp.zeros((2, FF), f32)
    b_whole = lax.dynamic_update_slice(b_whole, grad_b_gateup.reshape(2, hidden), (0, me * hidden))
    early = lax.psum(
        jnp.concatenate([grad_gain_two, grad_gain_three, grad_b_down, b_whole.reshape(2 * FF)]), ALL
    )
    late = lax.psum(grad_gain_one, ALL)

    def mine(vector):
        count = vector.shape[0] // (n * nf)
        return lax.dynamic_slice_in_dim(vector, place * count, count, 0)

    return (
        result.astype(bf16)[None],
        grad_inputs[None],
        grad_cond,
        mine(late),
        natural_columns(own_self, 3, n).astype(f32),
        grad_w_out.astype(f32),
        mine(early[:D]),
        natural_columns(rest[:, :, 2 * wide : 3 * wide], 1, n).astype(f32),
        natural_columns(rest[:, :, : 2 * wide], 2, n).astype(f32),
        grad_w_cross.astype(f32),
        mine(early[D : 2 * D]),
        natural_columns(rest[:, :, 3 * wide :], 2, n).astype(f32),
        mine(early[3 * D :]),
        grad_w_down.astype(f32),
        mine(early[2 * D : 3 * D]),
    )


def solution(mesh):
    rows_of = P("fsdp", "seq", None)
    matrix = P(ALL, None)
    vector = P(ALL)
    return jax.shard_map(
        shards,
        mesh=mesh,
        in_specs=(
            rows_of,
            P("fsdp", None, None, None),
            P("fsdp", None),
            rows_of,
            vector,
            matrix,
            matrix,
            vector,
            matrix,
            matrix,
            matrix,
            vector,
            matrix,
            vector,
            matrix,
            vector,
        ),
        out_specs=(
            rows_of,
            rows_of,
            P("fsdp", None, None, None),
            vector,
            matrix,
            matrix,
            vector,
            matrix,
            matrix,
            matrix,
            vector,
            matrix,
            vector,
            matrix,
            vector,
        ),
        check_vma=False,
    )
```

time: 3380 us -> 1070 us (0.32)
  waiting for transfers between devices: 2620 us -> 409 us
  matrix products: 409 us -> 185 us
  Pallas kernels: 0 us -> 104 us
  starting transfers between devices: 0.76 us -> 71 us
    reduce_scatter x8 -> x6, waiting for transfers between devices: 1980 us -> 193 us  [the longest x3 144 us: scatter_columns(): lax.psum_scatter(ordered, 'fsdp', scatter_dimension=0, tiled=True)]
    all_gather x9 -> x5, waiting for transfers between devices: 595 us -> 0.02 us  [the longest x1 0.01 us: shards(): lax.all_gather(jnp.concatenate([out_self, out_cross], axis=0), 'fsdp', ax...]
    ppermute x0 -> x60, waiting for transfers between devices: none -> 216 us  [hop(): return lax.ppermute(value, 'seq', [(i, i ^ j) for i in range(4)])]
    dot_general x47 -> x17, matrix products: 226 us -> 58.5 us  [dot(): return jnp.dot(left, right, preferred_element_type=f32)]
    pallas_call x0 -> x4, Pallas kernels: none -> 104 us  [the longest x2 54.2 us: attend(): pl.pallas_call(functools.partial(attend_kernel, rope, tile), out_shape=sh...]
    ppermute x0 -> x60, starting transfers between devices: none -> 60.8 us  [hop(): return lax.ppermute(value, 'seq', [(i, i ^ j) for i in range(4)])]
    psum x0 -> x1, blocking collectives: none -> 48.9 us  [shards(): late = lax.psum(grad_gain_one, ALL)]
    dot_general x7, matrix products: 89.1 us -> 47.5 us  [outer_sum(): lax.dot_general(left, right, (((0,), (0,)), ((), ())), preferred_element_...]
  transfers between devices with their start and end apart: 19 -> 75, of which waited for: 18 -> 42; matrix products, arithmetic and copies ran while one was open for 12% -> 27% of each run, Pallas kernels for 0% -> 8%
where the time goes in v1:
time: 1070 us; the launch traced here: 1060 us
  waiting for transfers between devices  409 us (38%)
  matrix products  185 us (17%)
  local copies, waits for them, and re-layouts  126 us (12%)
  Pallas kernels  104 us (10%)
  blocking collectives  82.7 us (8%)
  starting transfers between devices  71 us (7%)
  other arithmetic  61.2 us (6%)
  between operations  15.7 us (1%)
    ppermute x60, waiting for transfers between devices, hop(): return lax.ppermute(value, 'seq', [(i, i ^ j) for i in range(4)])  216 us
    reduce_scatter x3, waiting for transfers between devices, scatter_columns(): lax.psum_scatter(ordered, 'fsdp', scatter_dimension=0, tiled=True)  144 us
    dot_general x16, matrix products, back_prod(): lax.dot_general(left, weight, (((1,), (1,)), ((), ())), preferred_element...  79.2 us
    ppermute x60, starting transfers between devices, hop(): return lax.ppermute(value, 'seq', [(i, i ^ j) for i in range(4)])  60.8 us
    dot_general x17, matrix products, dot(): return jnp.dot(left, right, preferred_element_type=f32)  58.5 us
    pallas_call x2, Pallas kernels, attend(): pl.pallas_call(functools.partial(attend_kernel, rope, tile), out_shape=sh...  54.2 us
    pallas_call x2, Pallas kernels, attend_back(): pl.pallas_call(functools.partial(attend_back_kernel, rope, tile), out_sha...  49.4 us
    reduce_scatter x3, waiting for transfers between devices, scatter_plain(): lax.psum_scatter(grad.astype(bf16), 'fsdp', scatter_dimension=0, tiled=True)  49 us
  transfers between devices with their start and end apart: 75, of which 42 were waited for; matrix products, arithmetic and copies ran while one was open for 27% of the time, Pallas kernels for 8%

profile of v1, /device:TPU:8, one launch (start us, length us, event | category | flops | bytes accessed | tf_op | source)
XLA Modules:
  0.0 1055.2 jit_solution(1438706827457099224)
XLA Ops:
  11.4 11.9 %all_to_all.20 = bf16[4,48,1280]{2,1,0:T(8,128)(2,1)} all-to-all(bf16[4,48,1280]{2,1,0:T(8,128)(2,1)S(1)} %pad_maximum_fusion.6), channel_id=1, replica_groups=mesh['seq'=4,'fsdp'=8] {'seq'}, dimensions={0} | all-to-all | bytes 983040 | tf_op jit(solution)/shard_map/all_to_all | solution.py:323
  27.0 21.9 %all_to_all.21 = bf16[4,48,4224]{2,1,0:T(8,128)(2,1)S(1)} all-to-all(bf16[4,48,4224]{2,1,0:T(8,128)(2,1)S(1)} %pad_maximum_fusion.2), channel_id=1, replica_groups=mesh['seq'=4,'fsdp'=8] {'seq'}, dimensions={0} | all-to-all | bytes 3244032 | tf_op jit(solution)/shard_map/all_to_all | solution.py:323
  62.3 14.2 %collective-permute-done.1 = bf16[320,1536]{1,0:T(8,128)(2,1)S(1)} collective-permute-done((bf16[320,1536]{1,0:T(8,128)(2,1)S(1)}, bf16[320,1536]{1,0:T(8,128)(2,1)S(1)}, u32[]{:S(2)}, u32[]{:S(2)}) %collective-permute-start.1) | collective-permute-done | bytes 983072 | tf_op jit(solution)/shard_map/ppermute | solution.py:74
  78.8 24.8 %collective-permute-done.2 = bf16[160,1536]{1,0:T(8,128)(2,1)S(1)} collective-permute-done((bf16[160,1536]{1,0:T(8,128)(2,1)S(1)}, bf16[160,1536]{1,0:T(8,128)(2,1)S(1)}, u32[]{:S(2)}, u32[]{:S(2)}) %collective-permute-start.2) | collective-permute-done | bytes 491552 | tf_op jit(solution)/shard_map/ppermute | solution.py:74
  121.3 38.7 %attend_self.1 = (bf16[1280,384]{1,0:T(8,128)(2,1)}, bf16[1280,384]{1,0:T(8,128)(2,1)}, bf16[1280,384]{1,0:T(8,128)(2,1)}, bf16[1280,384]{1,0:T(8,128)(2,1)}, f32[3,8,1280]{2,1,0:T(8,128)}) custom-call(f32[1280,1152]{1,0:T(8,128)} %fusion.47.refs_0_.refs_1_.refs_2_, f32[1280,1152]{1,0:T(8,128)} %fusion.47.refs_0_.refs_1_.refs_2_, ...), custom_call_target="tpu_custom_call" | custom-call | flops 5033164800 | bytes 11796480 | tf_op jit(solution)/shard_map/attend_self/pallas_call | solution.py:250
  166.1 9.9 collective-permute-done.5
  184.9 9.8 collective-permute-done.6
  242.8 15.6 %attend_cross.1 = (bf16[1280,384]{1,0:T(8,128)(2,1)}, f32[3,8,1280]{2,1,0:T(8,128)}) custom-call(bf16[1280,384]{1,0:T(8,128)(2,1)} %convolution_convert_fusion.9.refs_0_, bf16[272,768]{1,0:T(8,128)(2,1)} %pad.9.refs_1_.refs_2_, bf16[272,768]{1,0:T(8,128)(2,1)} %pad.9.refs_1_.refs_2_, s32[1,1280]{1,0:T(1,128)} %broadcast_in_dim.31.refs_5_.refs_3_.refs_6_.refs_8_, ...), custom_call_target="tpu_custom_call" | custom-call | flops 1069547520 | bytes 7151616 | tf_op jit(solution)/shard_map/attend_cross/pallas_call | solution.py:250
  304.9 11.8 %collective-permute-done.21 = bf16[320,1536]{1,0:T(8,128)(2,1)} collective-permute-done((bf16[320,1536]{1,0:T(8,128)(2,1)}, bf16[320,1536]{1,0:T(8,128)(2,1)}, u32[]{:S(2)}, u32[]{:S(2)}) %collective-permute-start.21) | collective-permute-done | bytes 983072 | tf_op jit(solution)/shard_map/ppermute | solution.py:74
  338.3 11.4 %convolution_add_fusion = f32[1280,1536]{1,0:T(8,128)} fusion(bf16[1280,1536]{1,0:T(8,128)(2,1)} %constant_dynamic-update-slice_fusion.10, bf16[1536,3072]{1,0:T(8,128)(2,1)} %bitcast.156, f32[1536]{0:T(1024)S(1)} %get-tuple-element.160), kind=kOutput, calls=%fused_computation.15 | convolution fusion | flops 6041763840 | bytes 16521216 | tf_op jit(solution)/shard_map/dot_general | solution.py:62
  358.5 17.7 %multiply_convert_fusion = (bf16[1280,1536]{1,0:T(8,128)(2,1)S(1)}, bf16[1280,1536]{1,0:T(8,128)(2,1)}, bf16[1280,1536]{1,0:T(8,128)(2,1)}) fusion(f32[1280,1536]{1,0:T(8,128)} %convolution_add_fusion.1, f32[1280,1536]{1,0:T(8,128)} %convolution_add_fusion, bf16[1280,1536]{1,0:T(8,128)(2,1)} %constant_dynamic-update-slice_fusion.15, ...), kind=kOutput, calls=%fused_computation.20 | convolution fusion | flops 6069288960 | bytes 36175872 | tf_op jit(solution)/shard_map/dot_general | solution.py:70
  445.1 11.9 %collective-permute-done.41 = bf16[320,1536]{1,0:T(8,128)(2,1)} collective-permute-done((bf16[320,1536]{1,0:T(8,128)(2,1)}, bf16[320,1536]{1,0:T(8,128)(2,1)}, u32[]{:S(2)}, u32[]{:S(2)}) %collective-permute-start.41) | collective-permute-done | bytes 983072 | tf_op jit(solution)/shard_map/ppermute | solution.py:74
  475.3 14.2 %back_cross.1 = (bf16[1280,384]{1,0:T(8,128)(2,1)}, bf16[272,384]{1,0:T(8,128)(2,1)}, bf16[272,384]{1,0:T(8,128)(2,1)}) custom-call(bf16[1280,384]{1,0:T(8,128)(2,1)} %convolution_convert_fusion.9.refs_0_, bf16[272,768]{1,0:T(8,128)(2,1)} %pad.9.refs_1_.refs_2_, bf16[272,768]{1,0:T(8,128)(2,1)} %pad.9.refs_1_.refs_2_, ...), custom_call_target="tpu_custom_call" | custom-call | flops 2673868800 | bytes 7151616 | tf_op jit(solution)/shard_map/back_cross/pallas_call | solution.py:285
  534.5 12.8 %collective-permute-done.51 = bf16[320,1536]{1,0:T(8,128)(2,1)S(1)} collective-permute-done((bf16[320,1536]{1,0:T(8,128)(2,1)S(1)}, bf16[320,1536]{1,0:T(8,128)(2,1)S(1)}, u32[]{:S(2)}, u32[]{:S(2)}) %collective-permute-start.51) | collective-permute-done | bytes 983072 | tf_op jit(solution)/shard_map/ppermute | solution.py:74
  563.7 35.2 %back_self.1 = (bf16[1280,384]{1,0:T(8,128)(2,1)}, bf16[1280,384]{1,0:T(8,128)(2,1)}, bf16[1280,384]{1,0:T(8,128)(2,1)}) custom-call(bf16[1280,384]{1,0:T(8,128)(2,1)} %get-tuple-element.32.refs_0_, bf16[1280,384]{1,0:T(8,128)(2,1)} %get-tuple-element.33.refs_1_, bf16[1280,384]{1,0:T(8,128)(2,1)} %get-tuple-element.34.refs_2_, ...), custom_call_target="tpu_custom_call" | custom-call | flops 12582912000 | bytes 11796480 | tf_op jit(solution)/shard_map/back_self/pallas_call | solution.py:285
  625.3 18.7 %convolution_convert_fusion = bf16[1536,3072]{1,0:T(8,128)(2,1)} fusion(bf16[1280,1536]{1,0:T(8,128)(2,1)} %constant_dynamic-update-slice_fusion.10, bf16[1280,1536]{1,0:T(8,128)(2,1)} %copy-done.18, bf16[1280,1536]{1,0:T(8,128)(2,1)} %get-tuple-element.140), kind=kOutput, calls=%fused_computation.10 | convolution fusion | flops 12100042752 | bytes 21233664 | tf_op jit(solution)/shard_map/dot_general | solution.py:66
  670.5 10.0 convolution_convert_fusion.1
  690.5 13.9 %collective-permute-done.26 = bf16[160,1536]{1,0:T(8,128)(2,1)S(1)} collective-permute-done((bf16[160,1536]{1,0:T(8,128)(2,1)S(1)}, bf16[160,1536]{1,0:T(8,128)(2,1)S(1)}, u32[]{:S(2)}, u32[]{:S(2)}) %collective-permute-start.26) | collective-permute-done | bytes 491552 | tf_op jit(solution)/shard_map/ppermute | solution.py:74
  719.4 27.6 %reduce-scatter.15.cloned.1.call-done = bf16[48,1536]{1,0:T(8,128)(2,1)} async-done(((bf16[384,1536]{1,0:T(8,128)(2,1)}), bf16[48,1536]{1,0:T(8,128)(2,1)}) %reduce-scatter.15.cloned.1.call-update) | async-done | bytes 147472 | tf_op jit(solution)/shard_map/reduce_scatter | solution.py:340
  777.3 9.6 collective-permute-done.56
  794.8 40.6 %reduce-scatter.11.cloned.1.call-done = bf16[192,1152]{1,0:T(8,128)(2,1)} async-done(((bf16[1536,1152]{1,0:T(8,128)(2,1)}), bf16[192,1152]{1,0:T(8,128)(2,1)}) %reduce-scatter.11.cloned.1.call-update) | async-done | bytes 442384 | tf_op jit(solution)/shard_map/reduce_scatter | solution.py:336
  835.4 101.8 %reduce-scatter.13.cloned.1.call-done = bf16[192,3072]{1,0:T(8,128)(2,1)} async-done(((bf16[1536,3072]{1,0:T(8,128)(2,1)}), bf16[192,3072]{1,0:T(8,128)(2,1)}) %reduce-scatter.13.cloned.1.call-update) | async-done | bytes 1179664 | tf_op jit(solution)/shard_map/reduce_scatter | solution.py:336
  950.3 48.9 %psum.22 = f32[1536]{0:T(1024)S(1)} all-reduce(f32[1536]{0:T(1024)S(1)} %get-tuple-element.124), channel_id=1, replica_groups=mesh['seq'=4,'fsdp'=8] {'seq','fsdp'}, use_global_device_ids=true, to_apply=%region_19.20 | all-reduce | flops 1536 | bytes 12288 | tf_op jit(solution)/shard_map/psum | solution.py:501
  1004.9 21.5 %reduce-scatter.17.cloned.1.call-done = bf16[192,1536]{1,0:T(8,128)(2,1)} async-done(((bf16[1536,1536]{1,0:T(8,128)(2,1)}), bf16[192,1536]{1,0:T(8,128)(2,1)}) %reduce-scatter.17.cloned.1.call-update) | async-done | bytes 589840 | tf_op jit(solution)/shard_map/reduce_scatter | solution.py:340
  (503 shorter events, 485.4 us)
Async XLA Ops:
  7.2 98.9 %all-gather.8.cloned.1.call-start = ((), (), s32[]{:S(2)}) async-start(), calls=%async_computation.11 | async-start | bytes 2654208 | tf_op jit(solution)/shard_map/all_gather | solution.py:403
  9.1 99.9 %all-gather.6.cloned.1.call-start = ((), (), s32[]{:S(2)}) async-start(), calls=%async_computation.10 | async-start | bytes 4423680 | tf_op jit(solution)/shard_map/all_gather | solution.py:328
  23.3 191.0 %all-gather.10.cloned.1.call-start = ((), (), s32[]{:S(2)}) async-start(), calls=%async_computation.12 | async-start | bytes 3981312 | tf_op jit(solution)/shard_map/all_gather | solution.py:328
  49.7 279.9 %all-gather.12.cloned.1.call-start = ((), (), s32[]{:S(2)}) async-start(), calls=%async_computation.13 | async-start | bytes 10616832 | tf_op jit(solution)/shard_map/all_gather | solution.py:328
  51.0 307.5 %all-gather.14.cloned.1.call-start = ((), (), s32[]{:S(2)}) async-start(), calls=%async_computation.14 | async-start | bytes 5308416 | tf_op jit(solution)/shard_map/all_gather | solution.py:410
  51.0 26.9 %collective-permute-start = (bf16[320,1536]{1,0:T(8,128)(2,1)S(1)}, bf16[320,1536]{1,0:T(8,128)(2,1)S(1)}, u32[]{:S(2)}, u32[]{:S(2)}) collective-permute-start(bf16[320,1536]{1,0:T(8,128)(2,1)S(1)} %bitcast.143), channel_id=1, source_target_pairs={{0,8},{8,0},{16,24},{24,16},{1,9},{9,1},{17,25},{25,17},{2,10},{10... | collective-permute-start | bytes 2949128 | tf_op jit(solution)/shard_map/ppermute | solution.py:74
  52.3 154.0 %collective-permute-start.30 = (bf16[320,1536]{1,0:T(8,128)(2,1)}, bf16[320,1536]{1,0:T(8,128)(2,1)}, u32[]{:S(2)}, u32[]{:S(2)}) collective-permute-start(bf16[320,1536]{1,0:T(8,128)(2,1)} %bitcast.31), channel_id=1, source_target_pairs={{0,8},{8,0},{16,24},{24,16},{1,9},{9,1},{17,25},{25,17},{2,10},{10... | collective-permute-start | bytes 2949128 | tf_op jit(solution)/shard_map/ppermute | solution.py:74
  53.8 150.1 %collective-permute-start.31 = (bf16[320,1536]{1,0:T(8,128)(2,1)}, bf16[320,1536]{1,0:T(8,128)(2,1)}, u32[]{:S(2)}, u32[]{:S(2)}) collective-permute-start(bf16[320,1536]{1,0:T(8,128)(2,1)} %bitcast.31), channel_id=1, source_target_pairs={{0,16},{8,24},{16,0},{24,8},{1,17},{9,25},{17,1},{25,9},{2,18},{10... | collective-permute-start | bytes 2949128 | tf_op jit(solution)/shard_map/ppermute | solution.py:74
  55.2 656.1 %all-reduce.7.cloned.1.call-start = ((), (), s32[]{:S(2)}) async-start(), calls=%async_computation.18 | async-start | bytes 139264 | tf_op jit(solution)/shard_map/psum | solution.py:498
  76.5 27.2 %collective-permute-start.2 = (bf16[160,1536]{1,0:T(8,128)(2,1)S(1)}, bf16[160,1536]{1,0:T(8,128)(2,1)S(1)}, u32[]{:S(2)}, u32[]{:S(2)}) collective-permute-start(bf16[160,1536]{1,0:T(8,128)(2,1)S(1)} %slice.398), channel_id=1, source_target_pairs={{0,8},{8,0},{16,24},{24,16},{1,9},{9,1},{17,25},{25,17},{2,10},{10... | collective-permute-start | bytes 1474568 | tf_op jit(solution)/shard_map/ppermute | solution.py:74
  77.9 26.3 %collective-permute-start.3 = (bf16[160,1536]{1,0:T(8,128)(2,1)S(1)}, bf16[160,1536]{1,0:T(8,128)(2,1)S(1)}, u32[]{:S(2)}, u32[]{:S(2)}) collective-permute-start(bf16[160,1536]{1,0:T(8,128)(2,1)S(1)} %slice.399), channel_id=1, source_target_pairs={{0,16},{8,24},{16,0},{24,8},{1,17},{9,25},{17,1},{25,9},{2,18},{10... | collective-permute-start | bytes 1474568 | tf_op jit(solution)/shard_map/ppermute | solution.py:74
  197.9 28.2 %collective-permute-start.10 = (bf16[320,1536]{1,0:T(8,128)(2,1)}, bf16[320,1536]{1,0:T(8,128)(2,1)}, u32[]{:S(2)}, u32[]{:S(2)}) collective-permute-start(bf16[320,1536]{1,0:T(8,128)(2,1)} %get-tuple-element.138), channel_id=1, source_target_pairs={{0,8},{8,0},{16,24},{24,16},{1,9},{9,1},{17,25},{25,17},{2,10},{10... | collective-permute-start | bytes 2949128 | tf_op jit(solution)/shard_map/ppermute | solution.py:74
  205.8 91.9 %collective-permute-start.32 = (bf16[160,1536]{1,0:T(8,128)(2,1)}, bf16[160,1536]{1,0:T(8,128)(2,1)}, u32[]{:S(2)}, u32[]{:S(2)}) collective-permute-start(bf16[160,1536]{1,0:T(8,128)(2,1)} %slice.440), channel_id=1, source_target_pairs={{0,8},{8,0},{16,24},{24,16},{1,9},{9,1},{17,25},{25,17},{2,10},{10... | collective-permute-start | bytes 1474568 | tf_op jit(solution)/shard_map/ppermute | solution.py:74
  208.2 91.3 %collective-permute-start.33 = (bf16[160,1536]{1,0:T(8,128)(2,1)}, bf16[160,1536]{1,0:T(8,128)(2,1)}, u32[]{:S(2)}, u32[]{:S(2)}) collective-permute-start(bf16[160,1536]{1,0:T(8,128)(2,1)} %slice.441), channel_id=1, source_target_pairs={{0,16},{8,24},{16,0},{24,8},{1,17},{9,25},{17,1},{25,9},{2,18},{10... | collective-permute-start | bytes 1474568 | tf_op jit(solution)/shard_map/ppermute | solution.py:74
  519.0 196.6 %all-reduce.5.cloned.1.call-start = ((), (), s32[]{:S(2)}) async-start(), calls=%async_computation.15 | async-start | bytes 3342336 | tf_op jit(solution)/shard_map/psum | solution.py:479
  525.6 221.4 %reduce-scatter.15.cloned.1.call-start = ((), (), s32[]{:S(2)}) async-start(), calls=%async_computation.21 | async-start | bytes 1327104 | tf_op jit(solution)/shard_map/reduce_scatter | solution.py:340
  534.5 256.2 %reduce-scatter.7.cloned.1.call-start = ((), (), s32[]{:S(2)}) async-start(), calls=%async_computation.16 | async-start | bytes 3981312 | tf_op jit(solution)/shard_map/reduce_scatter | solution.py:336
  611.6 223.7 %reduce-scatter.11.cloned.1.call-start = ((), (), s32[]{:S(2)}) async-start(), calls=%async_computation.19 | async-start | bytes 3981312 | tf_op jit(solution)/shard_map/reduce_scatter | solution.py:336
  625.3 311.9 %reduce-scatter.13.cloned.1.call-start = ((), (), s32[]{:S(2)}) async-start(), calls=%async_computation.20 | async-start | bytes 10616832 | tf_op jit(solution)/shard_map/reduce_scatter | solution.py:336
  652.8 350.5 %reduce-scatter.9.cloned.1.call-start = ((), (), s32[]{:S(2)}) async-start(), calls=%async_computation.17 | async-start | bytes 1327104 | tf_op jit(solution)/shard_map/reduce_scatter | solution.py:340
  663.8 362.6 %reduce-scatter.17.cloned.1.call-start = ((), (), s32[]{:S(2)}) async-start(), calls=%async_computation.22 | async-start | bytes 5308416 | tf_op jit(solution)/shard_map/reduce_scatter | solution.py:340
  759.1 28.9 %collective-permute-start.59 = (bf16[160,1536]{1,0:T(8,128)(2,1)S(1)}, bf16[160,1536]{1,0:T(8,128)(2,1)S(1)}, u32[]{:S(2)}, u32[]{:S(2)}) collective-permute-start(bf16[160,1536]{1,0:T(8,128)(2,1)S(1)} %slice.659), channel_id=1, source_target_pairs={{0,16},{8,24},{16,0},{24,8},{1,17},{9,25},{17,1},{25,9},{2,18},{10... | collective-permute-start | bytes 1474568 | tf_op jit(solution)/shard_map/ppermute | solution.py:74
  790.7 149.1 %all-to-all-start.2 = ((bf16[4,48,1152]{2,1,0:T(8,128)(2,1)}), bf16[4,48,1152]{2,1,0:T(8,128)(2,1)S(1)}, u32[]{:S(2)}, u32[]{:S(2)}) async-start(bf16[4,48,1152]{2,1,0:T(8,128)(2,1)} %bitcast.189), calls=%async_computation.3 | async-start | bytes 884736 | tf_op jit(solution)/shard_map/all_to_all | solution.py:323
  939.8 91.0 %all-to-all-start.3 = ((bf16[4,48,4224]{2,1,0:T(8,128)(2,1)}), bf16[4,48,4224]{2,1,0:T(8,128)(2,1)}, u32[]{:S(2)}, u32[]{:S(2)}) async-start(bf16[4,48,4224]{2,1,0:T(8,128)(2,1)} %pad_maximum_fusion.3), calls=%async_computation.7 | async-start | bytes 3244032 | tf_op jit(solution)/shard_map/all_to_all | solution.py:323
  (111 other events, 1434.6 us)
Sparse Core Ops, SparseCore 0:
  10.3 32.2 all-gather.7
  44.3 43.1 all-gather.5
  89.1 40.4 all-gather.9
  131.7 87.9 all-gather.11
  221.1 51.3 all-gather.13
  519.1 120.1 all-reduce.6
  642.4 73.0 all-reduce.4
  717.8 29.0 reduce-scatter.14
  749.3 41.4 reduce-scatter.6
  793.0 42.3 reduce-scatter.10
  837.7 99.4 reduce-scatter.12
  939.9 30.2 reduce-scatter.8
  972.5 53.8 reduce-scatter.16

commit v2 on v1

--- a/solution.py
+++ b/solution.py
@@ -329,15 +329,44 @@
     return gathered.reshape(nf, n, r, c).transpose(1, 0, 2, 3).reshape(n * nf * r, c)
 
 
-def scatter_columns(grad, n, nf):
+def columns_by_owner(grad, n, nf):
     rows, c = grad.shape
     r = rows // (n * nf)
-    ordered = grad.astype(bf16).reshape(n, nf, r, c).transpose(1, 0, 2, 3).reshape(rows, c)
-    return lax.psum_scatter(ordered, "fsdp", scatter_dimension=0, tiled=True).reshape(n, r, c)
-
-
-def scatter_plain(grad):
-    return lax.psum_scatter(grad.astype(bf16), "fsdp", scatter_dimension=0, tiled=True)
+    return grad.astype(bf16).reshape(n, nf, r, c).transpose(1, 0, 2, 3).reshape(rows, c)
+
+
+def rows_by_owner(grad, n, nf):
+    rows, columns = grad.shape
+    r = rows // nf
+    return grad.reshape(nf, r, n, columns // n).transpose(0, 2, 1, 3).reshape(nf * n * r, columns // n)
+
+
+def share(rows_of_fsdp, n):
+    rows, c = rows_of_fsdp.shape
+    return to_seq(rows_of_fsdp.reshape(n, rows // n, c))
+
+
+def rows_to_pieces(shard, n):
+    r, columns = shard.shape
+    return shard.reshape(r, n, columns // n).transpose(1, 0, 2).reshape(n * r, columns // n)
+
+
+def after(value, *others):
+    return lax.optimization_barrier((value,) + others)[0]
+
+
+def sum_over_seq(value, n):
+    if n != 4:
+        return lax.psum(value, "seq")
+    half = value.shape[1] // 2
+
+    def step(part, j):
+        low = part.astype(bf16)
+        return low.astype(f32) + hop(low, j).astype(f32)
+
+    return jnp.concatenate(
+        [step(step(value[:, :half], 1), 2), step(step(value[:, half:], 2), 1)], axis=1
+    )
 
 
 def pad_heads(value, parts):
@@ -388,11 +417,15 @@
         [column_parts(proj_self, 3, n), jnp.broadcast_to(small[None], (n, r, LANES))], axis=2
     )
     self_pieces = to_seq(self_in)
-    rest_in = jnp.concatenate(
-        [column_parts(proj_keyval, 2, n), column_parts(proj_query, 1, n), column_parts(proj_gateup, 2, n)],
-        axis=2,
-    )
-    rest_pieces = to_seq(rest_in)
+    mid_pieces = to_seq(
+        after(
+            jnp.concatenate([column_parts(proj_keyval, 2, n), column_parts(proj_query, 1, n)], axis=2),
+            self_pieces,
+        )
+    )
+    group_tokens = gather_rows(after(tokens[0], self_pieces), n)
+    gateup_pieces = to_seq(after(column_parts(proj_gateup, 2, n), mid_pieces))
+
     self_all = gather_columns(self_pieces, n, nf)
     w_self = self_all[:, : 3 * wide]
     vectors = self_all[:, 3 * wide : 3 * wide + 12]
@@ -400,22 +433,27 @@
     b_gateup = vectors[:, 4:12].reshape(2 * FF).astype(f32)
     b_gate = lax.dynamic_slice_in_dim(b_gateup, me * hidden, hidden, 0)
     b_upper = lax.dynamic_slice_in_dim(b_gateup, FF + me * hidden, hidden, 0)
-    outs = lax.all_gather(jnp.concatenate([out_self, out_cross], axis=0), "fsdp", axis=0, tiled=True)
-    outs = outs.reshape(nf, 2, r, D)
-    w_out = outs[:, 0].reshape(nf * r, D)
-    w_cross = outs[:, 1].reshape(nf * r, D)
-    kvq = gather_columns(rest_pieces[:, :, : 3 * wide], n, nf)
+    mid = jnp.concatenate(
+        [
+            mid_pieces.reshape(n * r, 3 * wide),
+            rows_to_pieces(out_self, n),
+            rows_to_pieces(out_cross, n),
+        ],
+        axis=1,
+    )
+    mid = lax.all_gather(mid, "fsdp", axis=0, tiled=True).reshape(nf, n, r, 5 * wide)
+    kvq = mid[..., : 3 * wide].transpose(1, 0, 2, 3).reshape(D, 3 * wide)
     w_keyval, w_query = kvq[:, : 2 * wide], kvq[:, 2 * wide :]
-    w_gateup = gather_columns(rest_pieces[:, :, 3 * wide :], n, nf)
-    w_down = lax.all_gather(proj_down, "fsdp", axis=0, tiled=True)
+    w_out = mid[..., 3 * wide : 4 * wide].transpose(0, 2, 1, 3).reshape(nf * r, D)
+    w_cross = mid[..., 4 * wide :].transpose(0, 2, 1, 3).reshape(nf * r, D)
+    w_gateup = gather_columns(gateup_pieces, n, nf)
+    w_down = lax.all_gather(after(proj_down, gateup_pieces), "fsdp", axis=0, tiled=True)
 
     group_lengths = lengths[0]
     order = block_ids(n)
     all_rows = (order[:, None] * rows + jnp.arange(rows, dtype=jnp.int32)[None, :]).reshape(group)
     ids, positions = seq_info(all_rows, group_lengths)
     tables = angle_tables(positions)
-    group_tokens = gather_rows(tokens[0], n)
-    group_grad = gather_rows(grad_output[0], n)
 
     def block(value, j):
         return lax.slice_in_dim(value, j * rows, (j + 1) * rows, axis=0)
@@ -424,6 +462,7 @@
     normal_one, scaled_one, _ = norm_rows(inputs, gain_one)
     normed_one = norm_rows(group_tokens.astype(f32), gain_one)[2].astype(bf16)
     packed = pad_heads(dot(normed_one, w_self), 3)
+    group_grad = gather_rows(after(grad_output[0], packed), n)
     q, k, v, mixed, lse = attend(packed, packed, packed, (0, pairs, 2 * pairs), pairs, ids, ids, tables)
     mixed_in = mixed[:, :wide]
     first = inputs + scatter_rows(lambda j: dot(block(mixed_in, j), w_out), n)
@@ -453,13 +492,17 @@
 
     grad_rows = grad_output[0].astype(f32)
     grad_b_down = jnp.sum(grad_rows, axis=0)
+    grad_w_down = outer_sum(active, group_grad).astype(bf16)
     grad_active = back_prod(group_grad, w_down)
     grad_gate = grad_active * upper * sigma * (1.0 + gate * (1.0 - sigma))
     grad_upper = grad_active * silu_gate
     grad_gateup = jnp.concatenate([grad_gate, grad_upper], axis=1).astype(bf16)
-    grad_w_down = scatter_plain(outer_sum(active, group_grad))
+    own_down = lax.psum_scatter(grad_w_down, "fsdp", scatter_dimension=0, tiled=True)
+    grad_gateup, result = lax.optimization_barrier((grad_gateup, result))
     through = scatter_rows(lambda j: back_prod(block(grad_gateup, j), w_gateup), n)
-    grad_w_gateup = scatter_columns(outer_sum(normed_three, grad_gateup), n, nf)
+    grad_w_gateup = columns_by_owner(outer_sum(normed_three, grad_gateup), n, nf)
+    through, grad_w_gateup = lax.optimization_barrier((through, grad_w_gateup))
+    own_gateup = lax.psum_scatter(after(grad_w_gateup, own_down), "fsdp", scatter_dimension=0, tiled=True)
     grad_b_gateup = jnp.sum(grad_gateup.astype(f32), axis=0)
     through, grad_gain_three = norm_back(through, normal_three, scaled_three, gain_three)
     grad_second = grad_rows + through
@@ -472,54 +515,82 @@
     dcq, dck, dcv = dcq[:, :wide], dck[:count, :wide], dcv[:count, :wide]
     through = scatter_rows(lambda j: back_prod(block(dcq, j), w_query), n)
     grad_keyval = jnp.concatenate([dck, dcv], axis=1)
-    grad_w_cross = scatter_plain(outer_sum(cmix_in, group_second))
-    grad_w_kvq = scatter_columns(
-        jnp.concatenate([outer_sum(cond_rows, grad_keyval), outer_sum(normed_two, dcq)], axis=1), n, nf
-    )
-    grad_cond = lax.psum(back_prod(grad_keyval, w_keyval), "seq").reshape(1, SEQS_GRP, COND, D)
+    grad_w_cross = outer_sum(cmix_in, group_second).astype(bf16)
+    b_whole = lax.dynamic_update_slice(
+        jnp.zeros((2, FF), f32), grad_b_gateup.reshape(2, hidden), (0, me * hidden)
+    )
+    vectors = jnp.concatenate(
+        [v.reshape(n, nf, r, -1) for v in (grad_gain_three, grad_b_down, b_whole)], axis=3
+    )
+    vectors = vectors.astype(bf16).transpose(1, 0, 2, 3).reshape(nf * n * r, -1)
+    vectors = jnp.pad(vectors, ((0, 0), (0, LANES - vectors.shape[1])))
+    grad_w_mid = jnp.concatenate(
+        [
+            columns_by_owner(outer_sum(cond_rows, grad_keyval), n, nf),
+            columns_by_owner(outer_sum(normed_two, dcq), n, nf),
+            vectors,
+            rows_by_owner(grad_w_cross, n, nf),
+        ],
+        axis=1,
+    )
+    through, grad_w_mid = lax.optimization_barrier((through, grad_w_mid))
+    own_mid = lax.psum_scatter(after(grad_w_mid, own_gateup), "fsdp", scatter_dimension=0, tiled=True)
     through, grad_gain_two = norm_back(through, normal_two, scaled_two, gain_two)
     grad_first = grad_second + through
 
     group_first = gather_rows(grad_first.astype(bf16), n)
+    own_gateup = share(after(own_gateup, group_first), n)
     grad_mixed = pad_heads(back_prod(group_first, w_out).astype(bf16), 1)
+    grad_w_out = outer_sum(mixed_in, group_first).astype(bf16)
     dq, dk, dv = attend_back(q, k, v, (0, 0, 0), pairs, grad_mixed, mixed, lse, ids, ids, tables)
+    own_gateup = after(own_gateup, dq)
     grad_packed = jnp.concatenate([dq[:, :wide], dk[:, :wide], dv[:, :wide]], axis=1)
+    w_grad = outer_sum(normed_one, grad_packed)
+    gain_part = (jnp.sum(w_grad * w_self.astype(f32), axis=1) / gain_one).reshape(n, nf, r, 1)
+    gain_part = jnp.concatenate([gain_part, grad_gain_two.reshape(n, nf, r, 1)], axis=3)
+    gain_part = gain_part.astype(bf16).transpose(1, 0, 2, 3).reshape(nf * n * r, 2)
+    grad_w_self = jnp.concatenate(
+        [
+            columns_by_owner(w_grad, n, nf),
+            jnp.pad(gain_part, ((0, 0), (0, LANES - 2))),
+            rows_by_owner(grad_w_out, n, nf),
+        ],
+        axis=1,
+    )
+    grad_packed, grad_w_self, own_gateup = lax.optimization_barrier((grad_packed, grad_w_self, own_gateup))
+    own_self = lax.psum_scatter(after(grad_w_self, own_mid), "fsdp", scatter_dimension=0, tiled=True)
     through = scatter_rows(lambda j: back_prod(block(grad_packed, j), w_self), n)
-    grad_w_out = scatter_plain(outer_sum(mixed_in, group_first))
-    grad_w_self = scatter_columns(outer_sum(normed_one, grad_packed), n, nf)
-    through, grad_gain_one = norm_back(through, normal_one, scaled_one, gain_one)
-    grad_inputs = grad_first + through
-
-    rest = to_seq(jnp.concatenate([grad_w_kvq, grad_w_gateup], axis=2))
-    own_self = to_seq(grad_w_self)
-    place = me * nf + lax.axis_index("fsdp")
-    b_whole = jnp.zeros((2, FF), f32)
-    b_whole = lax.dynamic_update_slice(b_whole, grad_b_gateup.reshape(2, hidden), (0, me * hidden))
-    early = lax.psum(
-        jnp.concatenate([grad_gain_two, grad_gain_three, grad_b_down, b_whole.reshape(2 * FF)]), ALL
-    )
-    late = lax.psum(grad_gain_one, ALL)
-
-    def mine(vector):
-        count = vector.shape[0] // (n * nf)
-        return lax.dynamic_slice_in_dim(vector, place * count, count, 0)
+    grad_cond = sum_over_seq(after(back_prod(grad_keyval, w_keyval), through), n)
+    grad_cond = grad_cond.reshape(1, SEQS_GRP, COND, D)
+    grad_inputs = grad_first + norm_back(through, normal_one, scaled_one, gain_one)[0]
+
+    def joined(pieces):
+        return pieces.reshape(n, r, wide).transpose(1, 0, 2).reshape(r, D)
+
+    split = 3 * wide + LANES
+    mid_part = share(own_mid[:, :split], n)
+    vectors = jnp.sum(mid_part[:, :, 3 * wide :].astype(f32), axis=0)
+    own_cross = joined(own_mid[:, split:])
+    own_out = joined(own_self[:, split:])
+    self_part = share(own_self[:, :split], n)
+    gains = jnp.sum(self_part[:, :, 3 * wide :].astype(f32), axis=0)
 
     return (
         result.astype(bf16)[None],
         grad_inputs[None],
         grad_cond,
-        mine(late),
-        natural_columns(own_self, 3, n).astype(f32),
-        grad_w_out.astype(f32),
-        mine(early[:D]),
-        natural_columns(rest[:, :, 2 * wide : 3 * wide], 1, n).astype(f32),
-        natural_columns(rest[:, :, : 2 * wide], 2, n).astype(f32),
-        grad_w_cross.astype(f32),
-        mine(early[D : 2 * D]),
-        natural_columns(rest[:, :, 3 * wide :], 2, n).astype(f32),
-        mine(early[3 * D :]),
-        grad_w_down.astype(f32),
-        mine(early[2 * D : 3 * D]),
+        gains[:, 0],
+        natural_columns(self_part[:, :, : 3 * wide], 3, n).astype(f32),
+        own_out.astype(f32),
+        gains[:, 1],
+        natural_columns(mid_part[:, :, 2 * wide : 3 * wide], 1, n).astype(f32),
+        natural_columns(mid_part[:, :, : 2 * wide], 2, n).astype(f32),
+        own_cross.astype(f32),
+        vectors[:, 0],
+        natural_columns(own_gateup, 2, n).astype(f32),
+        vectors[:, 2:10].reshape(8 * r),
+        own_down.astype(f32),
+        vectors[:, 1],
     )
 
 

time: 1070 us -> 842 us (0.79)
  waiting for transfers between devices: 409 us -> 211 us
  blocking collectives: 82.7 us -> 28.5 us
  starting transfers between devices: 71 us -> 83.8 us
  other arithmetic: 61.2 us -> 72.1 us
    reduce_scatter x6 -> x4, waiting for transfers between devices: 193 us -> 0.05 us  [the longest x1 0.02 us: shards(): lax.psum_scatter(after(grad_w_self, own_mid), 'fsdp', scatter_dimension=0...]
    psum x1 -> x0, blocking collectives: 48.9 us -> none  [shards(): late = lax.psum(grad_gain_one, ALL)]
    ppermute x60 -> x64, waiting for transfers between devices: 216 us -> 190 us  [hop(): return lax.ppermute(value, 'seq', [(i, i ^ j) for i in range(4)])]
    all_to_all x2 -> x4, waiting for transfers between devices: 0.01 us -> 20.9 us  [to_seq(): return lax.all_to_all(pieces, 'seq', 0, 0, tiled=True)]
    dot_general x16, matrix products: 79.2 us -> 63.9 us  [back_prod(): lax.dot_general(left, weight, (((1,), (1,)), ((), ())), preferred_element...]
    ppermute x60 -> x64, starting transfers between devices: 60.8 us -> 67.6 us  [hop(): return lax.ppermute(value, 'seq', [(i, i ^ j) for i in range(4)])]
    unnamed x147 -> x200, local copies, waits for them, and re-layouts: 38.7 us -> 37.7 us
  transfers between devices with their start and end apart: 75 -> 76, of which waited for: 42 -> 41; matrix products, arithmetic and copies ran while one was open for 27% -> 38% of each run, Pallas kernels for 8% -> 13%
where the time goes in v2:
time: 842 us; the launch traced here: 829 us
  waiting for transfers between devices  211 us (25%)
  matrix products  180 us (21%)
  local copies, waits for them, and re-layouts  133 us (16%)
  Pallas kernels  104 us (12%)
  starting transfers between devices  83.8 us (10%)
  other arithmetic  72.1 us (9%)
  blocking collectives  28.5 us (3%)
  between operations  16.3 us (2%)
    ppermute x64, waiting for transfers between devices, hop(): return lax.ppermute(value, 'seq', [(i, i ^ j) for i in range(4)])  190 us
    ppermute x64, starting transfers between devices, hop(): return lax.ppermute(value, 'seq', [(i, i ^ j) for i in range(4)])  67.6 us
    dot_general x17, matrix products, dot(): return jnp.dot(left, right, preferred_element_type=f32)  64.4 us
    dot_general x16, matrix products, back_prod(): lax.dot_general(left, weight, (((1,), (1,)), ((), ())), preferred_element...  63.9 us
    pallas_call x2, Pallas kernels, attend(): pl.pallas_call(functools.partial(attend_kernel, rope, tile), out_shape=sh...  54.2 us
    dot_general x7, matrix products, outer_sum(): lax.dot_general(left, right, (((0,), (0,)), ((), ())), preferred_element_...  51.8 us
    pallas_call x2, Pallas kernels, attend_back(): pl.pallas_call(functools.partial(attend_back_kernel, rope, tile), out_sha...  49.4 us
    unnamed x200, local copies, waits for them, and re-layouts  37.7 us
  transfers between devices with their start and end apart: 76, of which 41 were waited for; matrix products, arithmetic and copies ran while one was open for 38% of the time, Pallas kernels for 13%

profile of v2, /device:TPU:8, one launch (start us, length us, event | category | flops | bytes accessed | tf_op | source)
XLA Modules:
  0.0 828.5 jit_solution(5615338156081525194)
XLA Ops:
  10.9 12.0 %all_to_all.30 = bf16[4,48,1280]{2,1,0:T(8,128)(2,1)} all-to-all(bf16[4,48,1280]{2,1,0:T(8,128)(2,1)S(1)} %pad_maximum_fusion.5), channel_id=1, replica_groups=mesh['seq'=4,'fsdp'=8] {'seq'}, dimensions={0} | all-to-all | bytes 983040 | tf_op jit(solution)/shard_map/all_to_all | solution.py:323
  37.9 16.5 %all_to_all.31 = bf16[4,48,3072]{2,1,0:T(8,128)(2,1)} all-to-all(bf16[4,48,3072]{2,1,0:T(8,128)(2,1)S(1)} %reshape.459), channel_id=1, replica_groups=mesh['seq'=4,'fsdp'=8] {'seq'}, dimensions={0} | all-to-all | bytes 2359296 | tf_op jit(solution)/shard_map/all_to_all | solution.py:323
  65.6 15.6 %collective-permute-done.1 = bf16[320,1536]{1,0:T(8,128)(2,1)S(1)} collective-permute-done((bf16[320,1536]{1,0:T(8,128)(2,1)S(1)}, bf16[320,1536]{1,0:T(8,128)(2,1)S(1)}, u32[]{:S(2)}, u32[]{:S(2)}) %collective-permute-start.1) | collective-permute-done | bytes 983072 | tf_op jit(solution)/shard_map/ppermute | solution.py:74
  101.5 9.4 %fusion.49.refs_0_.refs_1_.refs_2_ = f32[1280,1152]{1,0:T(8,128)} fusion(bf16[1536,1280]{1,0:T(8,128)(2,1)S(1)} %bitcast.208, bf16[1280,1536]{1,0:T(8,128)(2,1)} %constant_dynamic-update-slice_fusion, f32[1536]{0:T(1024)S(1)} %get-tuple-element.193, f32[1280]{0:T(1024)S(1)} %add_rsqrt_fusion, f32[1280]{0:T(1024)S(1)} %broadcast_multiply_fusion), kind=kOutput, calls=%fused_computation.101 | convolution fusion | flops 4539678720 | bytes 13393920 | tf_op jit(solution)/shard_map/dot_general | solution.py:62
  114.1 38.4 %attend_self.1 = (bf16[1280,384]{1,0:T(8,128)(2,1)}, bf16[1280,384]{1,0:T(8,128)(2,1)}, bf16[1280,384]{1,0:T(8,128)(2,1)}, bf16[1280,384]{1,0:T(8,128)(2,1)}, f32[3,8,1280]{2,1,0:T(8,128)}) custom-call(f32[1280,1152]{1,0:T(8,128)} %fusion.49.refs_0_.refs_1_.refs_2_, f32[1280,1152]{1,0:T(8,128)} %fusion.49.refs_0_.refs_1_.refs_2_, ...), custom_call_target="tpu_custom_call" | custom-call | flops 5033164800 | bytes 11796480 | tf_op jit(solution)/shard_map/attend_self/pallas_call | solution.py:250
  190.4 11.5 %collective-permute-done.10 = bf16[160,1536]{1,0:T(8,128)(2,1)S(1)} collective-permute-done((bf16[160,1536]{1,0:T(8,128)(2,1)S(1)}, bf16[160,1536]{1,0:T(8,128)(2,1)S(1)}, u32[]{:S(2)}, u32[]{:S(2)}) %collective-permute-start.10) | collective-permute-done | bytes 491552 | tf_op jit(solution)/shard_map/ppermute | solution.py:74
  210.0 14.8 %collective-permute-done.15 = bf16[320,1536]{1,0:T(8,128)(2,1)S(1)} collective-permute-done((bf16[320,1536]{1,0:T(8,128)(2,1)S(1)}, bf16[320,1536]{1,0:T(8,128)(2,1)S(1)}, u32[]{:S(2)}, u32[]{:S(2)}) %collective-permute-start.15) | collective-permute-done | bytes 983072 | tf_op jit(solution)/shard_map/ppermute | solution.py:74
  239.7 15.7 %attend_cross.1 = (bf16[1280,384]{1,0:T(8,128)(2,1)}, f32[3,8,1280]{2,1,0:T(8,128)}) custom-call(bf16[1280,384]{1,0:T(8,128)(2,1)} %convolution_convert_fusion.8.refs_0_, bf16[272,768]{1,0:T(8,128)(2,1)} %pad.17.refs_1_.refs_2_, bf16[272,768]{1,0:T(8,128)(2,1)} %pad.17.refs_1_.refs_2_, s32[1,1280]{1,0:T(1,128)} %broadcast_in_dim.31.refs_5_.refs_3_.refs_6_.refs_8_, ...), custom_call_target="tpu_custom_call" | custom-call | flops 1069547520 | bytes 7151616 | tf_op jit(solution)/shard_map/attend_cross/pallas_call | solution.py:250
  274.9 13.5 %collective-permute-done.20 = bf16[160,1536]{1,0:T(8,128)(2,1)S(1)} collective-permute-done((bf16[160,1536]{1,0:T(8,128)(2,1)S(1)}, bf16[160,1536]{1,0:T(8,128)(2,1)S(1)}, u32[]{:S(2)}, u32[]{:S(2)}) %collective-permute-start.20) | collective-permute-done | bytes 491552 | tf_op jit(solution)/shard_map/ppermute | solution.py:74
  294.7 11.4 %fusion.140 = f32[1280,1536]{1,0:T(8,128)} fusion(bf16[1280,1536]{1,0:T(8,128)(2,1)} %constant_dynamic-update-slice_fusion.5, bf16[1536,1536]{1,0:T(8,128)(2,1)} %all-gather.7.cloned.1.call-done), kind=kOutput, calls=%fused_computation.311 | convolution fusion | flops 6039797760 | bytes 16515072 | tf_op jit(solution)/shard_map/dot_general | solution.py:70
  324.2 8.7 %copy.226 = bf16[4,8,48,3072]{3,2,1,0:T(8,128)(2,1)} copy(bf16[4,8,48,3072]{3,2,0,1:T(8,128)(2,1)} %bitcast.195) | data formatting | bytes 18874368 | tf_op jit(solution)/shard_map/transpose | solution.py:329
  333.0 11.4 %convolution_add_fusion = f32[1280,1536]{1,0:T(8,128)} fusion(bf16[1280,1536]{1,0:T(8,128)(2,1)} %constant_dynamic-update-slice_fusion.15, bf16[1536,3072]{1,0:T(8,128)(2,1)} %bitcast.196, f32[1536]{0:T(1024)S(1)} %get-tuple-element.236), kind=kOutput, calls=%fused_computation.9 | convolution fusion | flops 6041763840 | bytes 16521216 | tf_op jit(solution)/shard_map/dot_general | solution.py:62
  344.4 16.2 %multiply_convert_fusion = (bf16[1280,1536]{1,0:T(8,128)(2,1)}, bf16[1280,1536]{1,0:T(8,128)(2,1)}, bf16[1280,1536]{1,0:T(8,128)(2,1)}) fusion(f32[1280,1536]{1,0:T(8,128)} %convolution_add_fusion, f32[1280,1536]{1,0:T(8,128)} %fusion.140, f32[1536]{0:T(1024)S(1)} %get-tuple-element.235, bf16[1280,1536]{1,0:T(8,128)(2,1)} %constant_dynamic-update-slice_fusion.15, ...), kind=kOutput, calls=%fused_computation.17 | convolution fusion | flops 6071255040 | bytes 36184064 | tf_op jit(solution)/shard_map/dot_general | solution.py:62
  360.6 10.8 %convolution_convert_fusion.1 = bf16[1536,1536]{1,0:T(8,128)(2,1)} fusion(bf16[1280,1536]{1,0:T(8,128)(2,1)} %get-tuple-element.212, bf16[1280,1536]{1,0:T(8,128)(2,1)} %constant_dynamic-update-slice_fusion.5), kind=kOutput, calls=%fused_computation.22 | convolution fusion | flops 6042157056 | bytes 12582912 | tf_op jit(solution)/shard_map/dot_general | solution.py:66
  430.7 17.3 %convolution_convert_fusion = bf16[1536,3072]{1,0:T(8,128)(2,1)} fusion(bf16[1280,1536]{1,0:T(8,128)(2,1)} %constant_dynamic-update-slice_fusion.15, bf16[1280,3072]{1,0:T(8,128)(2,1)S(1)} %bitcast.172), kind=kOutput, calls=%fused_computation.3 | convolution fusion | flops 12084314112 | bytes 21233664 | tf_op jit(solution)/shard_map/dot_general | solution.py:66
  452.5 8.7 %copy.227 = bf16[4,8,48,3072]{3,2,0,1:T(8,128)(2,1)} copy(bf16[4,8,48,3072]{3,2,1,0:T(8,128)(2,1)} %bitcast.204) | data formatting | bytes 18874368 | tf_op jit(solution)/shard_map/reshape | solution.py:335
  475.0 9.5 %collective-permute-done.36 = bf16[160,1536]{1,0:T(8,128)(2,1)S(1)} collective-permute-done((bf16[160,1536]{1,0:T(8,128)(2,1)S(1)}, bf16[160,1536]{1,0:T(8,128)(2,1)S(1)}, u32[]{:S(2)}, u32[]{:S(2)}) %collective-permute-start.36) | collective-permute-done | bytes 491552 | tf_op jit(solution)/shard_map/ppermute | solution.py:74
  484.8 8.8 %maximum_add_fusion.3 = f32[320,1536]{1,0:T(8,128)} fusion(f32[160,1536]{1,0:T(8,128)S(1)} %convert_add_fusion.5, f32[160,1536]{1,0:T(8,128)S(1)} %convert_add_fusion.6, bf16[1536,3072]{1,0:T(8,128)(2,1)} %bitcast.198, bf16[1280,3072]{1,0:T(8,128)(2,1)} %pad_maximum_fusion), kind=kOutput, calls=%fused_computation.68 | convolution fusion | flops 3020881920 | bytes 15335424 | tf_op jit(solution)/shard_map/dot_general | solution.py:70
  507.7 9.7 %collective-permute-done.41 = bf16[320,1536]{1,0:T(8,128)(2,1)S(1)} collective-permute-done((bf16[320,1536]{1,0:T(8,128)(2,1)}, bf16[320,1536]{1,0:T(8,128)(2,1)S(1)}, u32[]{:S(2)}, u32[]{:S(2)}) %collective-permute-start.41) | collective-permute-done | bytes 983072 | tf_op jit(solution)/shard_map/ppermute | solution.py:74
  534.0 14.2 %back_cross.1 = (bf16[1280,384]{1,0:T(8,128)(2,1)}, bf16[272,384]{1,0:T(8,128)(2,1)}, bf16[272,384]{1,0:T(8,128)(2,1)}) custom-call(bf16[1280,384]{1,0:T(8,128)(2,1)} %convolution_convert_fusion.8.refs_0_, bf16[272,768]{1,0:T(8,128)(2,1)} %pad.17.refs_1_.refs_2_, bf16[272,768]{1,0:T(8,128)(2,1)} %pad.17.refs_1_.refs_2_, ...), custom_call_target="tpu_custom_call" | custom-call | flops 2673868800 | bytes 7151616 | tf_op jit(solution)/shard_map/back_cross/pallas_call | solution.py:285
  613.5 16.5 %collective-permute-done.51 = bf16[320,1536]{1,0:T(8,128)(2,1)S(1)} collective-permute-done((bf16[320,1536]{1,0:T(8,128)(2,1)S(1)}, bf16[320,1536]{1,0:T(8,128)(2,1)S(1)}, u32[]{:S(2)}, u32[]{:S(2)}) %collective-permute-start.51) | collective-permute-done | bytes 983072 | tf_op jit(solution)/shard_map/ppermute | solution.py:74
  651.8 35.2 %back_self.1 = (bf16[1280,384]{1,0:T(8,128)(2,1)}, bf16[1280,384]{1,0:T(8,128)(2,1)}, bf16[1280,384]{1,0:T(8,128)(2,1)}) custom-call(bf16[1280,384]{1,0:T(8,128)(2,1)} %get-tuple-element.63.refs_0_, bf16[1280,384]{1,0:T(8,128)(2,1)} %get-tuple-element.64.refs_1_, bf16[1280,384]{1,0:T(8,128)(2,1)} %get-tuple-element.65.refs_2_, ...), custom_call_target="tpu_custom_call" | custom-call | flops 12582912000 | bytes 11796480 | tf_op jit(solution)/shard_map/back_self/pallas_call | solution.py:285
  691.4 9.8 %fusion.129 = (bf16[1536,1152]{1,0:T(8,128)(2,1)S(1)}, f32[1536]{0:T(1024)}) fusion(bf16[1536,1280]{1,0:T(8,128)(2,1)S(1)} %bitcast.210, bf16[1280,1152]{1,0:T(8,128)(2,1)S(1)} %constant_dynamic-update-slice_fusion.30, bf16[1280,1536]{1,0:T(8,128)(2,1)} %constant_dynamic-update-slice_fusion, f32[1536]{0:T(1024)S(1)} %copy-done.62, ...), kind=kOutput, calls=%fused_computation.300 | convolution fusion | flops 4546755072 | bytes 13981696 | tf_op jit(solution)/shard_map/dot_general | solution.py:66
  714.4 11.4 %all-to-all-done.3 = bf16[4,48,3072]{2,1,0:T(8,128)(2,1)} async-done(((bf16[4,48,3072]{2,1,0:T(8,128)(2,1)}), bf16[4,48,3072]{2,1,0:T(8,128)(2,1)}, u32[]{:S(2)}, u32[]{:S(2)}) %all-to-all-start.3) | async-done | bytes 1179680 | tf_op jit(solution)/shard_map/all_to_all | solution.py:323
  (591 shorter events, 465.1 us)
Async XLA Ops:
  7.2 90.8 %all-gather.5.cloned.1.call-start = ((), (), s32[]{:S(2)}) async-start(), calls=%async_computation.10 | async-start | bytes 4423680 | tf_op jit(solution)/shard_map/all_gather | solution.py:328
  28.0 137.8 %all-gather.9.cloned.1.call-start = ((), (), s32[]{:S(2)}) async-start(), calls=%async_computation.12 | async-start | bytes 6635520 | tf_op jit(solution)/shard_map/all_gather | solution.py:444
  35.0 259.6 %all-gather.7.cloned.1.call-start = ((), (), s32[]{:S(2)}) async-start(), calls=%async_computation.11 | async-start | bytes 5308416 | tf_op jit(solution)/shard_map/all_gather | solution.py:450
  54.4 269.8 %all-gather.11.cloned.1.call-start = ((), (), s32[]{:S(2)}) async-start(), calls=%async_computation.13 | async-start | bytes 10616832 | tf_op jit(solution)/shard_map/all_gather | solution.py:328
  58.5 22.8 %collective-permute-start = (bf16[320,1536]{1,0:T(8,128)(2,1)S(1)}, bf16[320,1536]{1,0:T(8,128)(2,1)S(1)}, u32[]{:S(2)}, u32[]{:S(2)}) collective-permute-start(bf16[320,1536]{1,0:T(8,128)(2,1)S(1)} %bitcast.183), channel_id=1, source_target_pairs={{0,8},{8,0},{16,24},{24,16},{1,9},{9,1},{17,25},{25,17},{2,10},{10... | collective-permute-start | bytes 2949128 | tf_op jit(solution)/shard_map/ppermute | solution.py:74
  59.5 21.7 %collective-permute-start.1 = (bf16[320,1536]{1,0:T(8,128)(2,1)S(1)}, bf16[320,1536]{1,0:T(8,128)(2,1)S(1)}, u32[]{:S(2)}, u32[]{:S(2)}) collective-permute-start(bf16[320,1536]{1,0:T(8,128)(2,1)S(1)} %bitcast.184), channel_id=1, source_target_pairs={{0,16},{8,24},{16,0},{24,8},{1,17},{9,25},{17,1},{25,9},{2,18},{10... | collective-permute-start | bytes 2949128 | tf_op jit(solution)/shard_map/ppermute | solution.py:74
  85.2 408.4 %reduce-scatter.5.cloned.1.call-start = ((), (), s32[]{:S(2)}) async-start(), calls=%async_computation.14 | async-start | bytes 5308416 | tf_op jit(solution)/shard_map/reduce_scatter | solution.py:500
  110.9 44.1 %collective-permute-start.4 = (bf16[320,1536]{1,0:T(8,128)(2,1)S(1)}, bf16[320,1536]{1,0:T(8,128)(2,1)}, u32[]{:S(2)}, u32[]{:S(2)}) collective-permute-start(bf16[320,1536]{1,0:T(8,128)(2,1)S(1)} %bitcast.215), channel_id=1, source_target_pairs={{0,8},{8,0},{16,24},{24,16},{1,9},{9,1},{17,25},{25,17},{2,10},{10... | collective-permute-start | bytes 2949128 | tf_op jit(solution)/shard_map/ppermute | solution.py:74
  112.1 40.5 %collective-permute-start.5 = (bf16[320,1536]{1,0:T(8,128)(2,1)S(1)}, bf16[320,1536]{1,0:T(8,128)(2,1)}, u32[]{:S(2)}, u32[]{:S(2)}) collective-permute-start(bf16[320,1536]{1,0:T(8,128)(2,1)S(1)} %bitcast.216), channel_id=1, source_target_pairs={{0,16},{8,24},{16,0},{24,8},{1,17},{9,25},{17,1},{25,9},{2,18},{10... | collective-permute-start | bytes 2949128 | tf_op jit(solution)/shard_map/ppermute | solution.py:74
  174.4 27.6 %collective-permute-start.13 = (bf16[160,1536]{1,0:T(8,128)(2,1)S(1)}, bf16[160,1536]{1,0:T(8,128)(2,1)S(1)}, u32[]{:S(2)}, u32[]{:S(2)}) collective-permute-start(bf16[160,1536]{1,0:T(8,128)(2,1)S(1)} %slice.685), channel_id=1, source_target_pairs={{0,16},{8,24},{16,0},{24,8},{1,17},{9,25},{17,1},{25,9},{2,18},{10... | collective-permute-start | bytes 1474568 | tf_op jit(solution)/shard_map/ppermute | solution.py:74
  203.8 21.8 %collective-permute-start.14 = (bf16[320,1536]{1,0:T(8,128)(2,1)S(1)}, bf16[320,1536]{1,0:T(8,128)(2,1)S(1)}, u32[]{:S(2)}, u32[]{:S(2)}) collective-permute-start(bf16[320,1536]{1,0:T(8,128)(2,1)S(1)} %get-tuple-element.211), channel_id=1, source_target_pairs={{0,8},{8,0},{16,24},{24,16},{1,9},{9,1},{17,25},{25,17},{2,10},{10... | collective-permute-start | bytes 2949128 | tf_op jit(solution)/shard_map/ppermute | solution.py:74
  262.9 25.6 %collective-permute-start.23 = (bf16[160,1536]{1,0:T(8,128)(2,1)S(1)}, bf16[160,1536]{1,0:T(8,128)(2,1)S(1)}, u32[]{:S(2)}, u32[]{:S(2)}) collective-permute-start(bf16[160,1536]{1,0:T(8,128)(2,1)S(1)} %slice.683), channel_id=1, source_target_pairs={{0,16},{8,24},{16,0},{24,8},{1,17},{9,25},{17,1},{25,9},{2,18},{10... | collective-permute-start | bytes 1474568 | tf_op jit(solution)/shard_map/ppermute | solution.py:74
  291.6 22.8 %collective-permute-start.24 = (bf16[320,1536]{1,0:T(8,128)(2,1)}, bf16[320,1536]{1,0:T(8,128)(2,1)S(1)}, u32[]{:S(2)}, u32[]{:S(2)}) collective-permute-start(bf16[320,1536]{1,0:T(8,128)(2,1)} %get-tuple-element.209), channel_id=1, source_target_pairs={{0,8},{8,0},{16,24},{24,16},{1,9},{9,1},{17,25},{25,17},{2,10},{10... | collective-permute-start | bytes 2949128 | tf_op jit(solution)/shard_map/ppermute | solution.py:74
  292.6 19.8 %collective-permute-start.25 = (bf16[320,1536]{1,0:T(8,128)(2,1)}, bf16[320,1536]{1,0:T(8,128)(2,1)}, u32[]{:S(2)}, u32[]{:S(2)}) collective-permute-start(bf16[320,1536]{1,0:T(8,128)(2,1)} %get-tuple-element.209), channel_id=1, source_target_pairs={{0,16},{8,24},{16,0},{24,8},{1,17},{9,25},{17,1},{25,9},{2,18},{10... | collective-permute-start | bytes 2949128 | tf_op jit(solution)/shard_map/ppermute | solution.py:74
  371.4 232.7 %reduce-scatter.7.cloned.1.call-start = ((), (), s32[]{:S(2)}) async-start(), calls=%async_computation.15 | async-start | bytes 10616832 | tf_op jit(solution)/shard_map/reduce_scatter | solution.py:505
  377.1 19.6 %collective-permute-start.29 = (bf16[160,1536]{1,0:T(8,128)(2,1)}, bf16[160,1536]{1,0:T(8,128)(2,1)}, u32[]{:S(2)}, u32[]{:S(2)}) collective-permute-start(bf16[160,1536]{1,0:T(8,128)(2,1)} %get-tuple-element.225), channel_id=1, source_target_pairs={{0,8},{8,0},{16,24},{24,16},{1,9},{9,1},{17,25},{25,17},{2,10},{10... | collective-permute-start | bytes 1474568 | tf_op jit(solution)/shard_map/ppermute | solution.py:74
  425.1 41.9 %collective-permute-start.35 = (bf16[160,1536]{1,0:T(8,128)(2,1)}, bf16[160,1536]{1,0:T(8,128)(2,1)S(1)}, u32[]{:S(2)}, u32[]{:S(2)}) collective-permute-start(bf16[160,1536]{1,0:T(8,128)(2,1)} %get-tuple-element.223), channel_id=1, source_target_pairs={{0,8},{8,0},{16,24},{24,16},{1,9},{9,1},{17,25},{25,17},{2,10},{10... | collective-permute-start | bytes 1474568 | tf_op jit(solution)/shard_map/ppermute | solution.py:74
  493.7 232.0 %reduce-scatter.9.cloned.1.call-start = ((), (), s32[]{:S(2)}) async-start(), calls=%async_computation.16 | async-start | bytes 5750784 | tf_op jit(solution)/shard_map/reduce_scatter | solution.py:537
  611.8 19.5 %collective-permute-start.50 = (bf16[320,1536]{1,0:T(8,128)(2,1)S(1)}, bf16[320,1536]{1,0:T(8,128)(2,1)S(1)}, u32[]{:S(2)}, u32[]{:S(2)}) collective-permute-start(bf16[320,1536]{1,0:T(8,128)(2,1)S(1)} %get-tuple-element.203), channel_id=1, source_target_pairs={{0,8},{8,0},{16,24},{24,16},{1,9},{9,1},{17,25},{25,17},{2,10},{10... | collective-permute-start | bytes 2949128 | tf_op jit(solution)/shard_map/ppermute | solution.py:74
  706.0 19.8 %all-to-all-start.3 = ((bf16[4,48,3072]{2,1,0:T(8,128)(2,1)}), bf16[4,48,3072]{2,1,0:T(8,128)(2,1)}, u32[]{:S(2)}, u32[]{:S(2)}) async-start(bf16[4,48,3072]{2,1,0:T(8,128)(2,1)} %bitcast.238), calls=%async_computation.5 | async-start | bytes 2359296 | tf_op jit(solution)/shard_map/all_to_all | solution.py:323
  710.2 96.5 %reduce-scatter.11.cloned.1.call-start = ((), (), s32[]{:S(2)}) async-start(), calls=%async_computation.17 | async-start | bytes 5750784 | tf_op jit(solution)/shard_map/reduce_scatter | solution.py:561
  733.7 20.0 %collective-permute-start.55 = (bf16[160,1536]{1,0:T(8,128)(2,1)}, bf16[160,1536]{1,0:T(8,128)(2,1)}, u32[]{:S(2)}, u32[]{:S(2)}) collective-permute-start(bf16[160,1536]{1,0:T(8,128)(2,1)} %get-tuple-element.219), channel_id=1, source_target_pairs={{0,8},{8,0},{16,24},{24,16},{1,9},{9,1},{17,25},{25,17},{2,10},{10... | collective-permute-start | bytes 1474568 | tf_op jit(solution)/shard_map/ppermute | solution.py:74
  737.5 20.5 %collective-permute-start.54 = (bf16[160,1536]{1,0:T(8,128)(2,1)}, bf16[160,1536]{1,0:T(8,128)(2,1)}, u32[]{:S(2)}, u32[]{:S(2)}) collective-permute-start(bf16[160,1536]{1,0:T(8,128)(2,1)} %slice.676), channel_id=1, source_target_pairs={{0,8},{8,0},{16,24},{24,16},{1,9},{9,1},{17,25},{25,17},{2,10},{10... | collective-permute-start | bytes 1474568 | tf_op jit(solution)/shard_map/ppermute | solution.py:74
  742.5 24.9 %collective-permute-start.59 = (bf16[160,1536]{1,0:T(8,128)(2,1)}, bf16[160,1536]{1,0:T(8,128)(2,1)}, u32[]{:S(2)}, u32[]{:S(2)}) collective-permute-start(bf16[160,1536]{1,0:T(8,128)(2,1)} %slice.675), channel_id=1, source_target_pairs={{0,16},{8,24},{16,0},{24,8},{1,17},{9,25},{17,1},{25,9},{2,18},{10... | collective-permute-start | bytes 1474568 | tf_op jit(solution)/shard_map/ppermute | solution.py:74
  (140 other events, 1744.3 us)
Sparse Core Ops, SparseCore 0:
  23.1 43.0 all-gather.4
  68.4 59.5 all-gather.8
  129.6 50.8 all-gather.6
  182.1 88.2 all-gather.10
  371.5 52.5 reduce-scatter.4
  493.8 97.0 reduce-scatter.6
  604.2 56.8 reduce-scatter.8
  725.9 56.2 reduce-scatter.10

commit v3 on v2

--- a/solution.py
+++ b/solution.py
@@ -127,15 +127,55 @@
     return jnp.where(lane // HEAD == h, value, jnp.zeros_like(value))
 
 
-def row_mask(value, h):
-    row = lax.broadcasted_iota(jnp.int32, value.shape, 0)
-    return jnp.where(row // HEAD == h, value, jnp.zeros_like(value))
+FAR = 1e30
+
+
+def pieces_of(value):
+    high = value.astype(bf16).astype(f32)
+    rest = value - high
+    middle = rest.astype(bf16).astype(f32)
+    return high, middle, rest - middle
+
+
+def key_lanes(keys, kid, h):
+    lane = lax.broadcasted_iota(jnp.int32, keys.shape, 1)
+    spare = lane % HEAD
+    ones = jnp.where(spare <= SEQS_GRP + 3, 1.0, 0.0)
+    padding = jnp.where(spare == SEQS_GRP, jnp.where(kid < 0, 1.0, 0.0), ones)
+    extra = jnp.where(spare < SEQS_GRP, jnp.where(kid == spare, 1.0, 0.0), padding)
+    return jnp.where(lane // HEAD == h, keys.astype(f32), extra).astype(bf16)
+
+
+def query_rows(turned, qid, h, offsets=()):
+    row = lax.broadcasted_iota(jnp.int32, turned.shape, 0)
+    spare = row % HEAD
+    extra = jnp.where(spare <= SEQS_GRP, jnp.where(qid == spare, 0.0, -FAR), 0.0)
+    for j, offset in enumerate(offsets):
+        extra = jnp.where(spare == SEQS_GRP + 1 + j, offset, extra)
+    return jnp.where(row // HEAD == h, turned, extra).astype(bf16)
+
+
+def value_lanes(values, h):
+    lane = lax.broadcasted_iota(jnp.int32, values.shape, 1)
+    ones = jnp.where(lane % HEAD < 3, 1.0, 0.0)
+    return jnp.where(lane // HEAD == h, values.astype(f32), ones).astype(bf16)
+
+
+def grad_rows_of(turned, h, offsets):
+    row = lax.broadcasted_iota(jnp.int32, turned.shape, 0)
+    extra = jnp.zeros_like(turned)
+    for j, offset in enumerate(offsets):
+        extra = jnp.where(row % HEAD == j, offset, extra)
+    return jnp.where(row // HEAD == h, turned, extra).astype(bf16)
+
+
+PAIR = LANES // HEAD
 
 
 def attend_kernel(rope, tile, *refs):
     if rope:
         q_ref, k_ref, v_ref, cos_ref, sin_ref, qid_ref, kid_ref = refs[:7]
-        qo_ref, ko_ref, vo_ref, o_ref, lse_ref, qt, vt, ot, kb = refs[7:]
+        qo_ref, ko_ref, vo_ref, o_ref, lse_ref, qt, kb, vt, ot = refs[7:]
         q, k = q_ref[...], k_ref[...]
         q = (q * cos_ref[...] + swap_halves(q) * sin_ref[...]).astype(bf16)
         k = (k * cos_ref[...] + swap_halves(k) * sin_ref[...]).astype(bf16)
@@ -144,62 +184,78 @@
         ko_ref[...] = k
         vo_ref[...] = v
     else:
-        q_ref, k_ref, v_ref, qid_ref, kid_ref, o_ref, lse_ref, qt, vt, ot, kb = refs
+        q_ref, k_ref, v_ref, qid_ref, kid_ref, o_ref, lse_ref, qt, kb, vt, ot = refs
         q, k, v = q_ref[...], k_ref[...], v_ref[...]
-    kb[...] = k
-    qt[...] = q.astype(f32).T.astype(bf16)
+    turned = q.astype(f32).T * 0.125
+    for h in range(PAIR):
+        qt[h] = query_rows(turned, qid_ref[...], h)
+        kb[h] = key_lanes(k, kid_ref[...], h)
     vt[...] = v.astype(f32).T.astype(bf16)
-
-    def body(t, carry):
-        at = pl.ds(pl.multiple_of(t * tile, tile), tile)
-        queries = qt[:, at]
-        allowed = kid_ref[...] == qid_ref[:, at]
-        for h in range(LANES // HEAD):
-            s = dot(kb[...], row_mask(queries, h)) * 0.125
-            s = jnp.where(allowed, s, masked_score)
-            top = jnp.max(s, axis=0, keepdims=True)
-            e = jnp.exp(s - top)
-            total = jnp.sum(e, axis=0, keepdims=True)
-            p = (e * (1.0 / total)).astype(bf16)
-            ot[head_rows(h), at] = dot(vt[head_rows(h), :], p)
-            lse_ref[0, h : h + 1, at] = top + jnp.log(total)
-        return carry
-
-    lax.fori_loop(0, qt.shape[1] // tile, body, 0)
+    units = [(t * tile, h) for t in range(ot.shape[1] // tile) for h in range(PAIR)]
+
+    def scores(unit):
+        start, h = unit
+        return dot(kb[h], qt[h, :, start : start + tile])
+
+    later = scores(units[0])
+    for i, (start, h) in enumerate(units):
+        s = later
+        if i + 1 < len(units):
+            later = scores(units[i + 1])
+        at = slice(start, start + tile)
+        top = jnp.max(s, axis=0, keepdims=True)
+        e = jnp.exp(s - top)
+        total = jnp.sum(e, axis=0, keepdims=True)
+        ot[head_rows(h), at] = dot(vt[head_rows(h), :], e.astype(bf16)) * (1.0 / total)
+        lse_ref[0, h : h + 1, at] = top + jnp.log(total)
     o_ref[...] = ot[...].T.astype(bf16)
 
 
 def attend_back_kernel(rope, tile, *refs):
     if rope:
         q_ref, k_ref, v_ref, do_ref, o_ref, lse_ref, cos_ref, sin_ref, qid_ref, kid_ref = refs[:10]
-        dq_ref, dk_ref, dv_ref, qt, dot_t, kt, dqt, dk_acc, dv_acc, delta = refs[10:]
+        dq_ref, dk_ref, dv_ref, qt, gt, kb, vb, kt, dqt, dk_acc, dv_acc = refs[10:]
     else:
         q_ref, k_ref, v_ref, do_ref, o_ref, lse_ref, qid_ref, kid_ref = refs[:8]
-        dq_ref, dk_ref, dv_ref, qt, dot_t, kt, dqt, dk_acc, dv_acc, delta = refs[8:]
-    qt[...] = q_ref[...].astype(f32).T.astype(bf16)
+        dq_ref, dk_ref, dv_ref, qt, gt, kb, vb, kt, dqt, dk_acc, dv_acc = refs[8:]
+    turned = q_ref[...].astype(f32).T * 0.125
+    grads = do_ref[...].astype(f32).T
+    product = grads * o_ref[...].astype(f32).T
     kt[...] = k_ref[...].astype(f32).T.astype(bf16)
-    dof_t = do_ref[...].astype(f32).T
-    dot_t[...] = dof_t.astype(bf16)
-    product = dof_t * o_ref[...].astype(f32).T
-    for h in range(LANES // HEAD):
-        delta[h : h + 1, :] = jnp.sum(product[head_rows(h), :], axis=0, keepdims=True)
-    dk_acc[...] = jnp.zeros_like(dk_acc)
-    dv_acc[...] = jnp.zeros_like(dv_acc)
-
-    def body(t, carry):
-        at = pl.ds(pl.multiple_of(t * tile, tile), tile)
-        allowed = kid_ref[...] == qid_ref[:, at]
-        for h in range(LANES // HEAD):
-            s = dot(k_ref[...], row_mask(qt[:, at], h)) * 0.125
-            p = jnp.where(allowed, jnp.exp(s - lse_ref[0, h : h + 1, at]), 0.0)
-            dp = dot(v_ref[...], row_mask(dot_t[:, at], h))
-            dv_acc[...] += dot(p.astype(bf16), lane_mask(do_ref[at, :], h))
-            ds = (p * (dp - delta[h : h + 1, at])).astype(bf16)
-            dk_acc[...] += dot(ds, lane_mask(q_ref[at, :], h))
-            dqt[head_rows(h), at] = dot(kt[head_rows(h), :], ds)
-        return carry
-
-    lax.fori_loop(0, qt.shape[1] // tile, body, 0)
+    for h in range(PAIR):
+        delta = jnp.sum(product[head_rows(h), :], axis=0, keepdims=True)
+        qt[h] = query_rows(turned, qid_ref[...], h, pieces_of(-lse_ref[0, h : h + 1, :]))
+        gt[h] = grad_rows_of(grads, h, pieces_of(-delta))
+        kb[h] = key_lanes(k_ref[...], kid_ref[...], h)
+        vb[h] = value_lanes(v_ref[...], h)
+    tiles = dqt.shape[1] // tile
+    units = [(t * tile, h) for t in range(tiles) for h in range(PAIR)]
+
+    def products(unit):
+        start, h = unit
+        at = slice(start, start + tile)
+        return dot(kb[h], qt[h, :, at]), dot(vb[h], gt[h, :, at])
+
+    later = products(units[0])
+    low_p, low_ds = [], []
+    for i, (start, h) in enumerate(units):
+        s, dp = later
+        if i + 1 < len(units):
+            later = products(units[i + 1])
+        at = slice(start, start + tile)
+        p = jnp.exp(s)
+        ds = (p * dp).astype(bf16)
+        dqt[head_rows(h), at] = dot(kt[head_rows(h), :], ds)
+        low_p.append(p.astype(bf16))
+        low_ds.append(ds)
+        if h == PAIR - 1:
+            rows_do = jnp.concatenate([lane_mask(do_ref[at, :], j) for j in range(PAIR)], axis=0)
+            rows_q = jnp.concatenate([lane_mask(q_ref[at, :], j) for j in range(PAIR)], axis=0)
+            dv = dot(jnp.concatenate(low_p, axis=1), rows_do)
+            dk = dot(jnp.concatenate(low_ds, axis=1), rows_q)
+            dv_acc[...] = dv if start == 0 else dv_acc[...] + dv
+            dk_acc[...] = dk if start == 0 else dk_acc[...] + dk
+            low_p, low_ds = [], []
     dq = dqt[...].T * 0.125
     dk = dk_acc[...] * 0.125
     if rope:
@@ -226,6 +282,7 @@
 
 
 LIMIT = 56 * 1024 * 1024
+TILE, CHUNK, GTILE = 256, 320, 512
 
 
 def attend(q, k, v, offsets, pairs, qid, kid, tables=None):
@@ -254,10 +311,10 @@
         in_specs=ins,
         out_specs=outs,
         scratch_shapes=[
-            pltpu.VMEM((LANES, nq), bf16),
+            pltpu.VMEM((PAIR, LANES, nq), bf16),
+            pltpu.VMEM((PAIR, nk, LANES), bf16),
             pltpu.VMEM((LANES, nk), bf16),
             pltpu.VMEM((LANES, nq), f32),
-            pltpu.VMEM((nk, LANES), bf16),
         ],
         compiler_params=pltpu.CompilerParams(vmem_limit_bytes=LIMIT),
         cost_estimate=pl.CostEstimate(
@@ -289,13 +346,14 @@
         in_specs=ins,
         out_specs=[spec(nq), spec(nk), spec(nk)],
         scratch_shapes=[
-            pltpu.VMEM((LANES, nq), bf16),
-            pltpu.VMEM((LANES, nq), bf16),
+            pltpu.VMEM((PAIR, LANES, nq), bf16),
+            pltpu.VMEM((PAIR, LANES, nq), bf16),
+            pltpu.VMEM((PAIR, nk, LANES), bf16),
+            pltpu.VMEM((PAIR, nk, LANES), bf16),
             pltpu.VMEM((LANES, nk), bf16),
             pltpu.VMEM((LANES, nq), f32),
             pltpu.VMEM((nk, LANES), f32),
             pltpu.VMEM((nk, LANES), f32),
-            pltpu.VMEM((8, nq), f32),
         ],
         compiler_params=pltpu.CompilerParams(vmem_limit_bytes=LIMIT),
         cost_estimate=pl.CostEstimate(
@@ -305,6 +363,280 @@
         ),
         name="back_self" if rope else "back_cross",
     )(*args)
+
+
+def contract(left, right, dims):
+    return lax.dot_general(left, right, (dims, ((), ())), preferred_element_type=f32)
+
+
+def feed_kernel(chunk, *refs):
+    h_ref, gy_ref, wg_ref, wu_ref, wd_ref, bg_ref, bu_ref = refs[:7]
+    act_ref, dg_ref, du_ref, sg_ref, su_ref, dh_ref, both, total = refs[7:]
+    step = pl.program_id(0)
+    span = wg_ref.shape[0] * wg_ref.shape[2]
+    tile = wg_ref.shape[3]
+    for j in range(wg_ref.shape[1]):
+        at = slice(j * span, (j + 1) * span)
+        both[at, :tile] = wg_ref[:, j].reshape(span, tile)
+        both[at, tile:] = wu_ref[:, j].reshape(span, tile)
+    sg_ref[...] = jnp.zeros_like(sg_ref)
+    su_ref[...] = jnp.zeros_like(su_ref)
+
+    @pl.when(step == 0)
+    def _():
+        total[...] = jnp.zeros_like(total)
+
+    def rows_at(i):
+        return slice(i * chunk, (i + 1) * chunk)
+
+    def products(i):
+        at = rows_at(i)
+        return dot(h_ref[at, :], both[...]), contract(gy_ref[at, :], wd_ref[...], ((1,), (1,)))
+
+    def finish(i, pair, grad):
+        at = rows_at(i)
+        gate = pair[:, :tile] + bg_ref[...]
+        upper = pair[:, tile:] + bu_ref[...]
+        sigma = jax.nn.sigmoid(gate)
+        silu = gate * sigma
+        act_ref[at, :] = (silu * upper).astype(bf16)
+        dg = (grad * upper * sigma * (1.0 + gate * (1.0 - sigma))).astype(bf16)
+        du = (grad * silu).astype(bf16)
+        dg_ref[at, :] = dg
+        du_ref[at, :] = du
+        sg_ref[...] += jnp.sum(dg.astype(f32), axis=0, keepdims=True)
+        su_ref[...] += jnp.sum(du.astype(f32), axis=0, keepdims=True)
+        return jnp.concatenate([dg, du], axis=1)
+
+    chunks = h_ref.shape[0] // chunk
+    now = products(0)
+    for i in range(chunks):
+        later = products(i + 1) if i + 1 < chunks else None
+        grads = finish(i, *now)
+        total[rows_at(i), :] += contract(grads, both[...], ((1,), (1,)))
+        now = later
+
+    @pl.when(step == pl.num_programs(0) - 1)
+    def _():
+        dh_ref[...] = total[...].astype(bf16)
+
+
+def feed(h, gy, w_gateup, w_down, b_gate, b_upper):
+    rows = h.shape[0]
+    hidden = w_down.shape[0]
+    tile = TILE if rows <= 1280 else 128
+    steps = hidden // tile
+    lead = w_gateup.shape[:3]
+    chunk = CHUNK if rows % CHUNK == 0 else rows
+    one = pl.Buffered(1)
+    rows_all = pl.BlockSpec((rows, D), lambda t: (0, 0), pipeline_mode=one)
+    columns = pl.BlockSpec((rows, tile), lambda t: (0, t))
+    vector = pl.BlockSpec((1, tile), lambda t: (0, t))
+    return pl.pallas_call(
+        functools.partial(feed_kernel, chunk),
+        out_shape=[jax.ShapeDtypeStruct((rows, hidden), bf16)] * 3
+        + [jax.ShapeDtypeStruct((1, hidden), f32)] * 2
+        + [jax.ShapeDtypeStruct((rows, D), bf16)],
+        grid=(steps,),
+        in_specs=[
+            rows_all,
+            rows_all,
+            pl.BlockSpec(lead + (tile,), lambda t: (0, 0, 0, t)),
+            pl.BlockSpec(lead + (tile,), lambda t: (0, 0, 0, t + steps)),
+            pl.BlockSpec((tile, D), lambda t: (t, 0)),
+            vector,
+            vector,
+        ],
+        out_specs=[columns, columns, columns, vector, vector, rows_all],
+        scratch_shapes=[
+            pltpu.VMEM((D, 2 * tile), bf16),
+            pltpu.VMEM((rows, D), f32),
+        ],
+        compiler_params=pltpu.CompilerParams(vmem_limit_bytes=LIMIT),
+        cost_estimate=pl.CostEstimate(
+            flops=2 * 5 * rows * D * hidden,
+            bytes_accessed=2 * (3 * rows * D + 3 * rows * hidden + 3 * D * hidden),
+            transcendentals=rows * hidden,
+        ),
+        name="feed",
+    )(h, gy, w_gateup, w_gateup, w_down, b_gate[None], b_upper[None])
+
+
+def place_rows(out_ref, start, value):
+    nf, _, r, _ = out_ref.shape
+    width = value.shape[1]
+    out_ref[:, 0, :, start : start + width] = value.astype(bf16).reshape(nf, r, width)
+
+
+def gateup_kernel(h_ref, dg_ref, du_ref, out_ref, turned):
+    step = pl.program_id(0)
+    half = pl.num_programs(0) // 2
+    nf, n, r, tile = out_ref.shape
+    wide = nf * r
+
+    @pl.when(step == 0)
+    def _():
+        for s in range(n):
+            at = slice(s * wide, (s + 1) * wide)
+            turned[at, :] = h_ref[:, at].T
+
+    def fill(grad):
+        for s in range(n):
+            value = dot(turned[s * wide : (s + 1) * wide, :], grad)
+            out_ref[:, s] = value.astype(bf16).reshape(nf, r, tile)
+
+    @pl.when(step < half)
+    def _():
+        fill(dg_ref[...])
+
+    @pl.when(step >= half)
+    def _():
+        fill(du_ref[...])
+
+
+def gateup_grads(h, dg, du, n, nf):
+    rows, hidden = dg.shape
+    r, wide = D // (n * nf), D // n
+    if r % 16 or wide % LANES:
+        joined = jnp.concatenate([dg, du], axis=1)
+        return columns_by_owner(outer_sum(h, joined), n, nf)
+    tile = GTILE
+    half = hidden // tile
+    out = pl.pallas_call(
+        gateup_kernel,
+        out_shape=jax.ShapeDtypeStruct((nf, n, r, 2 * hidden), bf16),
+        grid=(2 * half,),
+        in_specs=[
+            pl.BlockSpec((rows, D), lambda t: (0, 0), pipeline_mode=pl.Buffered(1)),
+            pl.BlockSpec((rows, tile), lambda t: (0, jnp.minimum(t, half - 1))),
+            pl.BlockSpec((rows, tile), lambda t: (0, jnp.maximum(t - half, 0))),
+        ],
+        out_specs=pl.BlockSpec((nf, n, r, tile), lambda t: (0, 0, 0, t)),
+        scratch_shapes=[pltpu.VMEM((D, rows), bf16)],
+        compiler_params=pltpu.CompilerParams(vmem_limit_bytes=LIMIT),
+        cost_estimate=pl.CostEstimate(
+            flops=4 * rows * D * hidden, bytes_accessed=4 * D * hidden + 6 * rows * hidden, transcendentals=0
+        ),
+        name="gateup_grads",
+    )(h, dg, du)
+    return out.reshape(D, 2 * hidden)
+
+
+def mid_kernel(cond_ref, dk_ref, dv_ref, h_ref, dq_ref, mix_ref, gy_ref, vec_ref, out_ref):
+    wide = dq_ref.shape[1]
+    outer = ((0,), (0,))
+    place_rows(out_ref, 0, contract(cond_ref[...], dk_ref[...], outer))
+    place_rows(out_ref, wide, contract(cond_ref[...], dv_ref[...], outer))
+    place_rows(out_ref, 2 * wide, contract(h_ref[...], dq_ref[...], outer))
+    out_ref[:, 0, :, 3 * wide : 3 * wide + LANES] = vec_ref[:, 0]
+    place_rows(out_ref, 3 * wide + LANES, contract(mix_ref[...], gy_ref[...], outer))
+
+
+def mid_grads(cond, dk, dv, h, dq, mix, gy, vectors, n, nf):
+    rows, wide = dq.shape
+    r = D // (n * nf)
+    if r % 16 or wide % LANES:
+        return jnp.concatenate(
+            [
+                columns_by_owner(outer_sum(cond, jnp.concatenate([dk, dv], axis=1)), n, nf),
+                columns_by_owner(outer_sum(h, dq), n, nf),
+                vectors,
+                rows_by_owner(outer_sum(mix, gy).astype(bf16), n, nf),
+            ],
+            axis=1,
+        )
+    count = cond.shape[0]
+    columns = 4 * wide + LANES
+
+    def full(value):
+        return pl.BlockSpec(value.shape, lambda s: (0, 0), pipeline_mode=pl.Buffered(1))
+
+    out = pl.pallas_call(
+        mid_kernel,
+        out_shape=jax.ShapeDtypeStruct((nf, n, r, columns), bf16),
+        grid=(n,),
+        in_specs=[
+            pl.BlockSpec((count, wide), lambda s: (0, s)),
+            full(dk),
+            full(dv),
+            pl.BlockSpec((rows, wide), lambda s: (0, s)),
+            full(dq),
+            full(mix),
+            pl.BlockSpec((rows, wide), lambda s: (0, s)),
+            pl.BlockSpec((nf, 1, r, LANES), lambda s: (0, s, 0, 0)),
+        ],
+        out_specs=pl.BlockSpec((nf, 1, r, columns), lambda s: (0, s, 0, 0)),
+        compiler_params=pltpu.CompilerParams(vmem_limit_bytes=LIMIT),
+        cost_estimate=pl.CostEstimate(
+            flops=2 * D * wide * (2 * count + 2 * rows),
+            bytes_accessed=2 * D * (columns + 2 * rows + count),
+            transcendentals=0,
+        ),
+        name="mid_grads",
+    )(cond, dk, dv, h, dq, mix, gy, vectors.reshape(nf, n, r, LANES))
+    return out.reshape(D, columns)
+
+
+def self_kernel(h_ref, dq_ref, dk_ref, dv_ref, w_ref, gain_ref, mix_ref, gy_ref, vec_ref, out_ref):
+    wide = dq_ref.shape[1]
+    nf, _, r, _ = out_ref.shape
+    outer = ((0,), (0,))
+    along = jnp.zeros((wide, 1), f32)
+    for j, ref in enumerate((dq_ref, dk_ref, dv_ref)):
+        grad = contract(h_ref[...], ref[...], outer)
+        place_rows(out_ref, j * wide, grad)
+        weight = w_ref[:, j * wide : (j + 1) * wide].astype(f32)
+        along = along + jnp.sum(grad * weight, axis=1, keepdims=True)
+    along = jnp.broadcast_to(along / gain_ref[...], (wide, LANES)).reshape(nf, r, LANES)
+    lane = lax.broadcasted_iota(jnp.int32, along.shape, 2)
+    vec = jnp.where(lane == 0, along, vec_ref[:, 0].astype(f32))
+    out_ref[:, 0, :, 3 * wide : 3 * wide + LANES] = vec.astype(bf16)
+    place_rows(out_ref, 3 * wide + LANES, contract(mix_ref[...], gy_ref[...], outer))
+
+
+def self_grads(h, dq, dk, dv, w_self, gain, mix, gy, vectors, n, nf):
+    rows, wide = dq.shape
+    r = D // (n * nf)
+    if r % 16 or wide % LANES:
+        grad = outer_sum(h, jnp.concatenate([dq, dk, dv], axis=1))
+        along = (jnp.sum(grad * w_self.astype(f32), axis=1) / gain).astype(bf16)
+        along = along.reshape(n, nf, r, 1).transpose(1, 0, 2, 3).reshape(D, 1)
+        return jnp.concatenate(
+            [
+                columns_by_owner(grad, n, nf),
+                jnp.concatenate([along, vectors[:, 1:]], axis=1),
+                rows_by_owner(outer_sum(mix, gy).astype(bf16), n, nf),
+            ],
+            axis=1,
+        )
+    columns = 4 * wide + LANES
+
+    def full(value):
+        return pl.BlockSpec(value.shape, lambda s: (0, 0), pipeline_mode=pl.Buffered(1))
+
+    out = pl.pallas_call(
+        self_kernel,
+        out_shape=jax.ShapeDtypeStruct((nf, n, r, columns), bf16),
+        grid=(n,),
+        in_specs=[
+            pl.BlockSpec((rows, wide), lambda s: (0, s)),
+            full(dq),
+            full(dk),
+            full(dv),
+            pl.BlockSpec((wide, 3 * wide), lambda s: (s, 0)),
+            pl.BlockSpec((wide, 1), lambda s: (s, 0)),
+            full(mix),
+            pl.BlockSpec((rows, wide), lambda s: (0, s)),
+            pl.BlockSpec((nf, 1, r, LANES), lambda s: (0, s, 0, 0)),
+        ],
+        out_specs=pl.BlockSpec((nf, 1, r, columns), lambda s: (0, s, 0, 0)),
+        compiler_params=pltpu.CompilerParams(vmem_limit_bytes=LIMIT),
+        cost_estimate=pl.CostEstimate(
+            flops=8 * D * wide * rows, bytes_accessed=2 * D * (columns + 2 * rows + 3 * wide), transcendentals=0
+        ),
+        name="self_grads",
+    )(h, dq, dk, dv, w_self, gain[:, None], mix, gy, vectors.reshape(nf, n, r, LANES))
+    return out.reshape(D, columns)
 
 
 def column_parts(shard, parts, n):
@@ -446,7 +778,10 @@
     w_keyval, w_query = kvq[:, : 2 * wide], kvq[:, 2 * wide :]
     w_out = mid[..., 3 * wide : 4 * wide].transpose(0, 2, 1, 3).reshape(nf * r, D)
     w_cross = mid[..., 4 * wide :].transpose(0, 2, 1, 3).reshape(nf * r, D)
-    w_gateup = gather_columns(gateup_pieces, n, nf)
+    w_gateup = lax.all_gather(gateup_pieces.reshape(n * r, 2 * hidden), "fsdp", axis=0, tiled=True)
+    w_gateup = w_gateup.reshape(nf, n, r, 2 * hidden)
+    if r % 16:
+        w_gateup = w_gateup.transpose(1, 0, 2, 3).reshape(1, 1, D, 2 * hidden)
     w_down = lax.all_gather(after(proj_down, gateup_pieces), "fsdp", axis=0, tiled=True)
 
     group_lengths = lengths[0]
@@ -483,27 +818,17 @@
 
     normal_three, scaled_three, normed = norm_rows(second, gain_three)
     normed_three = gather_rows(normed.astype(bf16), n)
-    gate = dot(normed_three, w_gateup[:, :hidden]) + b_gate
-    upper = dot(normed_three, w_gateup[:, hidden:]) + b_upper
-    sigma = jax.nn.sigmoid(gate)
-    silu_gate = gate * sigma
-    active = (silu_gate * upper).astype(bf16)
-    result = second + scatter_rows(lambda j: dot(block(active, j), w_down), n) + b_down
-
+    active, grad_gate, grad_upper, sum_gate, sum_upper, back_three = feed(
+        normed_three, group_grad, w_gateup, w_down, b_gate, b_upper
+    )
     grad_rows = grad_output[0].astype(f32)
     grad_b_down = jnp.sum(grad_rows, axis=0)
+    through = scatter_rows(lambda j: block(back_three, j).astype(f32), n)
     grad_w_down = outer_sum(active, group_grad).astype(bf16)
-    grad_active = back_prod(group_grad, w_down)
-    grad_gate = grad_active * upper * sigma * (1.0 + gate * (1.0 - sigma))
-    grad_upper = grad_active * silu_gate
-    grad_gateup = jnp.concatenate([grad_gate, grad_upper], axis=1).astype(bf16)
     own_down = lax.psum_scatter(grad_w_down, "fsdp", scatter_dimension=0, tiled=True)
-    grad_gateup, result = lax.optimization_barrier((grad_gateup, result))
-    through = scatter_rows(lambda j: back_prod(block(grad_gateup, j), w_gateup), n)
-    grad_w_gateup = columns_by_owner(outer_sum(normed_three, grad_gateup), n, nf)
+    grad_w_gateup = gateup_grads(normed_three, grad_gate, grad_upper, n, nf)
     through, grad_w_gateup = lax.optimization_barrier((through, grad_w_gateup))
     own_gateup = lax.psum_scatter(after(grad_w_gateup, own_down), "fsdp", scatter_dimension=0, tiled=True)
-    grad_b_gateup = jnp.sum(grad_gateup.astype(f32), axis=0)
     through, grad_gain_three = norm_back(through, normal_three, scaled_three, gain_three)
     grad_second = grad_rows + through
 
@@ -512,27 +837,18 @@
     dcq, dck, dcv = attend_back(
         cq, keyval, keyval, (0, 0, pairs), pairs, grad_cmix, cmix, clse, ids, cond_ids
     )
-    dcq, dck, dcv = dcq[:, :wide], dck[:count, :wide], dcv[:count, :wide]
+    dcq, dck, dcv = dcq[:, :wide], dck[:, :wide], dcv[:, :wide]
+    cond_full = jnp.pad(cond_rows, ((0, count_pad - count), (0, 0)))
     through = scatter_rows(lambda j: back_prod(block(dcq, j), w_query), n)
-    grad_keyval = jnp.concatenate([dck, dcv], axis=1)
-    grad_w_cross = outer_sum(cmix_in, group_second).astype(bf16)
     b_whole = lax.dynamic_update_slice(
-        jnp.zeros((2, FF), f32), grad_b_gateup.reshape(2, hidden), (0, me * hidden)
+        jnp.zeros((2, FF), f32), jnp.concatenate([sum_gate, sum_upper], axis=0), (0, me * hidden)
     )
     vectors = jnp.concatenate(
         [v.reshape(n, nf, r, -1) for v in (grad_gain_three, grad_b_down, b_whole)], axis=3
     )
     vectors = vectors.astype(bf16).transpose(1, 0, 2, 3).reshape(nf * n * r, -1)
     vectors = jnp.pad(vectors, ((0, 0), (0, LANES - vectors.shape[1])))
-    grad_w_mid = jnp.concatenate(
-        [
-            columns_by_owner(outer_sum(cond_rows, grad_keyval), n, nf),
-            columns_by_owner(outer_sum(normed_two, dcq), n, nf),
-            vectors,
-            rows_by_owner(grad_w_cross, n, nf),
-        ],
-        axis=1,
-    )
+    grad_w_mid = mid_grads(cond_full, dck, dcv, normed_two, dcq, cmix_in, group_second, vectors, n, nf)
     through, grad_w_mid = lax.optimization_barrier((through, grad_w_mid))
     own_mid = lax.psum_scatter(after(grad_w_mid, own_gateup), "fsdp", scatter_dimension=0, tiled=True)
     through, grad_gain_two = norm_back(through, normal_two, scaled_two, gain_two)
@@ -540,26 +856,24 @@
 
     group_first = gather_rows(grad_first.astype(bf16), n)
     own_gateup = share(after(own_gateup, group_first), n)
+    late_active = after(active, group_first)
+    result = second + scatter_rows(lambda j: dot(block(late_active, j), w_down), n) + b_down
     grad_mixed = pad_heads(back_prod(group_first, w_out).astype(bf16), 1)
-    grad_w_out = outer_sum(mixed_in, group_first).astype(bf16)
     dq, dk, dv = attend_back(q, k, v, (0, 0, 0), pairs, grad_mixed, mixed, lse, ids, ids, tables)
     own_gateup = after(own_gateup, dq)
-    grad_packed = jnp.concatenate([dq[:, :wide], dk[:, :wide], dv[:, :wide]], axis=1)
-    w_grad = outer_sum(normed_one, grad_packed)
-    gain_part = (jnp.sum(w_grad * w_self.astype(f32), axis=1) / gain_one).reshape(n, nf, r, 1)
-    gain_part = jnp.concatenate([gain_part, grad_gain_two.reshape(n, nf, r, 1)], axis=3)
-    gain_part = gain_part.astype(bf16).transpose(1, 0, 2, 3).reshape(nf * n * r, 2)
-    grad_w_self = jnp.concatenate(
-        [
-            columns_by_owner(w_grad, n, nf),
-            jnp.pad(gain_part, ((0, 0), (0, LANES - 2))),
-            rows_by_owner(grad_w_out, n, nf),
-        ],
-        axis=1,
-    )
-    grad_packed, grad_w_self, own_gateup = lax.optimization_barrier((grad_packed, grad_w_self, own_gateup))
+    dq, dk, dv = dq[:, :wide], dk[:, :wide], dv[:, :wide]
+    grad_packed = jnp.concatenate([dq, dk, dv], axis=1)
+    gains = grad_gain_two.astype(bf16).reshape(n, nf, r, 1).transpose(1, 0, 2, 3).reshape(D, 1)
+    gains = jnp.pad(gains, ((0, 0), (1, LANES - 2)))
+    grad_w_self = self_grads(
+        normed_one, dq, dk, dv, w_self, gain_one, mixed_in, group_first, gains, n, nf
+    )
+    grad_packed, grad_w_self, own_gateup, result = lax.optimization_barrier(
+        (grad_packed, grad_w_self, own_gateup, result)
+    )
     own_self = lax.psum_scatter(after(grad_w_self, own_mid), "fsdp", scatter_dimension=0, tiled=True)
     through = scatter_rows(lambda j: back_prod(block(grad_packed, j), w_self), n)
+    grad_keyval = jnp.concatenate([dck, dcv], axis=1)[:count]
     grad_cond = sum_over_seq(after(back_prod(grad_keyval, w_keyval), through), n)
     grad_cond = grad_cond.reshape(1, SEQS_GRP, COND, D)
     grad_inputs = grad_first + norm_back(through, normal_one, scaled_one, gain_one)[0]

time: 842 us -> 760 us (0.903)
  matrix products: 180 us -> 66.2 us
  Pallas kernels: 104 us -> 153 us
  local copies, waits for them, and re-layouts: 133 us -> 102 us
  waiting for transfers between devices: 211 us -> 231 us
    pallas_call x0 -> x4, Pallas kernels: none -> 83.9 us  [the longest x1 41.2 us: feed(): pl.pallas_call(functools.partial(feed_kernel, chunk), out_shape=[jax.Shap...]
    dot_general x7 -> x1, matrix products: 51.8 us -> 10 us  [outer_sum(): lax.dot_general(left, right, (((0,), (0,)), ((), ())), preferred_element_...]
    dot_general x16 -> x11, matrix products: 63.9 us -> 25.5 us  [back_prod(): lax.dot_general(left, weight, (((1,), (1,)), ((), ())), preferred_element...]
    dot_general x17 -> x15, matrix products: 64.4 us -> 30.6 us  [dot(): return jnp.dot(left, right, preferred_element_type=f32)]
    pallas_call x2, Pallas kernels: 54.2 us -> 29.6 us  [attend(): pl.pallas_call(functools.partial(attend_kernel, rope, tile), out_shape=sh...]
    ppermute x64, waiting for transfers between devices: 190 us -> 210 us  [hop(): return lax.ppermute(value, 'seq', [(i, i ^ j) for i in range(4)])]
    reshape x10 -> x1, local copies, waits for them, and re-layouts: 18.5 us -> 0.43 us  [shards(): grad_gain_two.astype(bf16).reshape(n, nf, r, 1).transpose(1, 0, 2, 3)]
    concatenate x3 -> x1, other arithmetic: 14.7 us -> 3.61 us  [shards(): grad_packed = jnp.concatenate([dq, dk, dv], axis=1)]
  transfers between devices with their start and end apart: 76 -> 76, of which waited for: 41 -> 36; matrix products, arithmetic and copies ran while one was open for 38% -> 28% of each run, Pallas kernels for 13% -> 15%
where the time goes in v3:
time: 760 us; the launch traced here: 751 us
  waiting for transfers between devices  231 us (30%)
  Pallas kernels  153 us (20%)
  local copies, waits for them, and re-layouts  102 us (13%)
  starting transfers between devices  83.5 us (11%)
  other arithmetic  70.8 us (9%)
  matrix products  66.2 us (9%)
  blocking collectives  28.5 us (4%)
  between operations  16.2 us (2%)
    ppermute x64, waiting for transfers between devices, hop(): return lax.ppermute(value, 'seq', [(i, i ^ j) for i in range(4)])  210 us
    ppermute x64, starting transfers between devices, hop(): return lax.ppermute(value, 'seq', [(i, i ^ j) for i in range(4)])  67.7 us
    pallas_call x1, Pallas kernels, feed(): pl.pallas_call(functools.partial(feed_kernel, chunk), out_shape=[jax.Shap...  41.2 us
    pallas_call x2, Pallas kernels, attend_back(): pl.pallas_call(functools.partial(attend_back_kernel, rope, tile), out_sha...  39 us
    unnamed x161, local copies, waits for them, and re-layouts  36 us
    dot_general x15, matrix products, dot(): return jnp.dot(left, right, preferred_element_type=f32)  30.6 us
    pallas_call x2, Pallas kernels, attend(): pl.pallas_call(functools.partial(attend_kernel, rope, tile), out_shape=sh...  29.6 us
    all_to_all x2, blocking collectives, to_seq(): return lax.all_to_all(pieces, 'seq', 0, 0, tiled=True)  28.5 us
  transfers between devices with their start and end apart: 76, of which 36 were waited for; matrix products, arithmetic and copies ran while one was open for 28% of the time, Pallas kernels for 15%

profile of v3, /device:TPU:8, one launch (start us, length us, event | category | flops | bytes accessed | tf_op | source)
XLA Modules:
  0.0 750.8 jit_solution(1303703600096083235)
XLA Ops:
  9.5 12.0 %all_to_all.30 = bf16[4,48,1280]{2,1,0:T(8,128)(2,1)} all-to-all(bf16[4,48,1280]{2,1,0:T(8,128)(2,1)S(1)} %pad_maximum_fusion.5), channel_id=1, replica_groups=mesh['seq'=4,'fsdp'=8] {'seq'}, dimensions={0} | all-to-all | bytes 983040 | tf_op jit(solution)/shard_map/all_to_all | solution.py:655
  36.6 16.5 %all_to_all.31 = bf16[4,48,3072]{2,1,0:T(8,128)(2,1)} all-to-all(bf16[4,48,3072]{2,1,0:T(8,128)(2,1)S(1)} %reshape.430), channel_id=1, replica_groups=mesh['seq'=4,'fsdp'=8] {'seq'}, dimensions={0} | all-to-all | bytes 2359296 | tf_op jit(solution)/shard_map/all_to_all | solution.py:655
  64.3 15.6 %collective-permute-done.1 = bf16[320,1536]{1,0:T(8,128)(2,1)S(1)} collective-permute-done((bf16[320,1536]{1,0:T(8,128)(2,1)S(1)}, bf16[320,1536]{1,0:T(8,128)(2,1)S(1)}, u32[]{:S(2)}, u32[]{:S(2)}) %collective-permute-start.1) | collective-permute-done | bytes 983072 | tf_op jit(solution)/shard_map/ppermute | solution.py:74
  103.7 7.0 fusion.103.refs_0_.refs_1_.refs_2_
  115.1 21.9 %attend_self.1 = (bf16[1280,384]{1,0:T(8,128)(2,1)}, bf16[1280,384]{1,0:T(8,128)(2,1)}, bf16[1280,384]{1,0:T(8,128)(2,1)}, bf16[1280,384]{1,0:T(8,128)(2,1)}, f32[3,8,1280]{2,1,0:T(8,128)}) custom-call(f32[1280,1152]{1,0:T(8,128)} %fusion.103.refs_0_.refs_1_.refs_2_, f32[1280,1152]{1,0:T(8,128)} %fusion.103.refs_0_.refs_1_.refs_2_, ...), custom_call_target="tpu_custom_call" | custom-call | flops 5033164800 | bytes 11796480 | tf_op jit(solution)/shard_map/attend_self/pallas_call | solution.py:307
  150.6 12.0 %collective-permute-done.5 = bf16[160,1536]{1,0:T(8,128)(2,1)S(1)} collective-permute-done((bf16[160,1536]{1,0:T(8,128)(2,1)S(1)}, bf16[160,1536]{1,0:T(8,128)(2,1)S(1)}, u32[]{:S(2)}, u32[]{:S(2)}) %collective-permute-start.5) | collective-permute-done | bytes 491552 | tf_op jit(solution)/shard_map/ppermute | solution.py:74
  172.2 9.9 %collective-permute-done.6 = bf16[160,1536]{1,0:T(8,128)(2,1)S(1)} collective-permute-done((bf16[160,1536]{1,0:T(8,128)(2,1)S(1)}, bf16[160,1536]{1,0:T(8,128)(2,1)S(1)}, u32[]{:S(2)}, u32[]{:S(2)}) %collective-permute-start.6) | collective-permute-done | bytes 491552 | tf_op jit(solution)/shard_map/ppermute | solution.py:74
  191.1 15.6 %collective-permute-done.11 = bf16[320,1536]{1,0:T(8,128)(2,1)S(1)} collective-permute-done((bf16[320,1536]{1,0:T(8,128)(2,1)S(1)}, bf16[320,1536]{1,0:T(8,128)(2,1)S(1)}, u32[]{:S(2)}, u32[]{:S(2)}) %collective-permute-start.11) | collective-permute-done | bytes 983072 | tf_op jit(solution)/shard_map/ppermute | solution.py:74
  220.9 7.7 %attend_cross.1 = (bf16[1280,384]{1,0:T(8,128)(2,1)}, f32[3,8,1280]{2,1,0:T(8,128)}) custom-call(bf16[1280,384]{1,0:T(8,128)(2,1)} %convolution_convert_fusion.3.refs_0_, bf16[272,768]{1,0:T(8,128)(2,1)} %pad.21.refs_1_.refs_2_, bf16[272,768]{1,0:T(8,128)(2,1)} %pad.21.refs_1_.refs_2_, s32[1,1280]{1,0:T(1,128)} %broadcast_in_dim.36.refs_5_.refs_3_.refs_6_.refs_8_, ...), custom_call_target="tpu_custom_call" | custom-call | flops 1069547520 | bytes 7151616 | tf_op jit(solution)/shard_map/attend_cross/pallas_call | solution.py:307
  251.8 10.4 %collective-permute-done.16 = bf16[160,1536]{1,0:T(8,128)(2,1)S(1)} collective-permute-done((bf16[160,1536]{1,0:T(8,128)(2,1)S(1)}, bf16[160,1536]{1,0:T(8,128)(2,1)S(1)}, u32[]{:S(2)}, u32[]{:S(2)}) %collective-permute-start.16) | collective-permute-done | bytes 491552 | tf_op jit(solution)/shard_map/ppermute | solution.py:74
  276.1 11.9 %collective-permute-done.21 = bf16[320,1536]{1,0:T(8,128)(2,1)S(1)} collective-permute-done((bf16[320,1536]{1,0:T(8,128)(2,1)S(1)}, bf16[320,1536]{1,0:T(8,128)(2,1)S(1)}, u32[]{:S(2)}, u32[]{:S(2)}) %collective-permute-start.21) | collective-permute-done | bytes 983072 | tf_op jit(solution)/shard_map/ppermute | solution.py:74
  298.7 41.2 %feed.1 = (bf16[1280,1536]{1,0:T(8,128)(2,1)}, bf16[1280,1536]{1,0:T(8,128)(2,1)}, bf16[1280,1536]{1,0:T(8,128)(2,1)}, f32[1,1536]{1,0:T(1,128)}, f32[1,1536]{1,0:T(1,128)}, /*index=5*/bf16[1280,1536]{1,0:T(8,128)(2,1)}) custom-call(bf16[1280,1536]{1,0:T(8,128)(2,1)} %constant_dynamic-update-slice_fusion.10.refs_0_.h_ref, ...), custom_call_target="tpu_custom_call" | custom-call | flops 30198988800 | bytes 37748736 | tf_op jit(solution)/shard_map/feed/pallas_call | solution.py:435
  339.9 10.0 %convolution_convert_fusion = bf16[1536,1536]{1,0:T(8,128)(2,1)} fusion(bf16[1280,1536]{1,0:T(8,128)(2,1)} %get-tuple-element.84, bf16[1280,1536]{1,0:T(8,128)(2,1)S(1)} %copy-done.43), kind=kOutput, calls=%fused_computation.7 | convolution fusion | flops 6042157056 | bytes 12582912 | tf_op jit(solution)/shard_map/dot_general | solution.py:66
  364.8 18.7 %gateup_grads.1 = bf16[8,4,48,3072]{3,2,1,0:T(8,128)(2,1)} custom-call(bf16[1280,1536]{1,0:T(8,128)(2,1)} %constant_dynamic-update-slice_fusion.10.refs_0_.h_ref, bf16[1280,1536]{1,0:T(8,128)(2,1)} %get-tuple-element.65.dg_ref, bf16[1280,1536]{1,0:T(8,128)(2,1)} %get-tuple-element.66.du_ref), custom_call_target="tpu_custom_call" | custom-call | flops 12079595520 | bytes 21233664 | tf_op jit(solution)/shard_map/gateup_grads/pallas_call | solution.py:505
  424.8 9.2 %collective-permute-done.35 = bf16[320,1536]{1,0:T(8,128)(2,1)} collective-permute-done((bf16[320,1536]{1,0:T(8,128)(2,1)}, bf16[320,1536]{1,0:T(8,128)(2,1)}, u32[]{:S(2)}, u32[]{:S(2)}) %collective-permute-start.35) | collective-permute-done | bytes 983072 | tf_op jit(solution)/shard_map/ppermute | solution.py:74
  457.9 9.7 %back_cross.1 = (bf16[1280,384]{1,0:T(8,128)(2,1)}, bf16[272,384]{1,0:T(8,128)(2,1)}, bf16[272,384]{1,0:T(8,128)(2,1)}) custom-call(bf16[1280,384]{1,0:T(8,128)(2,1)} %convolution_convert_fusion.3.refs_0_, bf16[272,768]{1,0:T(8,128)(2,1)} %pad.21.refs_1_.refs_2_, bf16[272,768]{1,0:T(8,128)(2,1)} %pad.21.refs_1_.refs_2_, ...), custom_call_target="tpu_custom_call" | custom-call | flops 2673868800 | bytes 7151616 | tf_op jit(solution)/shard_map/back_cross/pallas_call | solution.py:342
  478.1 10.7 %mid_grads.1 = bf16[8,4,48,1664]{3,2,1,0:T(8,128)(2,1)} custom-call(bf16[272,1536]{1,0:T(8,128)(2,1)} %pad.22.cond_ref, bf16[272,384]{1,0:T(8,128)(2,1)} %get-tuple-element.70.dk_ref, bf16[272,384]{1,0:T(8,128)(2,1)} %get-tuple-element.71.dv_ref, bf16[1280,1536]{1,0:T(8,128)(2,1)} %copy-done.17, bf16[1280,384]{1,0:T(8,128)(2,1)} %get-tuple-element.69.dq_ref, ...), custom_call_target="tpu_custom_call" | custom-call | flops 3661627392 | bytes 13811712 | tf_op jit(solution)/shard_map/mid_grads/pallas_call | solution.py:554
  494.6 13.6 %collective-permute-done.40 = bf16[160,1536]{1,0:T(8,128)(2,1)S(1)} collective-permute-done((bf16[160,1536]{1,0:T(8,128)(2,1)S(1)}, bf16[160,1536]{1,0:T(8,128)(2,1)S(1)}, u32[]{:S(2)}, u32[]{:S(2)}) %collective-permute-start.40) | collective-permute-done | bytes 491552 | tf_op jit(solution)/shard_map/ppermute | solution.py:74
  527.4 15.1 %collective-permute-done.45 = bf16[320,1536]{1,0:T(8,128)(2,1)S(1)} collective-permute-done((bf16[320,1536]{1,0:T(8,128)(2,1)}, bf16[320,1536]{1,0:T(8,128)(2,1)S(1)}, u32[]{:S(2)}, u32[]{:S(2)}) %collective-permute-start.45) | collective-permute-done | bytes 983072 | tf_op jit(solution)/shard_map/ppermute | solution.py:74
  571.7 29.4 %back_self.1 = (bf16[1280,384]{1,0:T(8,128)(2,1)}, bf16[1280,384]{1,0:T(8,128)(2,1)}, bf16[1280,384]{1,0:T(8,128)(2,1)}) custom-call(bf16[1280,384]{1,0:T(8,128)(2,1)} %get-tuple-element.55.refs_0_, bf16[1280,384]{1,0:T(8,128)(2,1)} %get-tuple-element.56.refs_1_, bf16[1280,384]{1,0:T(8,128)(2,1)} %get-tuple-element.57.refs_2_, ...), custom_call_target="tpu_custom_call" | custom-call | flops 12582912000 | bytes 11796480 | tf_op jit(solution)/shard_map/back_self/pallas_call | solution.py:342
  604.7 13.2 %self_grads.1 = bf16[8,4,48,1664]{3,2,1,0:T(8,128)(2,1)} custom-call(bf16[1280,1536]{1,0:T(8,128)(2,1)} %copy-done.22, bf16[1280,384]{1,0:T(8,128)(2,1)} %get-tuple-element.76.dq_ref, bf16[1280,384]{1,0:T(8,128)(2,1)} %get-tuple-element.77.dk_ref, bf16[1280,384]{1,0:T(8,128)(2,1)} %get-tuple-element.78.dv_ref, bf16[1536,1152]{1,0:T(8,128)(2,1)} %slice.428.w_ref, ...), custom_call_target="tpu_custom_call" | custom-call | flops 6039797760 | bytes 16515072 | tf_op jit(solution)/shard_map/self_grads/pallas_call | solution.py:617
  621.0 7.9 %collective-permute-done.50 = bf16[160,1536]{1,0:T(8,128)(2,1)S(1)} collective-permute-done((bf16[160,1536]{1,0:T(8,128)(2,1)S(1)}, bf16[160,1536]{1,0:T(8,128)(2,1)S(1)}, u32[]{:S(2)}, u32[]{:S(2)}) %collective-permute-start.50) | collective-permute-done | bytes 491552 | tf_op jit(solution)/shard_map/ppermute | solution.py:74
  679.3 11.8 %collective-permute-done.56 = bf16[160,1536]{1,0:T(8,128)(2,1)S(1)} collective-permute-done((bf16[160,1536]{1,0:T(8,128)(2,1)S(1)}, bf16[160,1536]{1,0:T(8,128)(2,1)S(1)}, u32[]{:S(2)}, u32[]{:S(2)}) %collective-permute-start.56) | collective-permute-done | bytes 491552 | tf_op jit(solution)/shard_map/ppermute | solution.py:74
  697.5 8.3 %collective-permute-done.60 = bf16[260,768]{1,0:T(8,128)(2,1)S(1)} collective-permute-done((bf16[260,768]{1,0:T(8,128)(2,1)S(1)}, bf16[260,768]{1,0:T(8,128)(2,1)S(1)}, u32[]{:S(2)}, u32[]{:S(2)}) %collective-permute-start.60) | collective-permute-done | bytes 399392 | tf_op jit(solution)/shard_map/ppermute | solution.py:74
  (524 shorter events, 395.3 us)
Async XLA Ops:
  7.2 89.4 %all-gather.5.cloned.1.call-start = ((), (), s32[]{:S(2)}) async-start(), calls=%async_computation.10 | async-start | bytes 4423680 | tf_op jit(solution)/shard_map/all_gather | solution.py:660
  26.7 115.5 %all-gather.7.cloned.1.call-start = ((), (), s32[]{:S(2)}) async-start(), calls=%async_computation.11 | async-start | bytes 6635520 | tf_op jit(solution)/shard_map/all_gather | solution.py:776
  33.8 264.9 %all-gather.11.cloned.1.call-start = ((), (), s32[]{:S(2)}) async-start(), calls=%async_computation.13 | async-start | bytes 5308416 | tf_op jit(solution)/shard_map/all_gather | solution.py:785
  53.2 245.5 %all-gather.9.cloned.1.call-start = ((), (), s32[]{:S(2)}) async-start(), calls=%async_computation.12 | async-start | bytes 10616832 | tf_op jit(solution)/shard_map/all_gather | solution.py:781
  83.9 318.1 %reduce-scatter.5.cloned.1.call-start = ((), (), s32[]{:S(2)}) async-start(), calls=%async_computation.14 | async-start | bytes 5308416 | tf_op jit(solution)/shard_map/reduce_scatter | solution.py:828
  110.7 29.5 %collective-permute-start.24 = (bf16[320,1536]{1,0:T(8,128)(2,1)S(1)}, bf16[320,1536]{1,0:T(8,128)(2,1)S(1)}, u32[]{:S(2)}, u32[]{:S(2)}) collective-permute-start(bf16[320,1536]{1,0:T(8,128)(2,1)S(1)} %bitcast.161), channel_id=1, source_target_pairs={{0,8},{8,0},{16,24},{24,16},{1,9},{9,1},{17,25},{25,17},{2,10},{10... | collective-permute-start | bytes 2949128 | tf_op jit(solution)/shard_map/ppermute | solution.py:74
  112.0 25.0 %collective-permute-start.25 = (bf16[320,1536]{1,0:T(8,128)(2,1)S(1)}, bf16[320,1536]{1,0:T(8,128)(2,1)}, u32[]{:S(2)}, u32[]{:S(2)}) collective-permute-start(bf16[320,1536]{1,0:T(8,128)(2,1)S(1)} %bitcast.162), channel_id=1, source_target_pairs={{0,16},{8,24},{16,0},{24,8},{1,17},{9,25},{17,1},{25,9},{2,18},{10... | collective-permute-start | bytes 2949128 | tf_op jit(solution)/shard_map/ppermute | solution.py:74
  138.9 133.5 %collective-permute-start.26 = (bf16[160,1536]{1,0:T(8,128)(2,1)}, bf16[160,1536]{1,0:T(8,128)(2,1)}, u32[]{:S(2)}, u32[]{:S(2)}) collective-permute-start(bf16[160,1536]{1,0:T(8,128)(2,1)} %slice.452), channel_id=1, source_target_pairs={{0,8},{8,0},{16,24},{24,16},{1,9},{9,1},{17,25},{25,17},{2,10},{10... | collective-permute-start | bytes 1474568 | tf_op jit(solution)/shard_map/ppermute | solution.py:74
  141.1 133.2 %collective-permute-start.27 = (bf16[160,1536]{1,0:T(8,128)(2,1)}, bf16[160,1536]{1,0:T(8,128)(2,1)}, u32[]{:S(2)}, u32[]{:S(2)}) collective-permute-start(bf16[160,1536]{1,0:T(8,128)(2,1)} %slice.453), channel_id=1, source_target_pairs={{0,16},{8,24},{16,0},{24,8},{1,17},{9,25},{17,1},{25,9},{2,18},{10... | collective-permute-start | bytes 1474568 | tf_op jit(solution)/shard_map/ppermute | solution.py:74
  148.4 23.0 %collective-permute-start.4 = (bf16[160,1536]{1,0:T(8,128)(2,1)S(1)}, bf16[160,1536]{1,0:T(8,128)(2,1)S(1)}, u32[]{:S(2)}, u32[]{:S(2)}) collective-permute-start(bf16[160,1536]{1,0:T(8,128)(2,1)S(1)} %slice.649), channel_id=1, source_target_pairs={{0,8},{8,0},{16,24},{24,16},{1,9},{9,1},{17,25},{25,17},{2,10},{10... | collective-permute-start | bytes 1474568 | tf_op jit(solution)/shard_map/ppermute | solution.py:74
  349.9 166.0 %reduce-scatter.7.cloned.1.call-start = ((), (), s32[]{:S(2)}) async-start(), calls=%async_computation.15 | async-start | bytes 10616832 | tf_op jit(solution)/shard_map/reduce_scatter | solution.py:831
  354.7 30.0 %collective-permute-start.28 = (bf16[160,1536]{1,0:T(8,128)(2,1)}, bf16[160,1536]{1,0:T(8,128)(2,1)}, u32[]{:S(2)}, u32[]{:S(2)}) collective-permute-start(bf16[160,1536]{1,0:T(8,128)(2,1)} %get-tuple-element.226), channel_id=1, source_target_pairs={{0,8},{8,0},{16,24},{24,16},{1,9},{9,1},{17,25},{25,17},{2,10},{10... | collective-permute-start | bytes 1474568 | tf_op jit(solution)/shard_map/ppermute | solution.py:74
  355.9 30.0 %collective-permute-start.33 = (bf16[160,1536]{1,0:T(8,128)(2,1)S(1)}, bf16[160,1536]{1,0:T(8,128)(2,1)}, u32[]{:S(2)}, u32[]{:S(2)}) collective-permute-start(bf16[160,1536]{1,0:T(8,128)(2,1)S(1)} %get-tuple-element.227), channel_id=1, source_target_pairs={{0,16},{8,24},{16,0},{24,8},{1,17},{9,25},{17,1},{25,9},{2,18},{10... | collective-permute-start | bytes 1474568 | tf_op jit(solution)/shard_map/ppermute | solution.py:74
  402.0 243.0 %reduce-scatter.9.cloned.1.call-start = ((), (), s32[]{:S(2)}) async-start(), calls=%async_computation.16 | async-start | bytes 5750784 | tf_op jit(solution)/shard_map/reduce_scatter | solution.py:853
  409.6 24.3 %collective-permute-start.35 = (bf16[320,1536]{1,0:T(8,128)(2,1)}, bf16[320,1536]{1,0:T(8,128)(2,1)}, u32[]{:S(2)}, u32[]{:S(2)}) collective-permute-start(bf16[320,1536]{1,0:T(8,128)(2,1)} %get-tuple-element.218), channel_id=1, source_target_pairs={{0,16},{8,24},{16,0},{24,8},{1,17},{9,25},{17,1},{25,9},{2,18},{10... | collective-permute-start | bytes 2949128 | tf_op jit(solution)/shard_map/ppermute | solution.py:74
  411.6 25.9 %collective-permute-start.34 = (bf16[320,1536]{1,0:T(8,128)(2,1)}, bf16[320,1536]{1,0:T(8,128)(2,1)}, u32[]{:S(2)}, u32[]{:S(2)}) collective-permute-start(bf16[320,1536]{1,0:T(8,128)(2,1)} %get-tuple-element.218), channel_id=1, source_target_pairs={{0,8},{8,0},{16,24},{24,16},{1,9},{9,1},{17,25},{25,17},{2,10},{10... | collective-permute-start | bytes 2949128 | tf_op jit(solution)/shard_map/ppermute | solution.py:74
  477.6 31.9 %collective-permute-start.43 = (bf16[160,1536]{1,0:T(8,128)(2,1)}, bf16[160,1536]{1,0:T(8,128)(2,1)}, u32[]{:S(2)}, u32[]{:S(2)}) collective-permute-start(bf16[160,1536]{1,0:T(8,128)(2,1)} %slice.644), channel_id=1, source_target_pairs={{0,16},{8,24},{16,0},{24,8},{1,17},{9,25},{17,1},{25,9},{2,18},{10... | collective-permute-start | bytes 1474568 | tf_op jit(solution)/shard_map/ppermute | solution.py:74
  522.4 22.9 %collective-permute-start.44 = (bf16[320,1536]{1,0:T(8,128)(2,1)}, bf16[320,1536]{1,0:T(8,128)(2,1)S(1)}, u32[]{:S(2)}, u32[]{:S(2)}) collective-permute-start(bf16[320,1536]{1,0:T(8,128)(2,1)} %get-tuple-element.215), channel_id=1, source_target_pairs={{0,8},{8,0},{16,24},{24,16},{1,9},{9,1},{17,25},{25,17},{2,10},{10... | collective-permute-start | bytes 2949128 | tf_op jit(solution)/shard_map/ppermute | solution.py:74
  560.1 57.9 %collective-permute-start.49 = (bf16[160,1536]{1,0:T(8,128)(2,1)S(1)}, bf16[160,1536]{1,0:T(8,128)(2,1)}, u32[]{:S(2)}, u32[]{:S(2)}) collective-permute-start(bf16[160,1536]{1,0:T(8,128)(2,1)S(1)} %get-tuple-element.234), channel_id=1, source_target_pairs={{0,8},{8,0},{16,24},{24,16},{1,9},{9,1},{17,25},{25,17},{2,10},{10... | collective-permute-start | bytes 1474568 | tf_op jit(solution)/shard_map/ppermute | solution.py:74
  562.5 58.5 %collective-permute-start.48 = (bf16[160,1536]{1,0:T(8,128)(2,1)S(1)}, bf16[160,1536]{1,0:T(8,128)(2,1)S(1)}, u32[]{:S(2)}, u32[]{:S(2)}) collective-permute-start(bf16[160,1536]{1,0:T(8,128)(2,1)S(1)} %slice.643), channel_id=1, source_target_pairs={{0,8},{8,0},{16,24},{24,16},{1,9},{9,1},{17,25},{25,17},{2,10},{10... | collective-permute-start | bytes 1474568 | tf_op jit(solution)/shard_map/ppermute | solution.py:74
  564.0 55.6 %collective-permute-start.51 = (bf16[160,1536]{1,0:T(8,128)(2,1)S(1)}, bf16[160,1536]{1,0:T(8,128)(2,1)S(1)}, u32[]{:S(2)}, u32[]{:S(2)}) collective-permute-start(bf16[160,1536]{1,0:T(8,128)(2,1)S(1)} %get-tuple-element.235), channel_id=1, source_target_pairs={{0,16},{8,24},{16,0},{24,8},{1,17},{9,25},{17,1},{25,9},{2,18},{10... | collective-permute-start | bytes 1474568 | tf_op jit(solution)/shard_map/ppermute | solution.py:74
  567.0 66.9 %collective-permute-start.53 = (bf16[160,1536]{1,0:T(8,128)(2,1)}, bf16[160,1536]{1,0:T(8,128)(2,1)}, u32[]{:S(2)}, u32[]{:S(2)}) collective-permute-start(bf16[160,1536]{1,0:T(8,128)(2,1)} %slice.642), channel_id=1, source_target_pairs={{0,16},{8,24},{16,0},{24,8},{1,17},{9,25},{17,1},{25,9},{2,18},{10... | collective-permute-start | bytes 1474568 | tf_op jit(solution)/shard_map/ppermute | solution.py:74
  633.7 95.1 %reduce-scatter.11.cloned.1.call-start = ((), (), s32[]{:S(2)}) async-start(), calls=%async_computation.17 | async-start | bytes 5750784 | tf_op jit(solution)/shard_map/reduce_scatter | solution.py:874
  663.7 28.5 %collective-permute-start.59 = (bf16[160,1536]{1,0:T(8,128)(2,1)}, bf16[160,1536]{1,0:T(8,128)(2,1)}, u32[]{:S(2)}, u32[]{:S(2)}) collective-permute-start(bf16[160,1536]{1,0:T(8,128)(2,1)} %slice.640), channel_id=1, source_target_pairs={{0,16},{8,24},{16,0},{24,8},{1,17},{9,25},{17,1},{25,9},{2,18},{10... | collective-permute-start | bytes 1474568 | tf_op jit(solution)/shard_map/ppermute | solution.py:74
  (120 other events, 1286.4 us)
Sparse Core Ops, SparseCore 0:
  21.7 43.0 all-gather.4
  67.0 59.5 all-gather.6
  128.2 50.9 all-gather.10
  180.7 88.2 all-gather.8
  350.1 51.9 reduce-scatter.4
  404.2 98.2 reduce-scatter.6
  516.1 54.4 reduce-scatter.8
  645.1 53.9 reduce-scatter.10

commit v4 on v3

--- a/solution.py
+++ b/solution.py
@@ -70,6 +70,12 @@
     return lax.dot_general(left, weight, (((1,), (1,)), ((), ())), preferred_element_type=f32)
 
 
+def after(value, *others):
+    if not others:
+        return value
+    return lax.optimization_barrier((value,) + others)[0]
+
+
 def hop(value, j):
     return lax.ppermute(value, "seq", [(i, i ^ j) for i in range(4)])
 
@@ -82,32 +88,52 @@
 
 def gather_rows(value, n):
     if n != 4:
-        return lax.all_gather(value, "seq", axis=0, tiled=True)
+        whole = lax.all_gather(value, "seq", axis=0, tiled=True)
+        return whole, (whole,), (whole,)
     half = value.shape[0] // 2
     first, second = hop(value, 1), hop(value, 2)
     third, fourth = hop(second[:half], 1), hop(first[half:], 2)
-    return jnp.concatenate([value, first, second, third, fourth], axis=0)
-
-
-def scatter_rows(blocks, n):
+    whole = jnp.concatenate([value, first, second, third, fourth], axis=0)
+    return whole, (first, second), (third, fourth)
+
+
+def scatter_rows(blocks, rows, n):
     if n != 4:
-        whole = jnp.concatenate([blocks(j) for j in range(n)], axis=0)
-        return lax.psum_scatter(whole.astype(bf16), "seq", scatter_dimension=0, tiled=True).astype(f32)
-    last = blocks(3).astype(bf16)
-    half = last.shape[0] // 2
-    to_first, to_second = hop(last[:half], 1), hop(last[half:], 2)
-    one, two = blocks(1), blocks(2)
-    plain_one, plain_two = hop(one[:half].astype(bf16), 1), hop(two[half:].astype(bf16), 2)
-    sum_one = hop((one[half:] + to_second.astype(f32)).astype(bf16), 1)
-    sum_two = hop((two[:half] + to_first.astype(f32)).astype(bf16), 2)
-    own = blocks(0)
-    return own + jnp.concatenate(
-        [
-            plain_one.astype(f32) + sum_two.astype(f32),
-            sum_one.astype(f32) + plain_two.astype(f32),
-        ],
-        axis=0,
-    )
+        whole = jnp.concatenate([blocks(j, 0, rows) for j in range(n)], axis=0).astype(bf16)
+        out = lax.psum_scatter(whole, "seq", scatter_dimension=0, tiled=True).astype(f32)
+        return out, (out,)
+    half = rows // 2
+    to_first = hop(blocks(3, 0, half).astype(bf16), 1)
+    to_second = hop(blocks(3, half, rows).astype(bf16), 2)
+    one, two = blocks(1, 0, rows).astype(f32), blocks(2, 0, rows).astype(f32)
+    one = jnp.concatenate([one[:half], one[half:] + to_second.astype(f32)], axis=0)
+    two = jnp.concatenate([two[:half] + to_first.astype(f32), two[half:]], axis=0)
+    one, two = hop(one.astype(bf16), 1), hop(two.astype(bf16), 2)
+    own = blocks(0, 0, rows).astype(f32)
+    return own + one.astype(f32) + two.astype(f32), (to_first, to_second)
+
+
+def scatter_start(partial, n):
+    if n != 4:
+        return (lax.psum_scatter(partial, "seq", scatter_dimension=0, tiled=True),)
+    half = partial.shape[0] // 8
+    return (
+        hop(partial[6 * half : 7 * half], 1),
+        hop(partial[7 * half :], 2),
+        hop(partial[2 * half : 3 * half], 1),
+        hop(partial[5 * half : 6 * half], 2),
+    )
+
+
+def scatter_end(partial, pieces, n):
+    if n != 4:
+        return pieces[0].astype(f32)
+    half = partial.shape[0] // 8
+    to_first, to_second, one, two = (piece.astype(f32) for piece in pieces)
+    sum_one = hop((partial[3 * half : 4 * half].astype(f32) + to_second).astype(bf16), 1)
+    sum_two = hop((partial[4 * half : 5 * half].astype(f32) + to_first).astype(bf16), 2)
+    others = jnp.concatenate([one + sum_two.astype(f32), sum_one.astype(f32) + two], axis=0)
+    return partial[: 2 * half].astype(f32) + others
 
 
 def swap_halves(value):
@@ -371,7 +397,7 @@
 
 def feed_kernel(chunk, *refs):
     h_ref, gy_ref, wg_ref, wu_ref, wd_ref, bg_ref, bu_ref = refs[:7]
-    act_ref, dg_ref, du_ref, sg_ref, su_ref, dh_ref, both, total = refs[7:]
+    act_ref, dg_ref, du_ref, sg_ref, su_ref, dh_ref, dw_ref, both, total = refs[7:]
     step = pl.program_id(0)
     span = wg_ref.shape[0] * wg_ref.shape[2]
     tile = wg_ref.shape[3]
@@ -415,6 +441,7 @@
         grads = finish(i, *now)
         total[rows_at(i), :] += contract(grads, both[...], ((1,), (1,)))
         now = later
+    dw_ref[...] = dot(act_ref[...].T, gy_ref[...]).astype(bf16)
 
     @pl.when(step == pl.num_programs(0) - 1)
     def _():
@@ -436,7 +463,7 @@
         functools.partial(feed_kernel, chunk),
         out_shape=[jax.ShapeDtypeStruct((rows, hidden), bf16)] * 3
         + [jax.ShapeDtypeStruct((1, hidden), f32)] * 2
-        + [jax.ShapeDtypeStruct((rows, D), bf16)],
+        + [jax.ShapeDtypeStruct((rows, D), bf16), jax.ShapeDtypeStruct((hidden, D), bf16)],
         grid=(steps,),
         in_specs=[
             rows_all,
@@ -447,15 +474,15 @@
             vector,
             vector,
         ],
-        out_specs=[columns, columns, columns, vector, vector, rows_all],
+        out_specs=[columns, columns, columns, vector, vector, rows_all, pl.BlockSpec((tile, D), lambda t: (t, 0))],
         scratch_shapes=[
             pltpu.VMEM((D, 2 * tile), bf16),
             pltpu.VMEM((rows, D), f32),
         ],
         compiler_params=pltpu.CompilerParams(vmem_limit_bytes=LIMIT),
         cost_estimate=pl.CostEstimate(
-            flops=2 * 5 * rows * D * hidden,
-            bytes_accessed=2 * (3 * rows * D + 3 * rows * hidden + 3 * D * hidden),
+            flops=2 * 6 * rows * D * hidden,
+            bytes_accessed=2 * (3 * rows * D + 3 * rows * hidden + 4 * D * hidden),
             transcendentals=rows * hidden,
         ),
         name="feed",
@@ -525,8 +552,9 @@
 def mid_kernel(cond_ref, dk_ref, dv_ref, h_ref, dq_ref, mix_ref, gy_ref, vec_ref, out_ref):
     wide = dq_ref.shape[1]
     outer = ((0,), (0,))
-    place_rows(out_ref, 0, contract(cond_ref[...], dk_ref[...], outer))
-    place_rows(out_ref, wide, contract(cond_ref[...], dv_ref[...], outer))
+    turned = cond_ref[...].T
+    place_rows(out_ref, 0, dot(turned, dk_ref[...]))
+    place_rows(out_ref, wide, dot(turned, dv_ref[...]))
     place_rows(out_ref, 2 * wide, contract(h_ref[...], dq_ref[...], outer))
     out_ref[:, 0, :, 3 * wide : 3 * wide + LANES] = vec_ref[:, 0]
     place_rows(out_ref, 3 * wide + LANES, contract(mix_ref[...], gy_ref[...], outer))
@@ -577,38 +605,33 @@
     return out.reshape(D, columns)
 
 
-def self_kernel(h_ref, dq_ref, dk_ref, dv_ref, w_ref, gain_ref, mix_ref, gy_ref, vec_ref, out_ref):
+def self_kernel(h_ref, dq_ref, dk_ref, dv_ref, w_ref, gain_ref, vec_ref, mix_ref, gy_ref, out_ref):
     wide = dq_ref.shape[1]
     nf, _, r, _ = out_ref.shape
-    outer = ((0,), (0,))
+    turned = h_ref[...].T
     along = jnp.zeros((wide, 1), f32)
     for j, ref in enumerate((dq_ref, dk_ref, dv_ref)):
-        grad = contract(h_ref[...], ref[...], outer)
+        grad = dot(turned, ref[...])
         place_rows(out_ref, j * wide, grad)
         weight = w_ref[:, j * wide : (j + 1) * wide].astype(f32)
         along = along + jnp.sum(grad * weight, axis=1, keepdims=True)
-    along = jnp.broadcast_to(along / gain_ref[...], (wide, LANES)).reshape(nf, r, LANES)
+    along = jnp.broadcast_to(along / gain_ref[:, 0:1].astype(f32), (wide, LANES)).reshape(nf, r, LANES)
     lane = lax.broadcasted_iota(jnp.int32, along.shape, 2)
     vec = jnp.where(lane == 0, along, vec_ref[:, 0].astype(f32))
     out_ref[:, 0, :, 3 * wide : 3 * wide + LANES] = vec.astype(bf16)
-    place_rows(out_ref, 3 * wide + LANES, contract(mix_ref[...], gy_ref[...], outer))
-
-
-def self_grads(h, dq, dk, dv, w_self, gain, mix, gy, vectors, n, nf):
+    place_rows(out_ref, 3 * wide + LANES, contract(mix_ref[...], gy_ref[...], ((0,), (0,))))
+
+
+def self_grads(h, dq, dk, dv, w_all, vectors, mix, gy, n, nf):
     rows, wide = dq.shape
     r = D // (n * nf)
     if r % 16 or wide % LANES:
         grad = outer_sum(h, jnp.concatenate([dq, dk, dv], axis=1))
-        along = (jnp.sum(grad * w_self.astype(f32), axis=1) / gain).astype(bf16)
+        along = jnp.sum(grad * w_all[:, : 3 * wide].astype(f32), axis=1)
+        along = (along / w_all[:, 3 * wide].astype(f32)).astype(bf16)
         along = along.reshape(n, nf, r, 1).transpose(1, 0, 2, 3).reshape(D, 1)
-        return jnp.concatenate(
-            [
-                columns_by_owner(grad, n, nf),
-                jnp.concatenate([along, vectors[:, 1:]], axis=1),
-                rows_by_owner(outer_sum(mix, gy).astype(bf16), n, nf),
-            ],
-            axis=1,
-        )
+        grad_out = rows_by_owner(outer_sum(mix, gy).astype(bf16), n, nf)
+        return jnp.concatenate([columns_by_owner(grad, n, nf), along, vectors[:, 1:], grad_out], axis=1)
     columns = 4 * wide + LANES
 
     def full(value):
@@ -624,18 +647,18 @@
             full(dk),
             full(dv),
             pl.BlockSpec((wide, 3 * wide), lambda s: (s, 0)),
-            pl.BlockSpec((wide, 1), lambda s: (s, 0)),
+            pl.BlockSpec((wide, LANES), lambda s: (s, 3 * wide // LANES)),
+            pl.BlockSpec((nf, 1, r, LANES), lambda s: (0, s, 0, 0)),
             full(mix),
             pl.BlockSpec((rows, wide), lambda s: (0, s)),
-            pl.BlockSpec((nf, 1, r, LANES), lambda s: (0, s, 0, 0)),
         ],
         out_specs=pl.BlockSpec((nf, 1, r, columns), lambda s: (0, s, 0, 0)),
         compiler_params=pltpu.CompilerParams(vmem_limit_bytes=LIMIT),
         cost_estimate=pl.CostEstimate(
-            flops=8 * D * wide * rows, bytes_accessed=2 * D * (columns + 2 * rows + 3 * wide), transcendentals=0
+            flops=8 * D * wide * rows, bytes_accessed=2 * D * (columns + rows + 3 * wide), transcendentals=0
         ),
         name="self_grads",
-    )(h, dq, dk, dv, w_self, gain[:, None], mix, gy, vectors.reshape(nf, n, r, LANES))
+    )(h, dq, dk, dv, w_all, w_all, vectors.reshape(nf, n, r, LANES), mix, gy)
     return out.reshape(D, columns)
 
 
@@ -651,6 +674,27 @@
     return pieces.reshape(n, r, parts, c).transpose(1, 2, 0, 3).reshape(r, parts * n * c)
 
 
+def spread_kernel(in_ref, out_ref):
+    c = in_ref.shape[2]
+    for s in range(in_ref.shape[0]):
+        out_ref[:, s * c : (s + 1) * c] = in_ref[s].astype(f32)
+
+
+def spread(pieces, width, parts, n, first=0):
+    r = pieces.shape[1]
+    c = width // n
+    if r % 16 or c % LANES:
+        return natural_columns(pieces[:, :, first * c : (first + parts) * c], parts, n).astype(f32)
+    return pl.pallas_call(
+        spread_kernel,
+        out_shape=jax.ShapeDtypeStruct((r, parts * n * c), f32),
+        grid=(parts,),
+        in_specs=[pl.BlockSpec((n, r, c), lambda p: (0, 0, first + p))],
+        out_specs=pl.BlockSpec((r, n * c), lambda p: (0, p)),
+        name="spread",
+    )(pieces)
+
+
 def to_seq(pieces):
     return lax.all_to_all(pieces, "seq", 0, 0, tiled=True)
 
@@ -683,22 +727,22 @@
     return shard.reshape(r, n, columns // n).transpose(1, 0, 2).reshape(n * r, columns // n)
 
 
-def after(value, *others):
-    return lax.optimization_barrier((value,) + others)[0]
-
-
-def sum_over_seq(value, n):
+def pair_sum(part, j):
+    low = part.astype(bf16)
+    return low.astype(f32) + hop(low, j).astype(f32)
+
+
+def sum_start(value, n):
     if n != 4:
-        return lax.psum(value, "seq")
+        return (lax.psum(value, "seq"),)
     half = value.shape[1] // 2
-
-    def step(part, j):
-        low = part.astype(bf16)
-        return low.astype(f32) + hop(low, j).astype(f32)
-
-    return jnp.concatenate(
-        [step(step(value[:, :half], 1), 2), step(step(value[:, half:], 2), 1)], axis=1
-    )
+    return pair_sum(value[:, :half], 1), pair_sum(value[:, half:], 2)
+
+
+def sum_end(parts, n):
+    if n != 4:
+        return parts[0]
+    return jnp.concatenate([pair_sum(parts[0], 2), pair_sum(parts[1], 1)], axis=1)
 
 
 def pad_heads(value, parts):
@@ -755,8 +799,8 @@
             self_pieces,
         )
     )
-    group_tokens = gather_rows(after(tokens[0], self_pieces), n)
-    gateup_pieces = to_seq(after(column_parts(proj_gateup, 2, n), mid_pieces))
+    group_tokens, _, ends = gather_rows(after(tokens[0], self_pieces), n)
+    group_grad, grad_early, grad_ends = gather_rows(after(grad_output[0], *ends), n)
 
     self_all = gather_columns(self_pieces, n, nf)
     w_self = self_all[:, : 3 * wide]
@@ -778,32 +822,36 @@
     w_keyval, w_query = kvq[:, : 2 * wide], kvq[:, 2 * wide :]
     w_out = mid[..., 3 * wide : 4 * wide].transpose(0, 2, 1, 3).reshape(nf * r, D)
     w_cross = mid[..., 4 * wide :].transpose(0, 2, 1, 3).reshape(nf * r, D)
-    w_gateup = lax.all_gather(gateup_pieces.reshape(n * r, 2 * hidden), "fsdp", axis=0, tiled=True)
-    w_gateup = w_gateup.reshape(nf, n, r, 2 * hidden)
-    if r % 16:
-        w_gateup = w_gateup.transpose(1, 0, 2, 3).reshape(1, 1, D, 2 * hidden)
-    w_down = lax.all_gather(after(proj_down, gateup_pieces), "fsdp", axis=0, tiled=True)
-
     group_lengths = lengths[0]
     order = block_ids(n)
     all_rows = (order[:, None] * rows + jnp.arange(rows, dtype=jnp.int32)[None, :]).reshape(group)
     ids, positions = seq_info(all_rows, group_lengths)
     tables = angle_tables(positions)
 
-    def block(value, j):
-        return lax.slice_in_dim(value, j * rows, (j + 1) * rows, axis=0)
+    def block(value, j, low, high):
+        return lax.slice_in_dim(value, j * rows + low, j * rows + high, axis=0)
+
+    def scattered(rows_of):
+        return scatter_rows(rows_of, rows, n)
 
     inputs = tokens[0].astype(f32)
     normal_one, scaled_one, _ = norm_rows(inputs, gain_one)
+    group_tokens, *tables = lax.optimization_barrier((group_tokens, *tables))
     normed_one = norm_rows(group_tokens.astype(f32), gain_one)[2].astype(bf16)
-    packed = pad_heads(dot(normed_one, w_self), 3)
-    group_grad = gather_rows(after(grad_output[0], packed), n)
+    packed = after(pad_heads(dot(normed_one, w_self), 3), *grad_early)
+    gateup_pieces = to_seq(after(column_parts(proj_gateup, 2, n), packed))
+    w_down = lax.all_gather(after(proj_down, mid_pieces), "fsdp", axis=0, tiled=True)
     q, k, v, mixed, lse = attend(packed, packed, packed, (0, pairs, 2 * pairs), pairs, ids, ids, tables)
-    mixed_in = mixed[:, :wide]
-    first = inputs + scatter_rows(lambda j: dot(block(mixed_in, j), w_out), n)
+    gateup_pieces = after(gateup_pieces.reshape(n * r, 2 * hidden), mixed)
+    w_gateup = lax.all_gather(gateup_pieces, "fsdp", axis=0, tiled=True)
+    w_gateup = w_gateup.reshape(nf, n, r, 2 * hidden)
+    if r % 16:
+        w_gateup = w_gateup.transpose(1, 0, 2, 3).reshape(1, 1, D, 2 * hidden)
+    mixed_in = after(mixed[:, :wide], *grad_ends)
+    first = inputs + scattered(lambda *at: dot(block(mixed_in, *at), w_out))[0]
 
     normal_two, scaled_two, normed = norm_rows(first, gain_two)
-    normed_two = gather_rows(normed.astype(bf16), n)
+    normed_two, _, _ = gather_rows(normed.astype(bf16), n)
     cq = pad_heads(dot(normed_two, w_query).astype(bf16), 1)
     cond_rows = conditioning[0].reshape(SEQS_GRP * COND, D)
     count = SEQS_GRP * COND
@@ -814,32 +862,32 @@
     cond_ids = jnp.where(index < count, index // COND, -1)
     cmix, clse = attend(cq, keyval, keyval, (0, 0, pairs), pairs, ids, cond_ids)
     cmix_in = cmix[:, :wide]
-    second = first + scatter_rows(lambda j: dot(block(cmix_in, j), w_cross), n)
+    second = first + scattered(lambda *at: dot(block(cmix_in, *at), w_cross))[0]
 
     normal_three, scaled_three, normed = norm_rows(second, gain_three)
-    normed_three = gather_rows(normed.astype(bf16), n)
-    active, grad_gate, grad_upper, sum_gate, sum_upper, back_three = feed(
+    normed_three, _, _ = gather_rows(normed.astype(bf16), n)
+    active, grad_gate, grad_upper, sum_gate, sum_upper, back_three, grad_w_down = feed(
         normed_three, group_grad, w_gateup, w_down, b_gate, b_upper
     )
     grad_rows = grad_output[0].astype(f32)
     grad_b_down = jnp.sum(grad_rows, axis=0)
-    through = scatter_rows(lambda j: block(back_three, j).astype(f32), n)
-    grad_w_down = outer_sum(active, group_grad).astype(bf16)
+    through, early = scattered(lambda *at: block(back_three, *at))
     own_down = lax.psum_scatter(grad_w_down, "fsdp", scatter_dimension=0, tiled=True)
-    grad_w_gateup = gateup_grads(normed_three, grad_gate, grad_upper, n, nf)
+    grad_w_gateup = gateup_grads(after(normed_three, *early), grad_gate, grad_upper, n, nf)
     through, grad_w_gateup = lax.optimization_barrier((through, grad_w_gateup))
-    own_gateup = lax.psum_scatter(after(grad_w_gateup, own_down), "fsdp", scatter_dimension=0, tiled=True)
     through, grad_gain_three = norm_back(through, normal_three, scaled_three, gain_three)
     grad_second = grad_rows + through
 
-    group_second = gather_rows(grad_second.astype(bf16), n)
+    group_second, early, _ = gather_rows(grad_second.astype(bf16), n)
+    grad_w_gateup = after(grad_w_gateup, own_down, *early)
+    own_gateup = lax.psum_scatter(grad_w_gateup, "fsdp", scatter_dimension=0, tiled=True)
     grad_cmix = pad_heads(back_prod(group_second, w_cross).astype(bf16), 1)
     dcq, dck, dcv = attend_back(
         cq, keyval, keyval, (0, 0, pairs), pairs, grad_cmix, cmix, clse, ids, cond_ids
     )
     dcq, dck, dcv = dcq[:, :wide], dck[:, :wide], dcv[:, :wide]
     cond_full = jnp.pad(cond_rows, ((0, count_pad - count), (0, 0)))
-    through = scatter_rows(lambda j: back_prod(block(dcq, j), w_query), n)
+    through, _ = scattered(lambda *at: back_prod(block(dcq, *at), w_query))
     b_whole = lax.dynamic_update_slice(
         jnp.zeros((2, FF), f32), jnp.concatenate([sum_gate, sum_upper], axis=0), (0, me * hidden)
     )
@@ -850,39 +898,43 @@
     vectors = jnp.pad(vectors, ((0, 0), (0, LANES - vectors.shape[1])))
     grad_w_mid = mid_grads(cond_full, dck, dcv, normed_two, dcq, cmix_in, group_second, vectors, n, nf)
     through, grad_w_mid = lax.optimization_barrier((through, grad_w_mid))
-    own_mid = lax.psum_scatter(after(grad_w_mid, own_gateup), "fsdp", scatter_dimension=0, tiled=True)
     through, grad_gain_two = norm_back(through, normal_two, scaled_two, gain_two)
     grad_first = grad_second + through
 
-    group_first = gather_rows(grad_first.astype(bf16), n)
-    own_gateup = share(after(own_gateup, group_first), n)
-    late_active = after(active, group_first)
-    result = second + scatter_rows(lambda j: dot(block(late_active, j), w_down), n) + b_down
-    grad_mixed = pad_heads(back_prod(group_first, w_out).astype(bf16), 1)
-    dq, dk, dv = attend_back(q, k, v, (0, 0, 0), pairs, grad_mixed, mixed, lse, ids, ids, tables)
-    own_gateup = after(own_gateup, dq)
-    dq, dk, dv = dq[:, :wide], dk[:, :wide], dv[:, :wide]
-    grad_packed = jnp.concatenate([dq, dk, dv], axis=1)
     gains = grad_gain_two.astype(bf16).reshape(n, nf, r, 1).transpose(1, 0, 2, 3).reshape(D, 1)
     gains = jnp.pad(gains, ((0, 0), (1, LANES - 2)))
-    grad_w_self = self_grads(
-        normed_one, dq, dk, dv, w_self, gain_one, mixed_in, group_first, gains, n, nf
-    )
-    grad_packed, grad_w_self, own_gateup, result = lax.optimization_barrier(
-        (grad_packed, grad_w_self, own_gateup, result)
-    )
+    group_first, _, _ = gather_rows(grad_first.astype(bf16), n)
+    group_first, gains = lax.optimization_barrier((group_first, gains))
+    grad_w_mid = after(grad_w_mid, own_gateup, group_first)
+    own_mid = lax.psum_scatter(grad_w_mid, "fsdp", scatter_dimension=0, tiled=True)
+    own_gateup = share(after(own_gateup, group_first), n)
+    grad_keyval = jnp.concatenate([dck, dcv], axis=1)[:count]
+    cond_part = after(back_prod(grad_keyval, w_keyval), group_first)
+    late_active = after(active, group_first)
+    down = dot(late_active, w_down).astype(bf16)
+    down_pieces = scatter_start(down, n)
+    grad_mixed = pad_heads(back_prod(group_first, w_out).astype(bf16), 1)
+    grad_mixed = after(grad_mixed, down)
+    dq, dk, dv = attend_back(q, k, v, (0, 0, 0), pairs, grad_mixed, mixed, lse, ids, ids, tables)
+    dq, dk, dv = dq[:, :wide], dk[:, :wide], dv[:, :wide]
+    dq, own_gateup = lax.optimization_barrier((after(dq, *down_pieces), own_gateup))
+    grad_w_self = self_grads(normed_one, dq, dk, dv, self_all, gains, mixed_in, group_first, n, nf)
+    dq, dk, dv, grad_w_self = lax.optimization_barrier((dq, dk, dv, grad_w_self))
     own_self = lax.psum_scatter(after(grad_w_self, own_mid), "fsdp", scatter_dimension=0, tiled=True)
-    through = scatter_rows(lambda j: back_prod(block(grad_packed, j), w_self), n)
-    grad_keyval = jnp.concatenate([dck, dcv], axis=1)[:count]
-    grad_cond = sum_over_seq(after(back_prod(grad_keyval, w_keyval), through), n)
-    grad_cond = grad_cond.reshape(1, SEQS_GRP, COND, D)
+    grad_packed = jnp.concatenate([dq, dk, dv], axis=1)
+    through, early = scattered(lambda *at: back_prod(block(grad_packed, *at), w_self))
+    mid_part = share(after(own_mid[:, : 3 * wide + LANES], *early), n)
+    through, mid_part = lax.optimization_barrier((through, mid_part))
+    down_pieces = [after(piece, *early) for piece in down_pieces]
+    result = second + scatter_end(down, down_pieces, n) + b_down
+    cond_parts = sum_start(after(cond_part, *early), n)
+    grad_cond = sum_end(cond_parts, n).reshape(1, SEQS_GRP, COND, D)
     grad_inputs = grad_first + norm_back(through, normal_one, scaled_one, gain_one)[0]
 
     def joined(pieces):
         return pieces.reshape(n, r, wide).transpose(1, 0, 2).reshape(r, D)
 
     split = 3 * wide + LANES
-    mid_part = share(own_mid[:, :split], n)
     vectors = jnp.sum(mid_part[:, :, 3 * wide :].astype(f32), axis=0)
     own_cross = joined(own_mid[:, split:])
     own_out = joined(own_self[:, split:])
@@ -894,14 +946,14 @@
         grad_inputs[None],
         grad_cond,
         gains[:, 0],
-        natural_columns(self_part[:, :, : 3 * wide], 3, n).astype(f32),
+        spread(self_part, D, 3, n),
         own_out.astype(f32),
         gains[:, 1],
-        natural_columns(mid_part[:, :, 2 * wide : 3 * wide], 1, n).astype(f32),
-        natural_columns(mid_part[:, :, : 2 * wide], 2, n).astype(f32),
+        spread(mid_part, D, 1, n, 2),
+        spread(mid_part, D, 2, n),
         own_cross.astype(f32),
         vectors[:, 0],
-        natural_columns(own_gateup, 2, n).astype(f32),
+        spread(own_gateup, FF, 2, n),
         vectors[:, 2:10].reshape(8 * r),
         own_down.astype(f32),
         vectors[:, 1],

time: 760 us -> 707 us (0.930)
  waiting for transfers between devices: 231 us -> 214 us
  blocking collectives: 28.5 us -> 12 us
  Pallas kernels: 153 us -> 169 us
  local copies, waits for them, and re-layouts: 102 us -> 88 us
  starting transfers between devices: 83.5 us -> 75.7 us
    all_to_all x2 -> x1, blocking collectives: 28.5 us -> 12 us  [to_seq(): return lax.all_to_all(pieces, 'seq', 0, 0, tiled=True)]
    convert_element_type x10 -> x0, local copies, waits for them, and re-layouts: 14.4 us -> none  [the longest x3 10.3 us: shards(): natural_columns(own_gateup, 2, n).astype(f32)]
    ppermute x64 -> x54, starting transfers between devices: 67.7 us -> 56.9 us  [hop(): return lax.ppermute(value, 'seq', [(i, i ^ j) for i in range(4)])]
    convert_element_type x15 -> x2, other arithmetic: 10.9 us -> 0.47 us  [the longest x1 0.28 us: scatter_end(): (partial[4 * half:5 * half].astype(f32) + to_first).astype(bf16)]
    dot_general x1 -> x0, matrix products: 10 us -> none  [outer_sum(): lax.dot_general(left, right, (((0,), (0,)), ((), ())), preferred_element_...]
    pallas_call x0 -> x4, Pallas kernels: none -> 8.78 us  [spread(): pl.pallas_call(spread_kernel, out_shape=jax.ShapeDtypeStruct((r, parts *...]
    all_to_all x4 -> x5, waiting for transfers between devices: 14.4 us -> 5.89 us  [to_seq(): return lax.all_to_all(pieces, 'seq', 0, 0, tiled=True)]
    dot_general x11 -> x13, matrix products: 25.5 us -> 31.6 us  [back_prod(): lax.dot_general(left, weight, (((1,), (1,)), ((), ())), preferred_element...]
  transfers between devices with their start and end apart: 76 -> 67, of which waited for: 36 -> 37; matrix products, arithmetic and copies ran while one was open for 28% -> 28% of each run, Pallas kernels for 15% -> 17%
where the time goes in v4:
time: 707 us; the launch traced here: 699 us
  waiting for transfers between devices  214 us (30%)
  Pallas kernels  169 us (24%)
  local copies, waits for them, and re-layouts  88 us (12%)
  starting transfers between devices  75.7 us (11%)
  other arithmetic  65.1 us (9%)
  matrix products  59.7 us (8%)
  between operations  15.9 us (2%)
  blocking collectives  12 us (2%)
    ppermute x54, waiting for transfers between devices, hop(): return lax.ppermute(value, 'seq', [(i, i ^ j) for i in range(4)])  207 us
    ppermute x54, starting transfers between devices, hop(): return lax.ppermute(value, 'seq', [(i, i ^ j) for i in range(4)])  56.9 us
    pallas_call x1, Pallas kernels, feed(): pl.pallas_call(functools.partial(feed_kernel, chunk), out_shape=[jax.Shap...  47.9 us
    pallas_call x2, Pallas kernels, attend_back(): pl.pallas_call(functools.partial(attend_back_kernel, rope, tile), out_sha...  39.4 us
    unnamed x172, local copies, waits for them, and re-layouts  39.1 us
    dot_general x13, matrix products, back_prod(): lax.dot_general(left, weight, (((1,), (1,)), ((), ())), preferred_element...  31.6 us
    pallas_call x2, Pallas kernels, attend(): pl.pallas_call(functools.partial(attend_kernel, rope, tile), out_shape=sh...  29.5 us
    dot_general x14, matrix products, dot(): return jnp.dot(left, right, preferred_element_type=f32)  28.1 us
  transfers between devices with their start and end apart: 67, of which 37 were waited for; matrix products, arithmetic and copies ran while one was open for 28% of the time, Pallas kernels for 17%

profile of v4, /device:TPU:8, one launch (start us, length us, event | category | flops | bytes accessed | tf_op | source)
XLA Modules:
  0.0 699.3 jit_solution(5697076053529598949)
XLA Ops:
  9.5 12.0 %all_to_all.30 = bf16[4,48,1280]{2,1,0:T(8,128)(2,1)} all-to-all(bf16[4,48,1280]{2,1,0:T(8,128)(2,1)S(1)} %pad_maximum_fusion.14), channel_id=1, replica_groups=mesh['seq'=4,'fsdp'=8] {'seq'}, dimensions={0} | all-to-all | bytes 983040 | tf_op jit(solution)/shard_map/all_to_all | solution.py:699
  45.2 15.8 %collective-permute-done.1 = bf16[320,1536]{1,0:T(8,128)(2,1)S(1)} collective-permute-done((bf16[320,1536]{1,0:T(8,128)(2,1)S(1)}, bf16[320,1536]{1,0:T(8,128)(2,1)S(1)}, u32[]{:S(2)}, u32[]{:S(2)}) %collective-permute-start.1) | collective-permute-done | bytes 983072 | tf_op jit(solution)/shard_map/ppermute | solution.py:80
  64.1 6.9 collective-permute-done.2
  83.8 7.0 %fusion.31.refs_0_.refs_1_.refs_2_ = f32[1280,1152]{1,0:T(8,128)} fusion(bf16[1280,1536]{1,0:T(8,128)(2,1)S(1)} %fusion.4.h_ref, bf16[1536,1280]{1,0:T(8,128)(2,1)S(1)} %bitcast.113), kind=kOutput, calls=%fused_computation.71 | convolution fusion | flops 4529848320 | bytes 13369344 | tf_op jit(solution)/shard_map/dot_general | solution.py:62
  97.8 21.5 %attend_self.1 = (bf16[1280,384]{1,0:T(8,128)(2,1)}, bf16[1280,384]{1,0:T(8,128)(2,1)}, bf16[1280,384]{1,0:T(8,128)(2,1)}, bf16[1280,384]{1,0:T(8,128)(2,1)}, f32[3,8,1280]{2,1,0:T(8,128)}) custom-call(f32[1280,1152]{1,0:T(8,128)} %fusion.31.refs_0_.refs_1_.refs_2_, f32[1280,1152]{1,0:T(8,128)} %fusion.31.refs_0_.refs_1_.refs_2_, ...), custom_call_target="tpu_custom_call" | custom-call | flops 5033164800 | bytes 11796480 | tf_op jit(solution)/shard_map/attend_self/pallas_call | solution.py:333
  154.3 14.4 %collective-permute-done.9 = bf16[320,1536]{1,0:T(8,128)(2,1)S(1)} collective-permute-done((bf16[320,1536]{1,0:T(8,128)(2,1)}, bf16[320,1536]{1,0:T(8,128)(2,1)S(1)}, u32[]{:S(2)}, u32[]{:S(2)}) %collective-permute-start.9) | collective-permute-done | bytes 983072 | tf_op jit(solution)/shard_map/ppermute | solution.py:80
  180.5 15.2 %collective-permute-done.13 = bf16[320,1536]{1,0:T(8,128)(2,1)S(1)} collective-permute-done((bf16[320,1536]{1,0:T(8,128)(2,1)S(1)}, bf16[320,1536]{1,0:T(8,128)(2,1)S(1)}, u32[]{:S(2)}, u32[]{:S(2)}) %collective-permute-start.13) | collective-permute-done | bytes 983072 | tf_op jit(solution)/shard_map/ppermute | solution.py:80
  196.6 8.1 %collective-permute-done.14 = bf16[160,1536]{1,0:T(8,128)(2,1)S(1)} collective-permute-done((bf16[160,1536]{1,0:T(8,128)(2,1)S(1)}, bf16[160,1536]{1,0:T(8,128)(2,1)S(1)}, u32[]{:S(2)}, u32[]{:S(2)}) %collective-permute-start.14) | collective-permute-done | bytes 491552 | tf_op jit(solution)/shard_map/ppermute | solution.py:80
  210.7 8.0 %attend_cross.1 = (bf16[1280,384]{1,0:T(8,128)(2,1)}, f32[3,8,1280]{2,1,0:T(8,128)}) custom-call(bf16[1280,384]{1,0:T(8,128)(2,1)} %convolution_convert_fusion.3.refs_0_, bf16[272,768]{1,0:T(8,128)(2,1)} %pad.21.refs_1_.refs_2_, bf16[272,768]{1,0:T(8,128)(2,1)} %pad.21.refs_1_.refs_2_, s32[1,1280]{1,0:T(1,128)} %broadcast_in_dim.36.refs_5_.refs_3_.refs_6_.refs_8_, ...), custom_call_target="tpu_custom_call" | custom-call | flops 1069547520 | bytes 7151616 | tf_op jit(solution)/shard_map/attend_cross/pallas_call | solution.py:333
  223.4 6.7 collective-permute-done.16
  241.5 9.9 %collective-permute-done.17 = bf16[320,1536]{1,0:T(8,128)(2,1)S(1)} collective-permute-done((bf16[320,1536]{1,0:T(8,128)(2,1)S(1)}, bf16[320,1536]{1,0:T(8,128)(2,1)S(1)}, u32[]{:S(2)}, u32[]{:S(2)}) %collective-permute-start.17) | collective-permute-done | bytes 983072 | tf_op jit(solution)/shard_map/ppermute | solution.py:80
  264.9 9.9 %collective-permute-done.21 = bf16[320,1536]{1,0:T(8,128)(2,1)} collective-permute-done((bf16[320,1536]{1,0:T(8,128)(2,1)}, bf16[320,1536]{1,0:T(8,128)(2,1)}, u32[]{:S(2)}, u32[]{:S(2)}) %collective-permute-start.21) | collective-permute-done | bytes 983072 | tf_op jit(solution)/shard_map/ppermute | solution.py:80
  288.2 47.9 %feed.1 = (bf16[1280,1536]{1,0:T(8,128)(2,1)}, bf16[1280,1536]{1,0:T(8,128)(2,1)}, bf16[1280,1536]{1,0:T(8,128)(2,1)}, f32[1,1536]{1,0:T(1,128)}, f32[1,1536]{1,...) custom-call(bf16[1280,1536]{1,0:T(8,128)(2,1)} %constant_dynamic-update-slice_fusion.10.refs_0_.h_ref, ...), custom_call_target="tpu_custom_call" | custom-call | flops 36238786560 | bytes 42467328 | tf_op jit(solution)/shard_map/feed/pallas_call | solution.py:462
  338.9 9.7 %collective-permute-done.24 = bf16[160,1536]{1,0:T(8,128)(2,1)S(1)} collective-permute-done((bf16[160,1536]{1,0:T(8,128)(2,1)S(1)}, bf16[160,1536]{1,0:T(8,128)(2,1)S(1)}, u32[]{:S(2)}, u32[]{:S(2)}) %collective-permute-start.24) | collective-permute-done | bytes 491552 | tf_op jit(solution)/shard_map/ppermute | solution.py:80
  355.2 18.9 %gateup_grads.1 = bf16[8,4,48,3072]{3,2,1,0:T(8,128)(2,1)} custom-call(bf16[1280,1536]{1,0:T(8,128)(2,1)} %constant_dynamic-update-slice_fusion.10.refs_0_.h_ref, bf16[1280,1536]{1,0:T(8,128)(2,1)} %get-tuple-element.91.dg_ref, bf16[1280,1536]{1,0:T(8,128)(2,1)} %get-tuple-element.92.du_ref), custom_call_target="tpu_custom_call" | custom-call | flops 12079595520 | bytes 21233664 | tf_op jit(solution)/shard_map/gateup_grads/pallas_call | solution.py:532
  386.0 12.8 %collective-permute-done.28 = bf16[320,1536]{1,0:T(8,128)(2,1)} collective-permute-done((bf16[320,1536]{1,0:T(8,128)(2,1)S(1)}, bf16[320,1536]{1,0:T(8,128)(2,1)}, u32[]{:S(2)}, u32[]{:S(2)}) %collective-permute-start.28) | collective-permute-done | bytes 983072 | tf_op jit(solution)/shard_map/ppermute | solution.py:80
  423.2 10.1 %back_cross.1 = (bf16[1280,384]{1,0:T(8,128)(2,1)}, bf16[272,384]{1,0:T(8,128)(2,1)}, bf16[272,384]{1,0:T(8,128)(2,1)}) custom-call(bf16[1280,384]{1,0:T(8,128)(2,1)} %convolution_convert_fusion.3.refs_0_, bf16[272,768]{1,0:T(8,128)(2,1)} %pad.21.refs_1_.refs_2_, bf16[272,768]{1,0:T(8,128)(2,1)} %pad.21.refs_1_.refs_2_, ...), custom_call_target="tpu_custom_call" | custom-call | flops 2673868800 | bytes 7151616 | tf_op jit(solution)/shard_map/back_cross/pallas_call | solution.py:368
  461.3 10.4 %mid_grads.1 = bf16[8,4,48,1664]{3,2,1,0:T(8,128)(2,1)} custom-call(bf16[272,1536]{1,0:T(8,128)(2,1)} %pad.22.cond_ref, bf16[272,384]{1,0:T(8,128)(2,1)} %get-tuple-element.96.dk_ref, bf16[272,384]{1,0:T(8,128)(2,1)} %get-tuple-element.97.dv_ref, bf16[1280,1536]{1,0:T(8,128)(2,1)} %copy-done.20, bf16[1280,384]{1,0:T(8,128)(2,1)} %get-tuple-element.95.dq_ref, ...), custom_call_target="tpu_custom_call" | custom-call | flops 3661627392 | bytes 13811712 | tf_op jit(solution)/shard_map/mid_grads/pallas_call | solution.py:582
  483.0 18.8 %collective-permute-done.37 = bf16[320,1536]{1,0:T(8,128)(2,1)S(1)} collective-permute-done((bf16[320,1536]{1,0:T(8,128)(2,1)}, bf16[320,1536]{1,0:T(8,128)(2,1)S(1)}, u32[]{:S(2)}, u32[]{:S(2)}) %collective-permute-start.37) | collective-permute-done | bytes 983072 | tf_op jit(solution)/shard_map/ppermute | solution.py:80
  519.0 8.3 %convolution_convert_fusion = bf16[1280,1536]{1,0:T(8,128)(2,1)S(1)} fusion(bf16[1280,1536]{1,0:T(8,128)(2,1)S(1)} %copy-done.70, bf16[1536,1536]{1,0:T(8,128)(2,1)} %all-gather.11.cloned.1.call-done.refs_4_), kind=kOutput, calls=%fused_computation.7 | convolution fusion | flops 6041763840 | bytes 12582912 | tf_op jit(solution)/shard_map/dot_general | solution.py:62
  537.2 29.2 %back_self.1 = (bf16[1280,384]{1,0:T(8,128)(2,1)}, bf16[1280,384]{1,0:T(8,128)(2,1)}, bf16[1280,384]{1,0:T(8,128)(2,1)}) custom-call(bf16[1280,384]{1,0:T(8,128)(2,1)} %get-tuple-element.103.refs_0_, bf16[1280,384]{1,0:T(8,128)(2,1)} %get-tuple-element.104.refs_1_, bf16[1280,384]{1,0:T(8,128)(2,1)} %get-tuple-element.105.refs_2_, ...), custom_call_target="tpu_custom_call" | custom-call | flops 12582912000 | bytes 11796480 | tf_op jit(solution)/shard_map/back_self/pallas_call | solution.py:368
  567.5 14.1 %self_grads.1 = bf16[8,4,48,1664]{3,2,1,0:T(8,128)(2,1)} custom-call(bf16[1280,1536]{1,0:T(8,128)(2,1)} %copy-done.13, bf16[1280,384]{1,0:T(8,128)(2,1)} %get-tuple-element.118.dq_ref, bf16[1280,384]{1,0:T(8,128)(2,1)} %get-tuple-element.119.dk_ref, bf16[1280,384]{1,0:T(8,128)(2,1)} %get-tuple-element.120.dv_ref, bf16[1536,1280]{1,0:T(8,128)(2,1)} %bitcast.115, ...), custom_call_target="tpu_custom_call" | custom-call | flops 6039797760 | bytes 12582912 | tf_op jit(solution)/shard_map/self_grads/pallas_call | solution.py:640
  624.5 9.5 %collective-permute-done.46 = bf16[160,1536]{1,0:T(8,128)(2,1)S(1)} collective-permute-done((bf16[160,1536]{1,0:T(8,128)(2,1)S(1)}, bf16[160,1536]{1,0:T(8,128)(2,1)S(1)}, u32[]{:S(2)}, u32[]{:S(2)}) %collective-permute-start.46) | collective-permute-done | bytes 491552 | tf_op jit(solution)/shard_map/ppermute | solution.py:80
  635.4 14.4 %collective-permute-done.47 = bf16[160,1536]{1,0:T(8,128)(2,1)S(1)} collective-permute-done((bf16[160,1536]{1,0:T(8,128)(2,1)S(1)}, bf16[160,1536]{1,0:T(8,128)(2,1)S(1)}, u32[]{:S(2)}, u32[]{:S(2)}) %collective-permute-start.47) | collective-permute-done | bytes 491552 | tf_op jit(solution)/shard_map/ppermute | solution.py:80
  (501 shorter events, 343.6 us)
Async XLA Ops:
  7.2 70.9 %all-gather.5.cloned.1.call-start = ((), (), s32[]{:S(2)}) async-start(), calls=%async_computation.10 | async-start | bytes 4423680 | tf_op jit(solution)/shard_map/all_gather | solution.py:704
  26.6 104.9 %all-gather.7.cloned.1.call-start = ((), (), s32[]{:S(2)}) async-start(), calls=%async_computation.11 | async-start | bytes 6635520 | tf_op jit(solution)/shard_map/all_gather | solution.py:820
  33.7 254.5 %all-gather.11.cloned.1.call-start = ((), (), s32[]{:S(2)}) async-start(), calls=%async_computation.13 | async-start | bytes 5308416 | tf_op jit(solution)/shard_map/all_gather | solution.py:843
  38.5 22.9 %collective-permute-start = (bf16[320,1536]{1,0:T(8,128)(2,1)S(1)}, bf16[320,1536]{1,0:T(8,128)(2,1)S(1)}, u32[]{:S(2)}, u32[]{:S(2)}) collective-permute-start(bf16[320,1536]{1,0:T(8,128)(2,1)S(1)} %bitcast.134), channel_id=1, source_target_pairs={{0,8},{8,0},{16,24},{24,16},{1,9},{9,1},{17,25},{25,17},{2,10},{10... | collective-permute-start | bytes 2949128 | tf_op jit(solution)/shard_map/ppermute | solution.py:80
  92.3 27.1 %all-to-all-start.2 = ((bf16[4,48,3072]{2,1,0:T(8,128)(2,1)}), bf16[4,48,3072]{2,1,0:T(8,128)(2,1)S(1)}, u32[]{:S(2)}, u32[]{:S(2)}) async-start(bf16[4,48,3072]{2,1,0:T(8,128)(2,1)} %reshape.406), calls=%async_computation.2 | async-start | bytes 2359296 | tf_op jit(solution)/shard_map/all_to_all | solution.py:699
  95.8 192.4 %all-gather.9.cloned.1.call-start = ((), (), s32[]{:S(2)}) async-start(), calls=%async_computation.12 | async-start | bytes 10616832 | tf_op jit(solution)/shard_map/all_gather | solution.py:846
  120.4 279.6 %reduce-scatter.5.cloned.1.call-start = ((), (), s32[]{:S(2)}) async-start(), calls=%async_computation.14 | async-start | bytes 5308416 | tf_op jit(solution)/shard_map/reduce_scatter | solution.py:875
  146.0 22.6 %collective-permute-start.9 = (bf16[320,1536]{1,0:T(8,128)(2,1)}, bf16[320,1536]{1,0:T(8,128)(2,1)S(1)}, u32[]{:S(2)}, u32[]{:S(2)}) collective-permute-start(bf16[320,1536]{1,0:T(8,128)(2,1)} %pad_maximum_fusion.1), channel_id=1, source_target_pairs={{0,8},{8,0},{16,24},{24,16},{1,9},{9,1},{17,25},{25,17},{2,10},{10... | collective-permute-start | bytes 2949128 | tf_op jit(solution)/shard_map/ppermute | solution.py:80
  173.2 22.7 %collective-permute-start.12 = (bf16[320,1536]{1,0:T(8,128)(2,1)S(1)}, bf16[320,1536]{1,0:T(8,128)(2,1)S(1)}, u32[]{:S(2)}, u32[]{:S(2)}) collective-permute-start(bf16[320,1536]{1,0:T(8,128)(2,1)S(1)} %get-tuple-element.267), channel_id=1, source_target_pairs={{0,8},{8,0},{16,24},{24,16},{1,9},{9,1},{17,25},{25,17},{2,10},{10... | collective-permute-start | bytes 2949128 | tf_op jit(solution)/shard_map/ppermute | solution.py:80
  254.1 23.3 %collective-permute-start.20 = (bf16[320,1536]{1,0:T(8,128)(2,1)}, bf16[320,1536]{1,0:T(8,128)(2,1)}, u32[]{:S(2)}, u32[]{:S(2)}) collective-permute-start(bf16[320,1536]{1,0:T(8,128)(2,1)} %get-tuple-element.263), channel_id=1, source_target_pairs={{0,8},{8,0},{16,24},{24,16},{1,9},{9,1},{17,25},{25,17},{2,10},{10... | collective-permute-start | bytes 2949128 | tf_op jit(solution)/shard_map/ppermute | solution.py:80
  336.2 177.4 %reduce-scatter.7.cloned.1.call-start = ((), (), s32[]{:S(2)}) async-start(), calls=%async_computation.15 | async-start | bytes 10616832 | tf_op jit(solution)/shard_map/reduce_scatter | solution.py:883
  351.6 22.5 %collective-permute-start.25 = (bf16[320,1536]{1,0:T(8,128)(2,1)}, bf16[320,1536]{1,0:T(8,128)(2,1)}, u32[]{:S(2)}, u32[]{:S(2)}) collective-permute-start(bf16[320,1536]{1,0:T(8,128)(2,1)} %pad_maximum_fusion.5), channel_id=1, source_target_pairs={{0,8},{8,0},{16,24},{24,16},{1,9},{9,1},{17,25},{25,17},{2,10},{10... | collective-permute-start | bytes 2949128 | tf_op jit(solution)/shard_map/ppermute | solution.py:80
  400.0 181.7 %reduce-scatter.9.cloned.1.call-start = ((), (), s32[]{:S(2)}) async-start(), calls=%async_computation.16 | async-start | bytes 5750784 | tf_op jit(solution)/shard_map/reduce_scatter | solution.py:909
  446.1 25.7 %collective-permute-start.33 = (bf16[320,1536]{1,0:T(8,128)(2,1)}, bf16[320,1536]{1,0:T(8,128)(2,1)}, u32[]{:S(2)}, u32[]{:S(2)}) collective-permute-start(bf16[320,1536]{1,0:T(8,128)(2,1)} %pad_maximum_fusion.7), channel_id=1, source_target_pairs={{0,8},{8,0},{16,24},{24,16},{1,9},{9,1},{17,25},{25,17},{2,10},{10... | collective-permute-start | bytes 2949128 | tf_op jit(solution)/shard_map/ppermute | solution.py:80
  529.6 37.8 %collective-permute-start.40 = (bf16[160,1536]{1,0:T(8,128)(2,1)}, bf16[160,1536]{1,0:T(8,128)(2,1)}, u32[]{:S(2)}, u32[]{:S(2)}) collective-permute-start(bf16[160,1536]{1,0:T(8,128)(2,1)} %get-tuple-element.272), channel_id=1, source_target_pairs={{0,8},{8,0},{16,24},{24,16},{1,9},{9,1},{17,25},{25,17},{2,10},{10... | collective-permute-start | bytes 1474568 | tf_op jit(solution)/shard_map/ppermute | solution.py:80
  530.1 37.3 %collective-permute-start.41 = (bf16[160,1536]{1,0:T(8,128)(2,1)}, bf16[160,1536]{1,0:T(8,128)(2,1)S(1)}, u32[]{:S(2)}, u32[]{:S(2)}) collective-permute-start(bf16[160,1536]{1,0:T(8,128)(2,1)} %get-tuple-element.275), channel_id=1, source_target_pairs={{0,8},{8,0},{16,24},{24,16},{1,9},{9,1},{17,25},{25,17},{2,10},{10... | collective-permute-start | bytes 1474568 | tf_op jit(solution)/shard_map/ppermute | solution.py:80
  531.6 35.8 %collective-permute-start.42 = (bf16[160,1536]{1,0:T(8,128)(2,1)S(1)}, bf16[160,1536]{1,0:T(8,128)(2,1)S(1)}, u32[]{:S(2)}, u32[]{:S(2)}) collective-permute-start(bf16[160,1536]{1,0:T(8,128)(2,1)S(1)} %get-tuple-element.274), channel_id=1, source_target_pairs={{0,16},{8,24},{16,0},{24,8},{1,17},{9,25},{17,1},{25,9},{2,18},{10... | collective-permute-start | bytes 1474568 | tf_op jit(solution)/shard_map/ppermute | solution.py:80
  533.6 33.8 %collective-permute-start.43 = (bf16[160,1536]{1,0:T(8,128)(2,1)S(1)}, bf16[160,1536]{1,0:T(8,128)(2,1)}, u32[]{:S(2)}, u32[]{:S(2)}) collective-permute-start(bf16[160,1536]{1,0:T(8,128)(2,1)S(1)} %get-tuple-element.273), channel_id=1, source_target_pairs={{0,16},{8,24},{16,0},{24,8},{1,17},{9,25},{17,1},{25,9},{2,18},{10... | collective-permute-start | bytes 1474568 | tf_op jit(solution)/shard_map/ppermute | solution.py:80
  533.6 33.8 %all-to-all-start.3 = ((bf16[4,48,3072]{2,1,0:T(8,128)(2,1)}), bf16[4,48,3072]{2,1,0:T(8,128)(2,1)S(1)}, u32[]{:S(2)}, u32[]{:S(2)}) async-start(bf16[4,48,3072]{2,1,0:T(8,128)(2,1)} %bitcast.165), calls=%async_computation.5 | async-start | bytes 2359296 | tf_op jit(solution)/shard_map/all_to_all | solution.py:699
  537.2 135.5 %reduce-scatter.11.cloned.1.call-start = ((), (), s32[]{:S(2)}) async-start(), calls=%async_computation.17 | async-start | bytes 5750784 | tf_op jit(solution)/shard_map/reduce_scatter | solution.py:923
  614.7 49.2 %collective-permute-start.48 = (bf16[320,1536]{1,0:T(8,128)(2,1)}, bf16[320,1536]{1,0:T(8,128)(2,1)}, u32[]{:S(2)}, u32[]{:S(2)}) collective-permute-start(bf16[320,1536]{1,0:T(8,128)(2,1)} %pad_maximum_fusion.9), channel_id=1, source_target_pairs={{0,8},{8,0},{16,24},{24,16},{1,9},{9,1},{17,25},{25,17},{2,10},{10... | collective-permute-start | bytes 2949128 | tf_op jit(solution)/shard_map/ppermute | solution.py:80
  617.4 46.5 %collective-permute-start.49 = (bf16[320,1536]{1,0:T(8,128)(2,1)}, bf16[320,1536]{1,0:T(8,128)(2,1)}, u32[]{:S(2)}, u32[]{:S(2)}) collective-permute-start(bf16[320,1536]{1,0:T(8,128)(2,1)} %pad_maximum_fusion.10), channel_id=1, source_target_pairs={{0,16},{8,24},{16,0},{24,8},{1,17},{9,25},{17,1},{25,9},{2,18},{10... | collective-permute-start | bytes 2949128 | tf_op jit(solution)/shard_map/ppermute | solution.py:80
  621.4 28.4 %collective-permute-start.47 = (bf16[160,1536]{1,0:T(8,128)(2,1)S(1)}, bf16[160,1536]{1,0:T(8,128)(2,1)S(1)}, u32[]{:S(2)}, u32[]{:S(2)}) collective-permute-start(bf16[160,1536]{1,0:T(8,128)(2,1)S(1)} %get-tuple-element.271), channel_id=1, source_target_pairs={{0,8},{8,0},{16,24},{24,16},{1,9},{9,1},{17,25},{25,17},{2,10},{10... | collective-permute-start | bytes 1474568 | tf_op jit(solution)/shard_map/ppermute | solution.py:80
  623.7 28.8 %collective-permute-start.51 = (bf16[260,768]{1,0:T(8,128)(2,1)S(1)}, bf16[260,768]{1,0:T(8,128)(2,1)S(1)}, u32[]{:S(2)}, u32[]{:S(2)}) collective-permute-start(bf16[260,768]{1,0:T(8,128)(2,1)S(1)} %get-tuple-element.282), channel_id=1, source_target_pairs={{0,16},{8,24},{16,0},{24,8},{1,17},{9,25},{17,1},{25,9},{2,18},{10... | collective-permute-start | bytes 1198088 | tf_op jit(solution)/shard_map/ppermute | solution.py:80
  (116 other events, 1089.3 us)
Sparse Core Ops, SparseCore 0:
  21.7 43.0 all-gather.4
  67.0 59.5 all-gather.6
  128.2 50.9 all-gather.10
  181.2 88.2 all-gather.8
  336.3 58.0 reduce-scatter.4
  400.1 107.1 reduce-scatter.6
  513.7 59.5 reduce-scatter.8
  581.8 60.9 reduce-scatter.10

commit v5 on v4

--- a/solution.py
+++ b/solution.py
@@ -1,4 +1,5 @@
 import functools
+import math
 
 import jax
 import jax.numpy as jnp
@@ -86,18 +87,19 @@
     return jnp.arange(n, dtype=jnp.int32)
 
 
-def gather_rows(value, n):
+def gather_rows(value, n, gates=()):
     if n != 4:
         whole = lax.all_gather(value, "seq", axis=0, tiled=True)
         return whole, (whole,), (whole,)
     half = value.shape[0] // 2
     first, second = hop(value, 1), hop(value, 2)
+    first, second = after(first, *gates), after(second, *gates)
     third, fourth = hop(second[:half], 1), hop(first[half:], 2)
     whole = jnp.concatenate([value, first, second, third, fourth], axis=0)
     return whole, (first, second), (third, fourth)
 
 
-def scatter_rows(blocks, rows, n):
+def scatter_rows(blocks, rows, n, gates=()):
     if n != 4:
         whole = jnp.concatenate([blocks(j, 0, rows) for j in range(n)], axis=0).astype(bf16)
         out = lax.psum_scatter(whole, "seq", scatter_dimension=0, tiled=True).astype(f32)
@@ -105,6 +107,7 @@
     half = rows // 2
     to_first = hop(blocks(3, 0, half).astype(bf16), 1)
     to_second = hop(blocks(3, half, rows).astype(bf16), 2)
+    to_first, to_second = after(to_first, *gates), after(to_second, *gates)
     one, two = blocks(1, 0, rows).astype(f32), blocks(2, 0, rows).astype(f32)
     one = jnp.concatenate([one[:half], one[half:] + to_second.astype(f32)], axis=0)
     two = jnp.concatenate([two[:half] + to_first.astype(f32), two[half:]], axis=0)
@@ -680,11 +683,15 @@
         out_ref[:, s * c : (s + 1) * c] = in_ref[s].astype(f32)
 
 
-def spread(pieces, width, parts, n, first=0):
+def spread(pieces, width, parts, n, start=0):
     r = pieces.shape[1]
     c = width // n
     if r % 16 or c % LANES:
-        return natural_columns(pieces[:, :, first * c : (first + parts) * c], parts, n).astype(f32)
+        return natural_columns(pieces[:, :, start : start + parts * c], parts, n).astype(f32)
+    step = math.gcd(c, start) if start else c
+    if step < c:
+        pieces, start = pieces[:, :, start : start + parts * c], 0
+    first = start // c
     return pl.pallas_call(
         spread_kernel,
         out_shape=jax.ShapeDtypeStruct((r, parts * n * c), f32),
@@ -842,12 +849,13 @@
     gateup_pieces = to_seq(after(column_parts(proj_gateup, 2, n), packed))
     w_down = lax.all_gather(after(proj_down, mid_pieces), "fsdp", axis=0, tiled=True)
     q, k, v, mixed, lse = attend(packed, packed, packed, (0, pairs, 2 * pairs), pairs, ids, ids, tables)
+    mixed = after(mixed, *grad_ends)
     gateup_pieces = after(gateup_pieces.reshape(n * r, 2 * hidden), mixed)
     w_gateup = lax.all_gather(gateup_pieces, "fsdp", axis=0, tiled=True)
     w_gateup = w_gateup.reshape(nf, n, r, 2 * hidden)
     if r % 16:
         w_gateup = w_gateup.transpose(1, 0, 2, 3).reshape(1, 1, D, 2 * hidden)
-    mixed_in = after(mixed[:, :wide], *grad_ends)
+    mixed_in = mixed[:, :wide]
     first = inputs + scattered(lambda *at: dot(block(mixed_in, *at), w_out))[0]
 
     normal_two, scaled_two, normed = norm_rows(first, gain_two)
@@ -903,15 +911,15 @@
 
     gains = grad_gain_two.astype(bf16).reshape(n, nf, r, 1).transpose(1, 0, 2, 3).reshape(D, 1)
     gains = jnp.pad(gains, ((0, 0), (1, LANES - 2)))
-    group_first, _, _ = gather_rows(grad_first.astype(bf16), n)
+    down = dot(after(active, grad_first), w_down).astype(bf16)
+    group_first, _, _ = gather_rows(grad_first.astype(bf16), n, (down,))
     group_first, gains = lax.optimization_barrier((group_first, gains))
     grad_w_mid = after(grad_w_mid, own_gateup, group_first)
     own_mid = lax.psum_scatter(grad_w_mid, "fsdp", scatter_dimension=0, tiled=True)
     own_gateup = share(after(own_gateup, group_first), n)
     grad_keyval = jnp.concatenate([dck, dcv], axis=1)[:count]
     cond_part = after(back_prod(grad_keyval, w_keyval), group_first)
-    late_active = after(active, group_first)
-    down = dot(late_active, w_down).astype(bf16)
+    down = after(down, group_first)
     down_pieces = scatter_start(down, n)
     grad_mixed = pad_heads(back_prod(group_first, w_out).astype(bf16), 1)
     grad_mixed = after(grad_mixed, down)
@@ -923,34 +931,34 @@
     own_self = lax.psum_scatter(after(grad_w_self, own_mid), "fsdp", scatter_dimension=0, tiled=True)
     grad_packed = jnp.concatenate([dq, dk, dv], axis=1)
     through, early = scattered(lambda *at: back_prod(block(grad_packed, *at), w_self))
-    mid_part = share(after(own_mid[:, : 3 * wide + LANES], *early), n)
-    through, mid_part = lax.optimization_barrier((through, mid_part))
     down_pieces = [after(piece, *early) for piece in down_pieces]
     result = second + scatter_end(down, down_pieces, n) + b_down
     cond_parts = sum_start(after(cond_part, *early), n)
-    grad_cond = sum_end(cond_parts, n).reshape(1, SEQS_GRP, COND, D)
-    grad_inputs = grad_first + norm_back(through, normal_one, scaled_one, gain_one)[0]
+    own_gateup = after(own_gateup, *early)
 
     def joined(pieces):
         return pieces.reshape(n, r, wide).transpose(1, 0, 2).reshape(r, D)
 
     split = 3 * wide + LANES
-    vectors = jnp.sum(mid_part[:, :, 3 * wide :].astype(f32), axis=0)
     own_cross = joined(own_mid[:, split:])
     own_out = joined(own_self[:, split:])
-    self_part = share(own_self[:, :split], n)
-    gains = jnp.sum(self_part[:, :, 3 * wide :].astype(f32), axis=0)
+    last_part = share(jnp.concatenate([own_mid[:, :split], own_self[:, :split]], axis=1), n)
+    grad_cond = sum_end([after(part, last_part) for part in cond_parts], n)
+    grad_cond = grad_cond.reshape(1, SEQS_GRP, COND, D)
+    vectors = jnp.sum(last_part[:, :, 3 * wide : split].astype(f32), axis=0)
+    grad_inputs = grad_first + norm_back(through, normal_one, scaled_one, gain_one)[0]
+    gains = jnp.sum(last_part[:, :, split + 3 * wide :].astype(f32), axis=0)
 
     return (
         result.astype(bf16)[None],
         grad_inputs[None],
         grad_cond,
         gains[:, 0],
-        spread(self_part, D, 3, n),
+        spread(last_part, D, 3, n, split),
         own_out.astype(f32),
         gains[:, 1],
-        spread(mid_part, D, 1, n, 2),
-        spread(mid_part, D, 2, n),
+        spread(last_part, D, 1, n, 2 * wide),
+        spread(last_part, D, 2, n),
         own_cross.astype(f32),
         vectors[:, 0],
         spread(own_gateup, FF, 2, n),

time: 707 us -> 691 us (0.977)
  waiting for transfers between devices: 214 us -> 200 us
    ppermute x54, waiting for transfers between devices: 207 us -> 188 us  [hop(): return lax.ppermute(value, 'seq', [(i, i ^ j) for i in range(4)])]
    all_to_all x5 -> x4, starting transfers between devices: 18.1 us -> 14.3 us  [to_seq(): return lax.all_to_all(pieces, 'seq', 0, 0, tiled=True)]
    unnamed x172 -> x174, local copies, waits for them, and re-layouts: 39.1 us -> 37.6 us
  transfers between devices with their start and end apart: 67 -> 66, of which waited for: 37 -> 36; matrix products, arithmetic and copies ran while one was open for 28% -> 27% of each run, Pallas kernels for 17% -> 18%
where the time goes in v5:
time: 691 us; the launch traced here: 682 us
  waiting for transfers between devices  200 us (29%)
  Pallas kernels  169 us (24%)
  local copies, waits for them, and re-layouts  82.5 us (12%)
  starting transfers between devices  77.8 us (11%)
  other arithmetic  63.3 us (9%)
  matrix products  60.9 us (9%)
  between operations  16 us (2%)
  blocking collectives  12 us (2%)
    ppermute x54, waiting for transfers between devices, hop(): return lax.ppermute(value, 'seq', [(i, i ^ j) for i in range(4)])  188 us
    ppermute x54, starting transfers between devices, hop(): return lax.ppermute(value, 'seq', [(i, i ^ j) for i in range(4)])  62.8 us
    pallas_call x1, Pallas kernels, feed(): pl.pallas_call(functools.partial(feed_kernel, chunk), out_shape=[jax.Shap...  47.9 us
    pallas_call x2, Pallas kernels, attend_back(): pl.pallas_call(functools.partial(attend_back_kernel, rope, tile), out_sha...  39.5 us
    unnamed x174, local copies, waits for them, and re-layouts  37.6 us
    dot_general x14, matrix products, dot(): return jnp.dot(left, right, preferred_element_type=f32)  30.7 us
    dot_general x13, matrix products, back_prod(): lax.dot_general(left, weight, (((1,), (1,)), ((), ())), preferred_element...  30.2 us
    pallas_call x2, Pallas kernels, attend(): pl.pallas_call(functools.partial(attend_kernel, rope, tile), out_shape=sh...  29.5 us
  transfers between devices with their start and end apart: 66, of which 36 were waited for; matrix products, arithmetic and copies ran while one was open for 27% of the time, Pallas kernels for 18%

profile of v5, /device:TPU:8, one launch (start us, length us, event | category | flops | bytes accessed | tf_op | source)
XLA Modules:
  0.0 682.2 jit_solution(7672259292251151859)
XLA Ops:
  9.5 12.0 %all_to_all.25 = bf16[4,48,1280]{2,1,0:T(8,128)(2,1)} all-to-all(bf16[4,48,1280]{2,1,0:T(8,128)(2,1)S(1)} %pad_maximum_fusion.15), channel_id=1, replica_groups=mesh['seq'=4,'fsdp'=8] {'seq'}, dimensions={0} | all-to-all | bytes 983040 | tf_op jit(solution)/shard_map/all_to_all | solution.py:706
  45.2 15.9 %collective-permute-done.1 = bf16[320,1536]{1,0:T(8,128)(2,1)S(1)} collective-permute-done((bf16[320,1536]{1,0:T(8,128)(2,1)S(1)}, bf16[320,1536]{1,0:T(8,128)(2,1)S(1)}, u32[]{:S(2)}, u32[]{:S(2)}) %collective-permute-start.1) | collective-permute-done | bytes 983072 | tf_op jit(solution)/shard_map/ppermute | solution.py:81
  64.1 6.9 %collective-permute-done.2 = bf16[160,1536]{1,0:T(8,128)(2,1)S(1)} collective-permute-done((bf16[160,1536]{1,0:T(8,128)(2,1)S(1)}, bf16[160,1536]{1,0:T(8,128)(2,1)S(1)}, u32[]{:S(2)}, u32[]{:S(2)}) %collective-permute-start.2) | collective-permute-done | bytes 491552 | tf_op jit(solution)/shard_map/ppermute | solution.py:81
  83.8 7.0 %fusion.31.refs_0_.refs_1_.refs_2_ = f32[1280,1152]{1,0:T(8,128)} fusion(bf16[1280,1536]{1,0:T(8,128)(2,1)S(1)} %fusion.4.h_ref, bf16[1536,1280]{1,0:T(8,128)(2,1)S(1)} %bitcast.112), kind=kOutput, calls=%fused_computation.70 | convolution fusion | flops 4529848320 | bytes 13369344 | tf_op jit(solution)/shard_map/dot_general | solution.py:63
  101.4 21.6 %attend_self.1 = (bf16[1280,384]{1,0:T(8,128)(2,1)}, bf16[1280,384]{1,0:T(8,128)(2,1)}, bf16[1280,384]{1,0:T(8,128)(2,1)}, bf16[1280,384]{1,0:T(8,128)(2,1)}, f32[3,8,1280]{2,1,0:T(8,128)}) custom-call(f32[1280,1152]{1,0:T(8,128)} %fusion.31.refs_0_.refs_1_.refs_2_, f32[1280,1152]{1,0:T(8,128)} %fusion.31.refs_0_.refs_1_.refs_2_, ...), custom_call_target="tpu_custom_call" | custom-call | flops 5033164800 | bytes 11796480 | tf_op jit(solution)/shard_map/attend_self/pallas_call | solution.py:336
  136.1 8.4 %collective-permute-done.8 = bf16[160,1536]{1,0:T(8,128)(2,1)S(1)} collective-permute-done((bf16[160,1536]{1,0:T(8,128)(2,1)S(1)}, bf16[160,1536]{1,0:T(8,128)(2,1)S(1)}, u32[]{:S(2)}, u32[]{:S(2)}) %collective-permute-start.8) | collective-permute-done | bytes 491552 | tf_op jit(solution)/shard_map/ppermute | solution.py:81
  151.6 17.5 %collective-permute-done.9 = bf16[320,1536]{1,0:T(8,128)(2,1)S(1)} collective-permute-done((bf16[320,1536]{1,0:T(8,128)(2,1)}, bf16[320,1536]{1,0:T(8,128)(2,1)S(1)}, u32[]{:S(2)}, u32[]{:S(2)}) %collective-permute-start.9) | collective-permute-done | bytes 983072 | tf_op jit(solution)/shard_map/ppermute | solution.py:81
  183.0 14.8 %collective-permute-done.13 = bf16[320,1536]{1,0:T(8,128)(2,1)S(1)} collective-permute-done((bf16[320,1536]{1,0:T(8,128)(2,1)S(1)}, bf16[320,1536]{1,0:T(8,128)(2,1)S(1)}, u32[]{:S(2)}, u32[]{:S(2)}) %collective-permute-start.13) | collective-permute-done | bytes 983072 | tf_op jit(solution)/shard_map/ppermute | solution.py:81
  200.7 7.4 %collective-permute-done.14 = bf16[160,1536]{1,0:T(8,128)(2,1)S(1)} collective-permute-done((bf16[160,1536]{1,0:T(8,128)(2,1)S(1)}, bf16[160,1536]{1,0:T(8,128)(2,1)S(1)}, u32[]{:S(2)}, u32[]{:S(2)}) %collective-permute-start.14) | collective-permute-done | bytes 491552 | tf_op jit(solution)/shard_map/ppermute | solution.py:81
  214.2 7.9 %attend_cross.1 = (bf16[1280,384]{1,0:T(8,128)(2,1)}, f32[3,8,1280]{2,1,0:T(8,128)}) custom-call(bf16[1280,384]{1,0:T(8,128)(2,1)} %convolution_convert_fusion.3.refs_0_, bf16[272,768]{1,0:T(8,128)(2,1)} %pad.21.refs_1_.refs_2_, bf16[272,768]{1,0:T(8,128)(2,1)} %pad.21.refs_1_.refs_2_, s32[1,1280]{1,0:T(1,128)} %broadcast_in_dim.36.refs_5_.refs_3_.refs_6_.refs_8_, ...), custom_call_target="tpu_custom_call" | custom-call | flops 1069547520 | bytes 7151616 | tf_op jit(solution)/shard_map/attend_cross/pallas_call | solution.py:336
  242.1 14.2 %collective-permute-done.17 = bf16[320,1536]{1,0:T(8,128)(2,1)S(1)} collective-permute-done((bf16[320,1536]{1,0:T(8,128)(2,1)S(1)}, bf16[320,1536]{1,0:T(8,128)(2,1)S(1)}, u32[]{:S(2)}, u32[]{:S(2)}) %collective-permute-start.17) | collective-permute-done | bytes 983072 | tf_op jit(solution)/shard_map/ppermute | solution.py:81
  266.9 12.3 %collective-permute-done.21 = bf16[320,1536]{1,0:T(8,128)(2,1)} collective-permute-done((bf16[320,1536]{1,0:T(8,128)(2,1)}, bf16[320,1536]{1,0:T(8,128)(2,1)}, u32[]{:S(2)}, u32[]{:S(2)}) %collective-permute-start.21) | collective-permute-done | bytes 983072 | tf_op jit(solution)/shard_map/ppermute | solution.py:81
  292.2 47.9 %feed.1 = (bf16[1280,1536]{1,0:T(8,128)(2,1)}, bf16[1280,1536]{1,0:T(8,128)(2,1)}, bf16[1280,1536]{1,0:T(8,128)(2,1)}, f32[1,1536]{1,0:T(1,128)}, f32[1,1536]{1,...) custom-call(bf16[1280,1536]{1,0:T(8,128)(2,1)} %constant_dynamic-update-slice_fusion.10.refs_0_.h_ref, ...), custom_call_target="tpu_custom_call" | custom-call | flops 36238786560 | bytes 42467328 | tf_op jit(solution)/shard_map/feed/pallas_call | solution.py:465
  344.6 6.3 collective-permute-done.24
  358.8 18.9 %gateup_grads.1 = bf16[8,4,48,3072]{3,2,1,0:T(8,128)(2,1)} custom-call(bf16[1280,1536]{1,0:T(8,128)(2,1)} %constant_dynamic-update-slice_fusion.10.refs_0_.h_ref, bf16[1280,1536]{1,0:T(8,128)(2,1)} %get-tuple-element.94.dg_ref, bf16[1280,1536]{1,0:T(8,128)(2,1)} %get-tuple-element.95.du_ref), custom_call_target="tpu_custom_call" | custom-call | flops 12079595520 | bytes 21233664 | tf_op jit(solution)/shard_map/gateup_grads/pallas_call | solution.py:535
  390.7 12.0 %collective-permute-done.28 = bf16[320,1536]{1,0:T(8,128)(2,1)} collective-permute-done((bf16[320,1536]{1,0:T(8,128)(2,1)S(1)}, bf16[320,1536]{1,0:T(8,128)(2,1)}, u32[]{:S(2)}, u32[]{:S(2)}) %collective-permute-start.28) | collective-permute-done | bytes 983072 | tf_op jit(solution)/shard_map/ppermute | solution.py:81
  425.8 10.2 %back_cross.1 = (bf16[1280,384]{1,0:T(8,128)(2,1)}, bf16[272,384]{1,0:T(8,128)(2,1)}, bf16[272,384]{1,0:T(8,128)(2,1)}) custom-call(bf16[1280,384]{1,0:T(8,128)(2,1)} %convolution_convert_fusion.3.refs_0_, bf16[272,768]{1,0:T(8,128)(2,1)} %pad.21.refs_1_.refs_2_, bf16[272,768]{1,0:T(8,128)(2,1)} %pad.21.refs_1_.refs_2_, ...), custom_call_target="tpu_custom_call" | custom-call | flops 2673868800 | bytes 7151616 | tf_op jit(solution)/shard_map/back_cross/pallas_call | solution.py:371
  442.2 8.6 %collective-permute-done.32 = bf16[160,1536]{1,0:T(8,128)(2,1)S(1)} collective-permute-done((bf16[160,1536]{1,0:T(8,128)(2,1)S(1)}, bf16[160,1536]{1,0:T(8,128)(2,1)S(1)}, u32[]{:S(2)}, u32[]{:S(2)}) %collective-permute-start.32) | collective-permute-done | bytes 491552 | tf_op jit(solution)/shard_map/ppermute | solution.py:81
  465.9 10.4 %mid_grads.1 = bf16[8,4,48,1664]{3,2,1,0:T(8,128)(2,1)} custom-call(bf16[272,1536]{1,0:T(8,128)(2,1)} %pad.22.cond_ref, bf16[272,384]{1,0:T(8,128)(2,1)} %get-tuple-element.99.dk_ref, bf16[272,384]{1,0:T(8,128)(2,1)} %get-tuple-element.100.dv_ref, bf16[1280,1536]{1,0:T(8,128)(2,1)} %copy-done.20, bf16[1280,384]{1,0:T(8,128)(2,1)} %get-tuple-element.98.dq_ref, ...), custom_call_target="tpu_custom_call" | custom-call | flops 3661627392 | bytes 13811712 | tf_op jit(solution)/shard_map/mid_grads/pallas_call | solution.py:585
  487.7 10.9 %convolution_convert_fusion = bf16[1280,1536]{1,0:T(8,128)(2,1)} fusion(bf16[1280,1536]{1,0:T(8,128)(2,1)} %get-tuple-element.104, bf16[1536,1536]{1,0:T(8,128)(2,1)} %all-gather.11.cloned.1.call-done.refs_4_), kind=kOutput, calls=%fused_computation.7 | convolution fusion | flops 6041763840 | bytes 12582912 | tf_op jit(solution)/shard_map/dot_general | solution.py:63
  527.5 29.3 %back_self.1 = (bf16[1280,384]{1,0:T(8,128)(2,1)}, bf16[1280,384]{1,0:T(8,128)(2,1)}, bf16[1280,384]{1,0:T(8,128)(2,1)}) custom-call(bf16[1280,384]{1,0:T(8,128)(2,1)} %get-tuple-element.109.refs_0_, bf16[1280,384]{1,0:T(8,128)(2,1)} %get-tuple-element.110.refs_1_, bf16[1280,384]{1,0:T(8,128)(2,1)} %get-tuple-element.111.refs_2_, ...), custom_call_target="tpu_custom_call" | custom-call | flops 12582912000 | bytes 11796480 | tf_op jit(solution)/shard_map/back_self/pallas_call | solution.py:371
  557.8 14.2 %self_grads.1 = bf16[8,4,48,1664]{3,2,1,0:T(8,128)(2,1)} custom-call(bf16[1280,1536]{1,0:T(8,128)(2,1)} %copy-done.13, bf16[1280,384]{1,0:T(8,128)(2,1)} %get-tuple-element.124.dq_ref, bf16[1280,384]{1,0:T(8,128)(2,1)} %get-tuple-element.125.dk_ref, bf16[1280,384]{1,0:T(8,128)(2,1)} %get-tuple-element.126.dv_ref, bf16[1536,1280]{1,0:T(8,128)(2,1)} %bitcast.114, ...), custom_call_target="tpu_custom_call" | custom-call | flops 6039797760 | bytes 12582912 | tf_op jit(solution)/shard_map/self_grads/pallas_call | solution.py:643
  611.3 10.3 %collective-permute-done.46 = bf16[160,1536]{1,0:T(8,128)(2,1)S(1)} collective-permute-done((bf16[160,1536]{1,0:T(8,128)(2,1)S(1)}, bf16[160,1536]{1,0:T(8,128)(2,1)S(1)}, u32[]{:S(2)}, u32[]{:S(2)}) %collective-permute-start.46) | collective-permute-done | bytes 491552 | tf_op jit(solution)/shard_map/ppermute | solution.py:81
  622.8 13.0 %collective-permute-done.47 = bf16[160,1536]{1,0:T(8,128)(2,1)S(1)} collective-permute-done((bf16[160,1536]{1,0:T(8,128)(2,1)S(1)}, bf16[160,1536]{1,0:T(8,128)(2,1)S(1)}, u32[]{:S(2)}, u32[]{:S(2)}) %collective-permute-start.47) | collective-permute-done | bytes 491552 | tf_op jit(solution)/shard_map/ppermute | solution.py:81
  (502 shorter events, 328.3 us)
Async XLA Ops:
  7.2 70.9 %all-gather.5.cloned.1.call-start = ((), (), s32[]{:S(2)}) async-start(), calls=%async_computation.9 | async-start | bytes 4423680 | tf_op jit(solution)/shard_map/all_gather | solution.py:711
  26.6 99.9 %all-gather.7.cloned.1.call-start = ((), (), s32[]{:S(2)}) async-start(), calls=%async_computation.10 | async-start | bytes 6635520 | tf_op jit(solution)/shard_map/all_gather | solution.py:827
  33.7 258.5 %all-gather.11.cloned.1.call-start = ((), (), s32[]{:S(2)}) async-start(), calls=%async_computation.12 | async-start | bytes 5308416 | tf_op jit(solution)/shard_map/all_gather | solution.py:850
  92.3 32.3 %all-to-all-start.2 = ((bf16[4,48,3072]{2,1,0:T(8,128)(2,1)}), bf16[4,48,3072]{2,1,0:T(8,128)(2,1)S(1)}, u32[]{:S(2)}, u32[]{:S(2)}) async-start(bf16[4,48,3072]{2,1,0:T(8,128)(2,1)} %reshape.403), calls=%async_computation.2 | async-start | bytes 2359296 | tf_op jit(solution)/shard_map/all_to_all | solution.py:706
  95.8 196.4 %all-gather.9.cloned.1.call-start = ((), (), s32[]{:S(2)}) async-start(), calls=%async_computation.11 | async-start | bytes 10616832 | tf_op jit(solution)/shard_map/all_gather | solution.py:854
  96.1 26.9 %collective-permute-start.6 = (bf16[160,1536]{1,0:T(8,128)(2,1)S(1)}, bf16[160,1536]{1,0:T(8,128)(2,1)S(1)}, u32[]{:S(2)}, u32[]{:S(2)}) collective-permute-start(bf16[160,1536]{1,0:T(8,128)(2,1)S(1)} %slice.388), channel_id=1, source_target_pairs={{0,8},{8,0},{16,24},{24,16},{1,9},{9,1},{17,25},{25,17},{2,10},{10... | collective-permute-start | bytes 1474568 | tf_op jit(solution)/shard_map/ppermute | solution.py:81
  98.2 24.8 %collective-permute-start.7 = (bf16[160,1536]{1,0:T(8,128)(2,1)S(1)}, bf16[160,1536]{1,0:T(8,128)(2,1)S(1)}, u32[]{:S(2)}, u32[]{:S(2)}) collective-permute-start(bf16[160,1536]{1,0:T(8,128)(2,1)S(1)} %slice.389), channel_id=1, source_target_pairs={{0,16},{8,24},{16,0},{24,8},{1,17},{9,25},{17,1},{25,9},{2,18},{10... | collective-permute-start | bytes 1474568 | tf_op jit(solution)/shard_map/ppermute | solution.py:81
  125.6 277.9 %reduce-scatter.5.cloned.1.call-start = ((), (), s32[]{:S(2)}) async-start(), calls=%async_computation.13 | async-start | bytes 5308416 | tf_op jit(solution)/shard_map/reduce_scatter | solution.py:883
  145.7 23.4 %collective-permute-start.9 = (bf16[320,1536]{1,0:T(8,128)(2,1)}, bf16[320,1536]{1,0:T(8,128)(2,1)S(1)}, u32[]{:S(2)}, u32[]{:S(2)}) collective-permute-start(bf16[320,1536]{1,0:T(8,128)(2,1)} %pad_maximum_fusion.1), channel_id=1, source_target_pairs={{0,8},{8,0},{16,24},{24,16},{1,9},{9,1},{17,25},{25,17},{2,10},{10... | collective-permute-start | bytes 2949128 | tf_op jit(solution)/shard_map/ppermute | solution.py:81
  148.3 23.2 %collective-permute-start.11 = (bf16[320,1536]{1,0:T(8,128)(2,1)}, bf16[320,1536]{1,0:T(8,128)(2,1)}, u32[]{:S(2)}, u32[]{:S(2)}) collective-permute-start(bf16[320,1536]{1,0:T(8,128)(2,1)} %pad_maximum_fusion.2), channel_id=1, source_target_pairs={{0,16},{8,24},{16,0},{24,8},{1,17},{9,25},{17,1},{25,9},{2,18},{10... | collective-permute-start | bytes 2949128 | tf_op jit(solution)/shard_map/ppermute | solution.py:81
  175.1 23.9 %collective-permute-start.12 = (bf16[320,1536]{1,0:T(8,128)(2,1)S(1)}, bf16[320,1536]{1,0:T(8,128)(2,1)S(1)}, u32[]{:S(2)}, u32[]{:S(2)}) collective-permute-start(bf16[320,1536]{1,0:T(8,128)(2,1)S(1)} %get-tuple-element.275), channel_id=1, source_target_pairs={{0,8},{8,0},{16,24},{24,16},{1,9},{9,1},{17,25},{25,17},{2,10},{10... | collective-permute-start | bytes 2949128 | tf_op jit(solution)/shard_map/ppermute | solution.py:81
  232.9 23.4 %collective-permute-start.17 = (bf16[320,1536]{1,0:T(8,128)(2,1)S(1)}, bf16[320,1536]{1,0:T(8,128)(2,1)S(1)}, u32[]{:S(2)}, u32[]{:S(2)}) collective-permute-start(bf16[320,1536]{1,0:T(8,128)(2,1)S(1)} %pad_maximum_fusion.3), channel_id=1, source_target_pairs={{0,8},{8,0},{16,24},{24,16},{1,9},{9,1},{17,25},{25,17},{2,10},{10... | collective-permute-start | bytes 2949128 | tf_op jit(solution)/shard_map/ppermute | solution.py:81
  340.1 173.2 %reduce-scatter.7.cloned.1.call-start = ((), (), s32[]{:S(2)}) async-start(), calls=%async_computation.14 | async-start | bytes 10616832 | tf_op jit(solution)/shard_map/reduce_scatter | solution.py:891
  403.5 168.6 %reduce-scatter.9.cloned.1.call-start = ((), (), s32[]{:S(2)}) async-start(), calls=%async_computation.15 | async-start | bytes 5750784 | tf_op jit(solution)/shard_map/reduce_scatter | solution.py:918
  451.9 24.5 %collective-permute-start.33 = (bf16[320,1536]{1,0:T(8,128)(2,1)}, bf16[320,1536]{1,0:T(8,128)(2,1)}, u32[]{:S(2)}, u32[]{:S(2)}) collective-permute-start(bf16[320,1536]{1,0:T(8,128)(2,1)} %pad_maximum_fusion.7), channel_id=1, source_target_pairs={{0,8},{8,0},{16,24},{24,16},{1,9},{9,1},{17,25},{25,17},{2,10},{10... | collective-permute-start | bytes 2949128 | tf_op jit(solution)/shard_map/ppermute | solution.py:81
  519.9 37.9 %collective-permute-start.40 = (bf16[160,1536]{1,0:T(8,128)(2,1)}, bf16[160,1536]{1,0:T(8,128)(2,1)}, u32[]{:S(2)}, u32[]{:S(2)}) collective-permute-start(bf16[160,1536]{1,0:T(8,128)(2,1)} %get-tuple-element.280), channel_id=1, source_target_pairs={{0,8},{8,0},{16,24},{24,16},{1,9},{9,1},{17,25},{25,17},{2,10},{10... | collective-permute-start | bytes 1474568 | tf_op jit(solution)/shard_map/ppermute | solution.py:81
  520.6 37.1 %collective-permute-start.41 = (bf16[160,1536]{1,0:T(8,128)(2,1)}, bf16[160,1536]{1,0:T(8,128)(2,1)S(1)}, u32[]{:S(2)}, u32[]{:S(2)}) collective-permute-start(bf16[160,1536]{1,0:T(8,128)(2,1)} %get-tuple-element.283), channel_id=1, source_target_pairs={{0,8},{8,0},{16,24},{24,16},{1,9},{9,1},{17,25},{25,17},{2,10},{10... | collective-permute-start | bytes 1474568 | tf_op jit(solution)/shard_map/ppermute | solution.py:81
  521.9 35.9 %collective-permute-start.42 = (bf16[160,1536]{1,0:T(8,128)(2,1)S(1)}, bf16[160,1536]{1,0:T(8,128)(2,1)S(1)}, u32[]{:S(2)}, u32[]{:S(2)}) collective-permute-start(bf16[160,1536]{1,0:T(8,128)(2,1)S(1)} %get-tuple-element.282), channel_id=1, source_target_pairs={{0,16},{8,24},{16,0},{24,8},{1,17},{9,25},{17,1},{25,9},{2,18},{10... | collective-permute-start | bytes 1474568 | tf_op jit(solution)/shard_map/ppermute | solution.py:81
  522.5 35.3 %collective-permute-start.43 = (bf16[160,1536]{1,0:T(8,128)(2,1)S(1)}, bf16[160,1536]{1,0:T(8,128)(2,1)}, u32[]{:S(2)}, u32[]{:S(2)}) collective-permute-start(bf16[160,1536]{1,0:T(8,128)(2,1)S(1)} %get-tuple-element.281), channel_id=1, source_target_pairs={{0,16},{8,24},{16,0},{24,8},{1,17},{9,25},{17,1},{25,9},{2,18},{10... | collective-permute-start | bytes 1474568 | tf_op jit(solution)/shard_map/ppermute | solution.py:81
  523.9 33.9 %all-to-all-start.3 = ((bf16[4,48,3072]{2,1,0:T(8,128)(2,1)}), bf16[4,48,3072]{2,1,0:T(8,128)(2,1)S(1)}, u32[]{:S(2)}, u32[]{:S(2)}) async-start(bf16[4,48,3072]{2,1,0:T(8,128)(2,1)} %bitcast.164), calls=%async_computation.5 | async-start | bytes 2359296 | tf_op jit(solution)/shard_map/all_to_all | solution.py:706
  527.5 110.9 %reduce-scatter.11.cloned.1.call-start = ((), (), s32[]{:S(2)}) async-start(), calls=%async_computation.16 | async-start | bytes 5750784 | tf_op jit(solution)/shard_map/reduce_scatter | solution.py:931
  602.0 42.3 %collective-permute-start.48 = (bf16[320,1536]{1,0:T(8,128)(2,1)}, bf16[320,1536]{1,0:T(8,128)(2,1)}, u32[]{:S(2)}, u32[]{:S(2)}) collective-permute-start(bf16[320,1536]{1,0:T(8,128)(2,1)} %pad_maximum_fusion.9), channel_id=1, source_target_pairs={{0,8},{8,0},{16,24},{24,16},{1,9},{9,1},{17,25},{25,17},{2,10},{10... | collective-permute-start | bytes 2949128 | tf_op jit(solution)/shard_map/ppermute | solution.py:81
  605.2 39.1 %collective-permute-start.49 = (bf16[320,1536]{1,0:T(8,128)(2,1)}, bf16[320,1536]{1,0:T(8,128)(2,1)}, u32[]{:S(2)}, u32[]{:S(2)}) collective-permute-start(bf16[320,1536]{1,0:T(8,128)(2,1)} %pad_maximum_fusion.10), channel_id=1, source_target_pairs={{0,16},{8,24},{16,0},{24,8},{1,17},{9,25},{17,1},{25,9},{2,18},{10... | collective-permute-start | bytes 2949128 | tf_op jit(solution)/shard_map/ppermute | solution.py:81
  609.6 26.2 %collective-permute-start.47 = (bf16[160,1536]{1,0:T(8,128)(2,1)S(1)}, bf16[160,1536]{1,0:T(8,128)(2,1)S(1)}, u32[]{:S(2)}, u32[]{:S(2)}) collective-permute-start(bf16[160,1536]{1,0:T(8,128)(2,1)S(1)} %get-tuple-element.279), channel_id=1, source_target_pairs={{0,8},{8,0},{16,24},{24,16},{1,9},{9,1},{17,25},{25,17},{2,10},{10... | collective-permute-start | bytes 1474568 | tf_op jit(solution)/shard_map/ppermute | solution.py:81
  (117 other events, 1039.1 us)
Sparse Core Ops, SparseCore 0:
  21.7 43.0 all-gather.4
  67.0 59.5 all-gather.6
  128.2 50.9 all-gather.10
  181.2 88.2 all-gather.8
  340.3 51.7 reduce-scatter.4
  403.6 98.3 reduce-scatter.6
  513.5 55.7 reduce-scatter.8
  572.2 57.9 reduce-scatter.10

commit v6 on v5

--- a/solution.py
+++ b/solution.py
@@ -809,26 +809,21 @@
     group_tokens, _, ends = gather_rows(after(tokens[0], self_pieces), n)
     group_grad, grad_early, grad_ends = gather_rows(after(grad_output[0], *ends), n)
 
-    self_all = gather_columns(self_pieces, n, nf)
+    first_in = jnp.concatenate([self_pieces.reshape(n * r, -1), rows_to_pieces(out_self, n)], axis=1)
+    first_all = lax.all_gather(first_in, "fsdp", axis=0, tiled=True).reshape(nf, n, r, 4 * wide + LANES)
+    self_all = first_all[..., : 3 * wide + LANES].transpose(1, 0, 2, 3).reshape(D, 3 * wide + LANES)
+    w_out = first_all[..., 3 * wide + LANES :].transpose(0, 2, 1, 3).reshape(nf * r, D)
     w_self = self_all[:, : 3 * wide]
     vectors = self_all[:, 3 * wide : 3 * wide + 12]
     gain_one, gain_two, gain_three, b_down = (vectors[:, j].astype(f32) for j in range(4))
     b_gateup = vectors[:, 4:12].reshape(2 * FF).astype(f32)
     b_gate = lax.dynamic_slice_in_dim(b_gateup, me * hidden, hidden, 0)
     b_upper = lax.dynamic_slice_in_dim(b_gateup, FF + me * hidden, hidden, 0)
-    mid = jnp.concatenate(
-        [
-            mid_pieces.reshape(n * r, 3 * wide),
-            rows_to_pieces(out_self, n),
-            rows_to_pieces(out_cross, n),
-        ],
-        axis=1,
-    )
-    mid = lax.all_gather(mid, "fsdp", axis=0, tiled=True).reshape(nf, n, r, 5 * wide)
+    mid = jnp.concatenate([mid_pieces.reshape(n * r, 3 * wide), rows_to_pieces(out_cross, n)], axis=1)
+    mid = lax.all_gather(mid, "fsdp", axis=0, tiled=True).reshape(nf, n, r, 4 * wide)
     kvq = mid[..., : 3 * wide].transpose(1, 0, 2, 3).reshape(D, 3 * wide)
     w_keyval, w_query = kvq[:, : 2 * wide], kvq[:, 2 * wide :]
-    w_out = mid[..., 3 * wide : 4 * wide].transpose(0, 2, 1, 3).reshape(nf * r, D)
-    w_cross = mid[..., 4 * wide :].transpose(0, 2, 1, 3).reshape(nf * r, D)
+    w_cross = mid[..., 3 * wide :].transpose(0, 2, 1, 3).reshape(nf * r, D)
     group_lengths = lengths[0]
     order = block_ids(n)
     all_rows = (order[:, None] * rows + jnp.arange(rows, dtype=jnp.int32)[None, :]).reshape(group)
@@ -943,7 +938,7 @@
     own_cross = joined(own_mid[:, split:])
     own_out = joined(own_self[:, split:])
     last_part = share(jnp.concatenate([own_mid[:, :split], own_self[:, :split]], axis=1), n)
-    grad_cond = sum_end([after(part, last_part) for part in cond_parts], n)
+    grad_cond = sum_end([after(part, through) for part in cond_parts], n)
     grad_cond = grad_cond.reshape(1, SEQS_GRP, COND, D)
     vectors = jnp.sum(last_part[:, :, 3 * wide : split].astype(f32), axis=0)
     grad_inputs = grad_first + norm_back(through, normal_one, scaled_one, gain_one)[0]

time: 691 us -> 681 us (0.986)
  blocking collectives: 12 us -> 0 us
  local copies, waits for them, and re-layouts: 82.5 us -> 91.4 us
    all_to_all x1 -> x0, blocking collectives: 12 us -> none  [to_seq(): return lax.all_to_all(pieces, 'seq', 0, 0, tiled=True)]
    ppermute x54, waiting for transfers between devices: 188 us -> 180 us  [hop(): return lax.ppermute(value, 'seq', [(i, i ^ j) for i in range(4)])]
    all_to_all x4 -> x5, waiting for transfers between devices: 10.7 us -> 16.6 us  [to_seq(): return lax.all_to_all(pieces, 'seq', 0, 0, tiled=True)]
    unnamed x174 -> x178, local copies, waits for them, and re-layouts: 37.6 us -> 42.9 us
    all_to_all x4 -> x5, starting transfers between devices: 14.3 us -> 18.3 us  [to_seq(): return lax.all_to_all(pieces, 'seq', 0, 0, tiled=True)]
  transfers between devices with their start and end apart: 66 -> 67, of which waited for: 36 -> 31; matrix products, arithmetic and copies ran while one was open for 27% -> 27% of each run, Pallas kernels for 18% -> 17%
where the time goes in v6:
time: 681 us; the launch traced here: 676 us
  waiting for transfers between devices  197 us (29%)
  Pallas kernels  169 us (25%)
  local copies, waits for them, and re-layouts  91.4 us (13%)
  starting transfers between devices  82.2 us (12%)
  other arithmetic  61.7 us (9%)
  matrix products  58.1 us (9%)
  between operations  16 us (2%)
    ppermute x54, waiting for transfers between devices, hop(): return lax.ppermute(value, 'seq', [(i, i ^ j) for i in range(4)])  180 us
    ppermute x54, starting transfers between devices, hop(): return lax.ppermute(value, 'seq', [(i, i ^ j) for i in range(4)])  63.2 us
    pallas_call x1, Pallas kernels, feed(): pl.pallas_call(functools.partial(feed_kernel, chunk), out_shape=[jax.Shap...  47.9 us
    unnamed x178, local copies, waits for them, and re-layouts  42.9 us
    pallas_call x2, Pallas kernels, attend_back(): pl.pallas_call(functools.partial(attend_back_kernel, rope, tile), out_sha...  39.4 us
    dot_general x14, matrix products, dot(): return jnp.dot(left, right, preferred_element_type=f32)  30.7 us
    pallas_call x2, Pallas kernels, attend(): pl.pallas_call(functools.partial(attend_kernel, rope, tile), out_shape=sh...  29.5 us
    dot_general x13, matrix products, back_prod(): lax.dot_general(left, weight, (((1,), (1,)), ((), ())), preferred_element...  27.4 us
  transfers between devices with their start and end apart: 67, of which 31 were waited for; matrix products, arithmetic and copies ran while one was open for 27% of the time, Pallas kernels for 17%

profile of v6, /device:TPU:8, one launch (start us, length us, event | category | flops | bytes accessed | tf_op | source)
XLA Modules:
  0.0 676.0 jit_solution(14598030423565156984)
XLA Ops:
  14.2 7.6 %all-to-all-done = bf16[4,48,1280]{2,1,0:T(8,128)(2,1)S(1)} async-done(((bf16[4,48,1280]{2,1,0:T(8,128)(2,1)}), bf16[4,48,1280]{2,1,0:T(8,128)(2,1)S(1)}, u32[]{:S(2)}, u32[]{:S(2)}) %all-to-all-start) | async-done | bytes 491552 | tf_op jit(solution)/shard_map/all_to_all | solution.py:706
  46.4 15.7 %collective-permute-done.1 = bf16[320,1536]{1,0:T(8,128)(2,1)S(1)} collective-permute-done((bf16[320,1536]{1,0:T(8,128)(2,1)S(1)}, bf16[320,1536]{1,0:T(8,128)(2,1)S(1)}, u32[]{:S(2)}, u32[]{:S(2)}) %collective-permute-start.1) | collective-permute-done | bytes 983072 | tf_op jit(solution)/shard_map/ppermute | solution.py:81
  65.5 7.4 %collective-permute-done.2 = bf16[160,1536]{1,0:T(8,128)(2,1)S(1)} collective-permute-done((bf16[160,1536]{1,0:T(8,128)(2,1)S(1)}, bf16[160,1536]{1,0:T(8,128)(2,1)S(1)}, u32[]{:S(2)}, u32[]{:S(2)}) %collective-permute-start.2) | collective-permute-done | bytes 491552 | tf_op jit(solution)/shard_map/ppermute | solution.py:81
  87.0 7.0 %fusion.31.refs_0_.refs_1_.refs_2_ = f32[1280,1152]{1,0:T(8,128)} fusion(bf16[1280,1536]{1,0:T(8,128)(2,1)S(1)} %fusion.4.h_ref, bf16[1536,1280]{1,0:T(8,128)(2,1)S(1)} %bitcast.112), kind=kOutput, calls=%fused_computation.72 | convolution fusion | flops 4529848320 | bytes 13369344 | tf_op jit(solution)/shard_map/dot_general | solution.py:63
  103.3 21.5 %attend_self.1 = (bf16[1280,384]{1,0:T(8,128)(2,1)}, bf16[1280,384]{1,0:T(8,128)(2,1)}, bf16[1280,384]{1,0:T(8,128)(2,1)}, bf16[1280,384]{1,0:T(8,128)(2,1)}, f32[3,8,1280]{2,1,0:T(8,128)}) custom-call(f32[1280,1152]{1,0:T(8,128)} %fusion.31.refs_0_.refs_1_.refs_2_, f32[1280,1152]{1,0:T(8,128)} %fusion.31.refs_0_.refs_1_.refs_2_, ...), custom_call_target="tpu_custom_call" | custom-call | flops 5033164800 | bytes 11796480 | tf_op jit(solution)/shard_map/attend_self/pallas_call | solution.py:336
  133.2 6.7 collective-permute-done.8
  148.8 13.8 %collective-permute-done.9 = bf16[320,1536]{1,0:T(8,128)(2,1)S(1)} collective-permute-done((bf16[320,1536]{1,0:T(8,128)(2,1)}, bf16[320,1536]{1,0:T(8,128)(2,1)S(1)}, u32[]{:S(2)}, u32[]{:S(2)}) %collective-permute-start.9) | collective-permute-done | bytes 983072 | tf_op jit(solution)/shard_map/ppermute | solution.py:81
  177.6 12.0 %collective-permute-done.13 = bf16[320,1536]{1,0:T(8,128)(2,1)} collective-permute-done((bf16[320,1536]{1,0:T(8,128)(2,1)}, bf16[320,1536]{1,0:T(8,128)(2,1)}, u32[]{:S(2)}, u32[]{:S(2)}) %collective-permute-start.13) | collective-permute-done | bytes 983072 | tf_op jit(solution)/shard_map/ppermute | solution.py:81
  207.3 7.9 %attend_cross.1 = (bf16[1280,384]{1,0:T(8,128)(2,1)}, f32[3,8,1280]{2,1,0:T(8,128)}) custom-call(bf16[1280,384]{1,0:T(8,128)(2,1)} %convolution_convert_fusion.3.refs_0_, bf16[272,768]{1,0:T(8,128)(2,1)} %pad.21.refs_1_.refs_2_, bf16[272,768]{1,0:T(8,128)(2,1)} %pad.21.refs_1_.refs_2_, s32[1,1280]{1,0:T(1,128)} %broadcast_in_dim.36.refs_5_.refs_3_.refs_6_.refs_8_, ...), custom_call_target="tpu_custom_call" | custom-call | flops 1069547520 | bytes 7151616 | tf_op jit(solution)/shard_map/attend_cross/pallas_call | solution.py:336
  227.1 6.6 collective-permute-done.18
  236.1 13.1 %collective-permute-done.17 = bf16[320,1536]{1,0:T(8,128)(2,1)S(1)} collective-permute-done((bf16[320,1536]{1,0:T(8,128)(2,1)S(1)}, bf16[320,1536]{1,0:T(8,128)(2,1)S(1)}, u32[]{:S(2)}, u32[]{:S(2)}) %collective-permute-start.17) | collective-permute-done | bytes 983072 | tf_op jit(solution)/shard_map/ppermute | solution.py:81
  259.7 10.6 %collective-permute-done.21 = bf16[320,1536]{1,0:T(8,128)(2,1)} collective-permute-done((bf16[320,1536]{1,0:T(8,128)(2,1)}, bf16[320,1536]{1,0:T(8,128)(2,1)}, u32[]{:S(2)}, u32[]{:S(2)}) %collective-permute-start.21) | collective-permute-done | bytes 983072 | tf_op jit(solution)/shard_map/ppermute | solution.py:81
  284.5 47.9 %feed.1 = (bf16[1280,1536]{1,0:T(8,128)(2,1)}, bf16[1280,1536]{1,0:T(8,128)(2,1)}, bf16[1280,1536]{1,0:T(8,128)(2,1)}, f32[1,1536]{1,0:T(1,128)}, f32[1,1536]{1,...) custom-call(bf16[1280,1536]{1,0:T(8,128)(2,1)} %constant_dynamic-update-slice_fusion.10.refs_0_.h_ref, ...), custom_call_target="tpu_custom_call" | custom-call | flops 36238786560 | bytes 42467328 | tf_op jit(solution)/shard_map/feed/pallas_call | solution.py:465
  336.0 9.2 %collective-permute-done.24 = bf16[160,1536]{1,0:T(8,128)(2,1)S(1)} collective-permute-done((bf16[160,1536]{1,0:T(8,128)(2,1)S(1)}, bf16[160,1536]{1,0:T(8,128)(2,1)S(1)}, u32[]{:S(2)}, u32[]{:S(2)}) %collective-permute-start.24) | collective-permute-done | bytes 491552 | tf_op jit(solution)/shard_map/ppermute | solution.py:81
  352.0 19.0 %gateup_grads.1 = bf16[8,4,48,3072]{3,2,1,0:T(8,128)(2,1)} custom-call(bf16[1280,1536]{1,0:T(8,128)(2,1)} %constant_dynamic-update-slice_fusion.10.refs_0_.h_ref, bf16[1280,1536]{1,0:T(8,128)(2,1)} %get-tuple-element.94.dg_ref, bf16[1280,1536]{1,0:T(8,128)(2,1)} %get-tuple-element.95.du_ref), custom_call_target="tpu_custom_call" | custom-call | flops 12079595520 | bytes 21233664 | tf_op jit(solution)/shard_map/gateup_grads/pallas_call | solution.py:535
  385.1 11.1 %collective-permute-done.28 = bf16[320,1536]{1,0:T(8,128)(2,1)} collective-permute-done((bf16[320,1536]{1,0:T(8,128)(2,1)S(1)}, bf16[320,1536]{1,0:T(8,128)(2,1)}, u32[]{:S(2)}, u32[]{:S(2)}) %collective-permute-start.28) | collective-permute-done | bytes 983072 | tf_op jit(solution)/shard_map/ppermute | solution.py:81
  420.5 10.1 %back_cross.1 = (bf16[1280,384]{1,0:T(8,128)(2,1)}, bf16[272,384]{1,0:T(8,128)(2,1)}, bf16[272,384]{1,0:T(8,128)(2,1)}) custom-call(bf16[1280,384]{1,0:T(8,128)(2,1)} %convolution_convert_fusion.3.refs_0_, bf16[272,768]{1,0:T(8,128)(2,1)} %pad.21.refs_1_.refs_2_, bf16[272,768]{1,0:T(8,128)(2,1)} %pad.21.refs_1_.refs_2_, ...), custom_call_target="tpu_custom_call" | custom-call | flops 2673868800 | bytes 7151616 | tf_op jit(solution)/shard_map/back_cross/pallas_call | solution.py:371
  437.6 8.7 %collective-permute-done.32 = bf16[160,1536]{1,0:T(8,128)(2,1)S(1)} collective-permute-done((bf16[160,1536]{1,0:T(8,128)(2,1)S(1)}, bf16[160,1536]{1,0:T(8,128)(2,1)S(1)}, u32[]{:S(2)}, u32[]{:S(2)}) %collective-permute-start.32) | collective-permute-done | bytes 491552 | tf_op jit(solution)/shard_map/ppermute | solution.py:81
  461.5 10.5 %mid_grads.1 = bf16[8,4,48,1664]{3,2,1,0:T(8,128)(2,1)} custom-call(bf16[272,1536]{1,0:T(8,128)(2,1)} %pad.22.cond_ref, bf16[272,384]{1,0:T(8,128)(2,1)} %get-tuple-element.99.dk_ref, bf16[272,384]{1,0:T(8,128)(2,1)} %get-tuple-element.100.dv_ref, bf16[1280,1536]{1,0:T(8,128)(2,1)} %copy-done.23, bf16[1280,384]{1,0:T(8,128)(2,1)} %get-tuple-element.98.dq_ref, ...), custom_call_target="tpu_custom_call" | custom-call | flops 3661627392 | bytes 13811712 | tf_op jit(solution)/shard_map/mid_grads/pallas_call | solution.py:585
  481.7 10.8 %convolution_convert_fusion = bf16[1280,1536]{1,0:T(8,128)(2,1)} fusion(bf16[1280,1536]{1,0:T(8,128)(2,1)} %get-tuple-element.104, bf16[1536,1536]{1,0:T(8,128)(2,1)} %all-gather.11.cloned.1.call-done.refs_4_), kind=kOutput, calls=%fused_computation.7 | convolution fusion | flops 6041763840 | bytes 12582912 | tf_op jit(solution)/shard_map/dot_general | solution.py:63
  520.5 29.3 %back_self.1 = (bf16[1280,384]{1,0:T(8,128)(2,1)}, bf16[1280,384]{1,0:T(8,128)(2,1)}, bf16[1280,384]{1,0:T(8,128)(2,1)}) custom-call(bf16[1280,384]{1,0:T(8,128)(2,1)} %get-tuple-element.109.refs_0_, bf16[1280,384]{1,0:T(8,128)(2,1)} %get-tuple-element.110.refs_1_, bf16[1280,384]{1,0:T(8,128)(2,1)} %get-tuple-element.111.refs_2_, ...), custom_call_target="tpu_custom_call" | custom-call | flops 12582912000 | bytes 11796480 | tf_op jit(solution)/shard_map/back_self/pallas_call | solution.py:371
  550.8 14.2 %self_grads.1 = bf16[8,4,48,1664]{3,2,1,0:T(8,128)(2,1)} custom-call(bf16[1280,1536]{1,0:T(8,128)(2,1)} %copy-done.14, bf16[1280,384]{1,0:T(8,128)(2,1)} %get-tuple-element.124.dq_ref, bf16[1280,384]{1,0:T(8,128)(2,1)} %get-tuple-element.125.dk_ref, bf16[1280,384]{1,0:T(8,128)(2,1)} %get-tuple-element.126.dv_ref, bf16[1536,1280]{1,0:T(8,128)(2,1)} %bitcast.114, ...), custom_call_target="tpu_custom_call" | custom-call | flops 6039797760 | bytes 12582912 | tf_op jit(solution)/shard_map/self_grads/pallas_call | solution.py:643
  606.5 10.3 %collective-permute-done.46 = bf16[160,1536]{1,0:T(8,128)(2,1)S(1)} collective-permute-done((bf16[160,1536]{1,0:T(8,128)(2,1)S(1)}, bf16[160,1536]{1,0:T(8,128)(2,1)S(1)}, u32[]{:S(2)}, u32[]{:S(2)}) %collective-permute-start.46) | collective-permute-done | bytes 491552 | tf_op jit(solution)/shard_map/ppermute | solution.py:81
  617.9 15.2 %collective-permute-done.47 = bf16[160,1536]{1,0:T(8,128)(2,1)S(1)} collective-permute-done((bf16[160,1536]{1,0:T(8,128)(2,1)S(1)}, bf16[160,1536]{1,0:T(8,128)(2,1)S(1)}, u32[]{:S(2)}, u32[]{:S(2)}) %collective-permute-start.47) | collective-permute-done | bytes 491552 | tf_op jit(solution)/shard_map/ppermute | solution.py:81
  (510 shorter events, 333.7 us)
Async XLA Ops:
  14.1 65.4 %all-gather.5.cloned.1.call-start = ((), (), s32[]{:S(2)}) async-start(), calls=%async_computation.9 | async-start | bytes 5750784 | tf_op jit(solution)/shard_map/all_gather | solution.py:813
  27.9 142.5 %all-gather.7.cloned.1.call-start = ((), (), s32[]{:S(2)}) async-start(), calls=%async_computation.10 | async-start | bytes 5308416 | tf_op jit(solution)/shard_map/all_gather | solution.py:823
  34.9 249.6 %all-gather.11.cloned.1.call-start = ((), (), s32[]{:S(2)}) async-start(), calls=%async_computation.12 | async-start | bytes 5308416 | tf_op jit(solution)/shard_map/all_gather | solution.py:845
  39.8 23.4 %collective-permute-start = (bf16[320,1536]{1,0:T(8,128)(2,1)S(1)}, bf16[320,1536]{1,0:T(8,128)(2,1)S(1)}, u32[]{:S(2)}, u32[]{:S(2)}) collective-permute-start(bf16[320,1536]{1,0:T(8,128)(2,1)S(1)} %bitcast.133), channel_id=1, source_target_pairs={{0,8},{8,0},{16,24},{24,16},{1,9},{9,1},{17,25},{25,17},{2,10},{10... | collective-permute-start | bytes 2949128 | tf_op jit(solution)/shard_map/ppermute | solution.py:81
  94.1 32.2 %all-to-all-start.2 = ((bf16[4,48,3072]{2,1,0:T(8,128)(2,1)}), bf16[4,48,3072]{2,1,0:T(8,128)(2,1)S(1)}, u32[]{:S(2)}, u32[]{:S(2)}) async-start(bf16[4,48,3072]{2,1,0:T(8,128)(2,1)} %reshape.403), calls=%async_computation.2 | async-start | bytes 2359296 | tf_op jit(solution)/shard_map/all_to_all | solution.py:706
  97.7 186.8 %all-gather.9.cloned.1.call-start = ((), (), s32[]{:S(2)}) async-start(), calls=%async_computation.11 | async-start | bytes 10616832 | tf_op jit(solution)/shard_map/all_gather | solution.py:849
  98.0 26.8 %collective-permute-start.6 = (bf16[160,1536]{1,0:T(8,128)(2,1)S(1)}, bf16[160,1536]{1,0:T(8,128)(2,1)S(1)}, u32[]{:S(2)}, u32[]{:S(2)}) collective-permute-start(bf16[160,1536]{1,0:T(8,128)(2,1)S(1)} %slice.393), channel_id=1, source_target_pairs={{0,8},{8,0},{16,24},{24,16},{1,9},{9,1},{17,25},{25,17},{2,10},{10... | collective-permute-start | bytes 1474568 | tf_op jit(solution)/shard_map/ppermute | solution.py:81
  100.0 24.7 %collective-permute-start.7 = (bf16[160,1536]{1,0:T(8,128)(2,1)S(1)}, bf16[160,1536]{1,0:T(8,128)(2,1)S(1)}, u32[]{:S(2)}, u32[]{:S(2)}) collective-permute-start(bf16[160,1536]{1,0:T(8,128)(2,1)S(1)} %slice.394), channel_id=1, source_target_pairs={{0,16},{8,24},{16,0},{24,8},{1,17},{9,25},{17,1},{25,9},{2,18},{10... | collective-permute-start | bytes 1474568 | tf_op jit(solution)/shard_map/ppermute | solution.py:81
  127.4 270.6 %reduce-scatter.5.cloned.1.call-start = ((), (), s32[]{:S(2)}) async-start(), calls=%async_computation.13 | async-start | bytes 5308416 | tf_op jit(solution)/shard_map/reduce_scatter | solution.py:878
  168.4 23.8 %collective-permute-start.12 = (bf16[320,1536]{1,0:T(8,128)(2,1)}, bf16[320,1536]{1,0:T(8,128)(2,1)}, u32[]{:S(2)}, u32[]{:S(2)}) collective-permute-start(bf16[320,1536]{1,0:T(8,128)(2,1)} %get-tuple-element.275), channel_id=1, source_target_pairs={{0,8},{8,0},{16,24},{24,16},{1,9},{9,1},{17,25},{25,17},{2,10},{10... | collective-permute-start | bytes 2949128 | tf_op jit(solution)/shard_map/ppermute | solution.py:81
  226.6 22.5 %collective-permute-start.17 = (bf16[320,1536]{1,0:T(8,128)(2,1)S(1)}, bf16[320,1536]{1,0:T(8,128)(2,1)S(1)}, u32[]{:S(2)}, u32[]{:S(2)}) collective-permute-start(bf16[320,1536]{1,0:T(8,128)(2,1)S(1)} %pad_maximum_fusion.3), channel_id=1, source_target_pairs={{0,8},{8,0},{16,24},{24,16},{1,9},{9,1},{17,25},{25,17},{2,10},{10... | collective-permute-start | bytes 2949128 | tf_op jit(solution)/shard_map/ppermute | solution.py:81
  332.4 173.8 %reduce-scatter.7.cloned.1.call-start = ((), (), s32[]{:S(2)}) async-start(), calls=%async_computation.14 | async-start | bytes 10616832 | tf_op jit(solution)/shard_map/reduce_scatter | solution.py:886
  398.0 167.1 %reduce-scatter.9.cloned.1.call-start = ((), (), s32[]{:S(2)}) async-start(), calls=%async_computation.15 | async-start | bytes 5750784 | tf_op jit(solution)/shard_map/reduce_scatter | solution.py:913
  447.4 24.6 %collective-permute-start.33 = (bf16[320,1536]{1,0:T(8,128)(2,1)}, bf16[320,1536]{1,0:T(8,128)(2,1)}, u32[]{:S(2)}, u32[]{:S(2)}) collective-permute-start(bf16[320,1536]{1,0:T(8,128)(2,1)} %pad_maximum_fusion.7), channel_id=1, source_target_pairs={{0,8},{8,0},{16,24},{24,16},{1,9},{9,1},{17,25},{25,17},{2,10},{10... | collective-permute-start | bytes 2949128 | tf_op jit(solution)/shard_map/ppermute | solution.py:81
  449.7 22.3 %collective-permute-start.35 = (bf16[320,1536]{1,0:T(8,128)(2,1)}, bf16[320,1536]{1,0:T(8,128)(2,1)}, u32[]{:S(2)}, u32[]{:S(2)}) collective-permute-start(bf16[320,1536]{1,0:T(8,128)(2,1)} %pad_maximum_fusion.8), channel_id=1, source_target_pairs={{0,16},{8,24},{16,0},{24,8},{1,17},{9,25},{17,1},{25,9},{2,18},{10... | collective-permute-start | bytes 2949128 | tf_op jit(solution)/shard_map/ppermute | solution.py:81
  512.9 37.9 %collective-permute-start.40 = (bf16[160,1536]{1,0:T(8,128)(2,1)}, bf16[160,1536]{1,0:T(8,128)(2,1)}, u32[]{:S(2)}, u32[]{:S(2)}) collective-permute-start(bf16[160,1536]{1,0:T(8,128)(2,1)} %get-tuple-element.278), channel_id=1, source_target_pairs={{0,8},{8,0},{16,24},{24,16},{1,9},{9,1},{17,25},{25,17},{2,10},{10... | collective-permute-start | bytes 1474568 | tf_op jit(solution)/shard_map/ppermute | solution.py:81
  513.7 37.0 %collective-permute-start.41 = (bf16[160,1536]{1,0:T(8,128)(2,1)}, bf16[160,1536]{1,0:T(8,128)(2,1)S(1)}, u32[]{:S(2)}, u32[]{:S(2)}) collective-permute-start(bf16[160,1536]{1,0:T(8,128)(2,1)} %get-tuple-element.281), channel_id=1, source_target_pairs={{0,8},{8,0},{16,24},{24,16},{1,9},{9,1},{17,25},{25,17},{2,10},{10... | collective-permute-start | bytes 1474568 | tf_op jit(solution)/shard_map/ppermute | solution.py:81
  514.9 35.8 %collective-permute-start.42 = (bf16[160,1536]{1,0:T(8,128)(2,1)S(1)}, bf16[160,1536]{1,0:T(8,128)(2,1)S(1)}, u32[]{:S(2)}, u32[]{:S(2)}) collective-permute-start(bf16[160,1536]{1,0:T(8,128)(2,1)S(1)} %get-tuple-element.280), channel_id=1, source_target_pairs={{0,16},{8,24},{16,0},{24,8},{1,17},{9,25},{17,1},{25,9},{2,18},{10... | collective-permute-start | bytes 1474568 | tf_op jit(solution)/shard_map/ppermute | solution.py:81
  516.2 34.5 %collective-permute-start.43 = (bf16[160,1536]{1,0:T(8,128)(2,1)S(1)}, bf16[160,1536]{1,0:T(8,128)(2,1)}, u32[]{:S(2)}, u32[]{:S(2)}) collective-permute-start(bf16[160,1536]{1,0:T(8,128)(2,1)S(1)} %get-tuple-element.279), channel_id=1, source_target_pairs={{0,16},{8,24},{16,0},{24,8},{1,17},{9,25},{17,1},{25,9},{2,18},{10... | collective-permute-start | bytes 1474568 | tf_op jit(solution)/shard_map/ppermute | solution.py:81
  516.9 33.8 %all-to-all-start.3 = ((bf16[4,48,3072]{2,1,0:T(8,128)(2,1)}), bf16[4,48,3072]{2,1,0:T(8,128)(2,1)S(1)}, u32[]{:S(2)}, u32[]{:S(2)}) async-start(bf16[4,48,3072]{2,1,0:T(8,128)(2,1)} %bitcast.165), calls=%async_computation.5 | async-start | bytes 2359296 | tf_op jit(solution)/shard_map/all_to_all | solution.py:706
  520.5 123.3 %reduce-scatter.11.cloned.1.call-start = ((), (), s32[]{:S(2)}) async-start(), calls=%async_computation.16 | async-start | bytes 5750784 | tf_op jit(solution)/shard_map/reduce_scatter | solution.py:926
  596.3 39.6 %collective-permute-start.48 = (bf16[320,1536]{1,0:T(8,128)(2,1)S(1)}, bf16[320,1536]{1,0:T(8,128)(2,1)S(1)}, u32[]{:S(2)}, u32[]{:S(2)}) collective-permute-start(bf16[320,1536]{1,0:T(8,128)(2,1)S(1)} %pad_maximum_fusion.9), channel_id=1, source_target_pairs={{0,8},{8,0},{16,24},{24,16},{1,9},{9,1},{17,25},{25,17},{2,10},{10... | collective-permute-start | bytes 2949128 | tf_op jit(solution)/shard_map/ppermute | solution.py:81
  598.6 37.3 %collective-permute-start.49 = (bf16[320,1536]{1,0:T(8,128)(2,1)S(1)}, bf16[320,1536]{1,0:T(8,128)(2,1)S(1)}, u32[]{:S(2)}, u32[]{:S(2)}) collective-permute-start(bf16[320,1536]{1,0:T(8,128)(2,1)S(1)} %pad_maximum_fusion.10), channel_id=1, source_target_pairs={{0,16},{8,24},{16,0},{24,8},{1,17},{9,25},{17,1},{25,9},{2,18},{10... | collective-permute-start | bytes 2949128 | tf_op jit(solution)/shard_map/ppermute | solution.py:81
  604.8 28.4 %collective-permute-start.47 = (bf16[160,1536]{1,0:T(8,128)(2,1)S(1)}, bf16[160,1536]{1,0:T(8,128)(2,1)S(1)}, u32[]{:S(2)}, u32[]{:S(2)}) collective-permute-start(bf16[160,1536]{1,0:T(8,128)(2,1)S(1)} %get-tuple-element.277), channel_id=1, source_target_pairs={{0,8},{8,0},{16,24},{24,16},{1,9},{9,1},{17,25},{25,17},{2,10},{10... | collective-permute-start | bytes 1474568 | tf_op jit(solution)/shard_map/ppermute | solution.py:81
  (120 other events, 1059.7 us)
Sparse Core Ops, SparseCore 0:
  22.8 53.4 all-gather.4
  78.5 50.6 all-gather.6
  130.9 50.5 all-gather.10
  183.5 88.2 all-gather.8
  332.6 52.3 reduce-scatter.4
  398.1 98.8 reduce-scatter.6
  506.4 57.8 reduce-scatter.8
  566.8 57.1 reduce-scatter.10

commit v7 on v6

--- a/solution.py
+++ b/solution.py
@@ -926,7 +926,7 @@
     own_self = lax.psum_scatter(after(grad_w_self, own_mid), "fsdp", scatter_dimension=0, tiled=True)
     grad_packed = jnp.concatenate([dq, dk, dv], axis=1)
     through, early = scattered(lambda *at: back_prod(block(grad_packed, *at), w_self))
-    down_pieces = [after(piece, *early) for piece in down_pieces]
+    down_pieces = [after(piece, through) for piece in down_pieces]
     result = second + scatter_end(down, down_pieces, n) + b_down
     cond_parts = sum_start(after(cond_part, *early), n)
     own_gateup = after(own_gateup, *early)
@@ -938,7 +938,7 @@
     own_cross = joined(own_mid[:, split:])
     own_out = joined(own_self[:, split:])
     last_part = share(jnp.concatenate([own_mid[:, :split], own_self[:, :split]], axis=1), n)
-    grad_cond = sum_end([after(part, through) for part in cond_parts], n)
+    grad_cond = sum_end([after(part, last_part) for part in cond_parts], n)
     grad_cond = grad_cond.reshape(1, SEQS_GRP, COND, D)
     vectors = jnp.sum(last_part[:, :, 3 * wide : split].astype(f32), axis=0)
     grad_inputs = grad_first + norm_back(through, normal_one, scaled_one, gain_one)[0]

time: 681 us -> 680 us (level)
  other arithmetic: 61.7 us -> 68.9 us
    ppermute x54, waiting for transfers between devices: 180 us -> 173 us  [hop(): return lax.ppermute(value, 'seq', [(i, i ^ j) for i in range(4)])]
    unnamed x178 -> x174, local copies, waits for them, and re-layouts: 42.9 us -> 39.5 us
  transfers between devices with their start and end apart: 67 -> 67, of which waited for: 31 -> 33; matrix products, arithmetic and copies ran while one was open for 27% -> 28% of each run, Pallas kernels for 17% -> 18%
where the time goes in v7:
time: 680 us; the launch traced here: 675 us
  waiting for transfers between devices  192 us (28%)
  Pallas kernels  169 us (25%)
  local copies, waits for them, and re-layouts  87.4 us (13%)
  starting transfers between devices  83 us (12%)
  other arithmetic  68.9 us (10%)
  matrix products  58.2 us (9%)
  between operations  16 us (2%)
    ppermute x54, waiting for transfers between devices, hop(): return lax.ppermute(value, 'seq', [(i, i ^ j) for i in range(4)])  173 us
    ppermute x54, starting transfers between devices, hop(): return lax.ppermute(value, 'seq', [(i, i ^ j) for i in range(4)])  64 us
    pallas_call x1, Pallas kernels, feed(): pl.pallas_call(functools.partial(feed_kernel, chunk), out_shape=[jax.Shap...  47.9 us
    unnamed x174, local copies, waits for them, and re-layouts  39.5 us
    pallas_call x2, Pallas kernels, attend_back(): pl.pallas_call(functools.partial(attend_back_kernel, rope, tile), out_sha...  39.3 us
    dot_general x14, matrix products, dot(): return jnp.dot(left, right, preferred_element_type=f32)  30.8 us
    pallas_call x2, Pallas kernels, attend(): pl.pallas_call(functools.partial(attend_kernel, rope, tile), out_shape=sh...  29.6 us
    dot_general x13, matrix products, back_prod(): lax.dot_general(left, weight, (((1,), (1,)), ((), ())), preferred_element...  27.4 us
  transfers between devices with their start and end apart: 67, of which 33 were waited for; matrix products, arithmetic and copies ran while one was open for 28% of the time, Pallas kernels for 18%

profile of v7, /device:TPU:8, one launch (start us, length us, event | category | flops | bytes accessed | tf_op | source)
XLA Modules:
  0.0 675.0 jit_solution(16857136889782537678)
XLA Ops:
  14.2 7.6 %all-to-all-done = bf16[4,48,1280]{2,1,0:T(8,128)(2,1)S(1)} async-done(((bf16[4,48,1280]{2,1,0:T(8,128)(2,1)}), bf16[4,48,1280]{2,1,0:T(8,128)(2,1)S(1)}, u32[]{:S(2)}, u32[]{:S(2)}) %all-to-all-start) | async-done | bytes 491552 | tf_op jit(solution)/shard_map/all_to_all | solution.py:706
  28.0 6.1 all-to-all-done.1
  46.4 15.7 %collective-permute-done.1 = bf16[320,1536]{1,0:T(8,128)(2,1)S(1)} collective-permute-done((bf16[320,1536]{1,0:T(8,128)(2,1)S(1)}, bf16[320,1536]{1,0:T(8,128)(2,1)S(1)}, u32[]{:S(2)}, u32[]{:S(2)}) %collective-permute-start.1) | collective-permute-done | bytes 983072 | tf_op jit(solution)/shard_map/ppermute | solution.py:81
  65.5 7.4 %collective-permute-done.2 = bf16[160,1536]{1,0:T(8,128)(2,1)S(1)} collective-permute-done((bf16[160,1536]{1,0:T(8,128)(2,1)S(1)}, bf16[160,1536]{1,0:T(8,128)(2,1)S(1)}, u32[]{:S(2)}, u32[]{:S(2)}) %collective-permute-start.2) | collective-permute-done | bytes 491552 | tf_op jit(solution)/shard_map/ppermute | solution.py:81
  87.0 7.0 %fusion.31.refs_0_.refs_1_.refs_2_ = f32[1280,1152]{1,0:T(8,128)} fusion(bf16[1280,1536]{1,0:T(8,128)(2,1)S(1)} %fusion.4.h_ref, bf16[1536,1280]{1,0:T(8,128)(2,1)S(1)} %bitcast.112), kind=kOutput, calls=%fused_computation.72 | convolution fusion | flops 4529848320 | bytes 13369344 | tf_op jit(solution)/shard_map/dot_general | solution.py:63
  103.3 21.6 %attend_self.1 = (bf16[1280,384]{1,0:T(8,128)(2,1)}, bf16[1280,384]{1,0:T(8,128)(2,1)}, bf16[1280,384]{1,0:T(8,128)(2,1)}, bf16[1280,384]{1,0:T(8,128)(2,1)}, f32[3,8,1280]{2,1,0:T(8,128)}) custom-call(f32[1280,1152]{1,0:T(8,128)} %fusion.31.refs_0_.refs_1_.refs_2_, f32[1280,1152]{1,0:T(8,128)} %fusion.31.refs_0_.refs_1_.refs_2_, ...), custom_call_target="tpu_custom_call" | custom-call | flops 5033164800 | bytes 11796480 | tf_op jit(solution)/shard_map/attend_self/pallas_call | solution.py:336
  133.3 6.7 collective-permute-done.8
  149.0 13.7 %collective-permute-done.9 = bf16[320,1536]{1,0:T(8,128)(2,1)S(1)} collective-permute-done((bf16[320,1536]{1,0:T(8,128)(2,1)}, bf16[320,1536]{1,0:T(8,128)(2,1)S(1)}, u32[]{:S(2)}, u32[]{:S(2)}) %collective-permute-start.9) | collective-permute-done | bytes 983072 | tf_op jit(solution)/shard_map/ppermute | solution.py:81
  177.6 12.0 %collective-permute-done.13 = bf16[320,1536]{1,0:T(8,128)(2,1)} collective-permute-done((bf16[320,1536]{1,0:T(8,128)(2,1)}, bf16[320,1536]{1,0:T(8,128)(2,1)}, u32[]{:S(2)}, u32[]{:S(2)}) %collective-permute-start.13) | collective-permute-done | bytes 983072 | tf_op jit(solution)/shard_map/ppermute | solution.py:81
  207.3 7.9 %attend_cross.1 = (bf16[1280,384]{1,0:T(8,128)(2,1)}, f32[3,8,1280]{2,1,0:T(8,128)}) custom-call(bf16[1280,384]{1,0:T(8,128)(2,1)} %convolution_convert_fusion.3.refs_0_, bf16[272,768]{1,0:T(8,128)(2,1)} %pad.21.refs_1_.refs_2_, bf16[272,768]{1,0:T(8,128)(2,1)} %pad.21.refs_1_.refs_2_, s32[1,1280]{1,0:T(1,128)} %broadcast_in_dim.36.refs_5_.refs_3_.refs_6_.refs_8_, ...), custom_call_target="tpu_custom_call" | custom-call | flops 1069547520 | bytes 7151616 | tf_op jit(solution)/shard_map/attend_cross/pallas_call | solution.py:336
  227.2 6.5 collective-permute-done.18
  236.1 13.1 %collective-permute-done.17 = bf16[320,1536]{1,0:T(8,128)(2,1)S(1)} collective-permute-done((bf16[320,1536]{1,0:T(8,128)(2,1)S(1)}, bf16[320,1536]{1,0:T(8,128)(2,1)S(1)}, u32[]{:S(2)}, u32[]{:S(2)}) %collective-permute-start.17) | collective-permute-done | bytes 983072 | tf_op jit(solution)/shard_map/ppermute | solution.py:81
  259.7 10.6 %collective-permute-done.21 = bf16[320,1536]{1,0:T(8,128)(2,1)} collective-permute-done((bf16[320,1536]{1,0:T(8,128)(2,1)}, bf16[320,1536]{1,0:T(8,128)(2,1)}, u32[]{:S(2)}, u32[]{:S(2)}) %collective-permute-start.21) | collective-permute-done | bytes 983072 | tf_op jit(solution)/shard_map/ppermute | solution.py:81
  284.4 47.9 %feed.1 = (bf16[1280,1536]{1,0:T(8,128)(2,1)}, bf16[1280,1536]{1,0:T(8,128)(2,1)}, bf16[1280,1536]{1,0:T(8,128)(2,1)}, f32[1,1536]{1,0:T(1,128)}, f32[1,1536]{1,...) custom-call(bf16[1280,1536]{1,0:T(8,128)(2,1)} %constant_dynamic-update-slice_fusion.10.refs_0_.h_ref, ...), custom_call_target="tpu_custom_call" | custom-call | flops 36238786560 | bytes 42467328 | tf_op jit(solution)/shard_map/feed/pallas_call | solution.py:465
  335.9 9.2 %collective-permute-done.24 = bf16[160,1536]{1,0:T(8,128)(2,1)S(1)} collective-permute-done((bf16[160,1536]{1,0:T(8,128)(2,1)S(1)}, bf16[160,1536]{1,0:T(8,128)(2,1)S(1)}, u32[]{:S(2)}, u32[]{:S(2)}) %collective-permute-start.24) | collective-permute-done | bytes 491552 | tf_op jit(solution)/shard_map/ppermute | solution.py:81
  351.9 19.0 %gateup_grads.1 = bf16[8,4,48,3072]{3,2,1,0:T(8,128)(2,1)} custom-call(bf16[1280,1536]{1,0:T(8,128)(2,1)} %constant_dynamic-update-slice_fusion.10.refs_0_.h_ref, bf16[1280,1536]{1,0:T(8,128)(2,1)} %get-tuple-element.94.dg_ref, bf16[1280,1536]{1,0:T(8,128)(2,1)} %get-tuple-element.95.du_ref), custom_call_target="tpu_custom_call" | custom-call | flops 12079595520 | bytes 21233664 | tf_op jit(solution)/shard_map/gateup_grads/pallas_call | solution.py:535
  384.9 10.5 %collective-permute-done.28 = bf16[320,1536]{1,0:T(8,128)(2,1)} collective-permute-done((bf16[320,1536]{1,0:T(8,128)(2,1)S(1)}, bf16[320,1536]{1,0:T(8,128)(2,1)}, u32[]{:S(2)}, u32[]{:S(2)}) %collective-permute-start.28) | collective-permute-done | bytes 983072 | tf_op jit(solution)/shard_map/ppermute | solution.py:81
  419.3 10.1 %back_cross.1 = (bf16[1280,384]{1,0:T(8,128)(2,1)}, bf16[272,384]{1,0:T(8,128)(2,1)}, bf16[272,384]{1,0:T(8,128)(2,1)}) custom-call(bf16[1280,384]{1,0:T(8,128)(2,1)} %convolution_convert_fusion.3.refs_0_, bf16[272,768]{1,0:T(8,128)(2,1)} %pad.21.refs_1_.refs_2_, bf16[272,768]{1,0:T(8,128)(2,1)} %pad.21.refs_1_.refs_2_, ...), custom_call_target="tpu_custom_call" | custom-call | flops 2673868800 | bytes 7151616 | tf_op jit(solution)/shard_map/back_cross/pallas_call | solution.py:371
  436.4 8.2 %collective-permute-done.32 = bf16[160,1536]{1,0:T(8,128)(2,1)S(1)} collective-permute-done((bf16[160,1536]{1,0:T(8,128)(2,1)S(1)}, bf16[160,1536]{1,0:T(8,128)(2,1)S(1)}, u32[]{:S(2)}, u32[]{:S(2)}) %collective-permute-start.32) | collective-permute-done | bytes 491552 | tf_op jit(solution)/shard_map/ppermute | solution.py:81
  460.2 10.4 %mid_grads.1 = bf16[8,4,48,1664]{3,2,1,0:T(8,128)(2,1)} custom-call(bf16[272,1536]{1,0:T(8,128)(2,1)} %pad.22.cond_ref, bf16[272,384]{1,0:T(8,128)(2,1)} %get-tuple-element.99.dk_ref, bf16[272,384]{1,0:T(8,128)(2,1)} %get-tuple-element.100.dv_ref, bf16[1280,1536]{1,0:T(8,128)(2,1)} %copy-done.23, bf16[1280,384]{1,0:T(8,128)(2,1)} %get-tuple-element.98.dq_ref, ...), custom_call_target="tpu_custom_call" | custom-call | flops 3661627392 | bytes 13811712 | tf_op jit(solution)/shard_map/mid_grads/pallas_call | solution.py:585
  481.1 10.9 %convolution_convert_fusion = bf16[1280,1536]{1,0:T(8,128)(2,1)} fusion(bf16[1280,1536]{1,0:T(8,128)(2,1)} %get-tuple-element.104, bf16[1536,1536]{1,0:T(8,128)(2,1)} %all-gather.11.cloned.1.call-done.refs_4_), kind=kOutput, calls=%fused_computation.7 | convolution fusion | flops 6041763840 | bytes 12582912 | tf_op jit(solution)/shard_map/dot_general | solution.py:63
  520.6 29.3 %back_self.1 = (bf16[1280,384]{1,0:T(8,128)(2,1)}, bf16[1280,384]{1,0:T(8,128)(2,1)}, bf16[1280,384]{1,0:T(8,128)(2,1)}) custom-call(bf16[1280,384]{1,0:T(8,128)(2,1)} %get-tuple-element.109.refs_0_, bf16[1280,384]{1,0:T(8,128)(2,1)} %get-tuple-element.110.refs_1_, bf16[1280,384]{1,0:T(8,128)(2,1)} %get-tuple-element.111.refs_2_, ...), custom_call_target="tpu_custom_call" | custom-call | flops 12582912000 | bytes 11796480 | tf_op jit(solution)/shard_map/back_self/pallas_call | solution.py:371
  550.9 14.2 %self_grads.1 = bf16[8,4,48,1664]{3,2,1,0:T(8,128)(2,1)} custom-call(bf16[1280,1536]{1,0:T(8,128)(2,1)} %copy-done.13, bf16[1280,384]{1,0:T(8,128)(2,1)} %get-tuple-element.124.dq_ref, bf16[1280,384]{1,0:T(8,128)(2,1)} %get-tuple-element.125.dk_ref, bf16[1280,384]{1,0:T(8,128)(2,1)} %get-tuple-element.126.dv_ref, bf16[1536,1280]{1,0:T(8,128)(2,1)} %bitcast.114, ...), custom_call_target="tpu_custom_call" | custom-call | flops 6039797760 | bytes 12582912 | tf_op jit(solution)/shard_map/self_grads/pallas_call | solution.py:643
  599.9 16.0 %collective-permute-done.50 = bf16[260,768]{1,0:T(8,128)(2,1)S(1)} collective-permute-done((bf16[260,768]{1,0:T(8,128)(2,1)}, bf16[260,768]{1,0:T(8,128)(2,1)S(1)}, u32[]{:S(2)}, u32[]{:S(2)}) %collective-permute-start.50) | collective-permute-done | bytes 399392 | tf_op jit(solution)/shard_map/ppermute | solution.py:81
  (506 shorter events, 337.4 us)
Async XLA Ops:
  14.1 65.4 %all-gather.5.cloned.1.call-start = ((), (), s32[]{:S(2)}) async-start(), calls=%async_computation.9 | async-start | bytes 5750784 | tf_op jit(solution)/shard_map/all_gather | solution.py:813
  27.9 142.6 %all-gather.7.cloned.1.call-start = ((), (), s32[]{:S(2)}) async-start(), calls=%async_computation.10 | async-start | bytes 5308416 | tf_op jit(solution)/shard_map/all_gather | solution.py:823
  34.9 249.4 %all-gather.11.cloned.1.call-start = ((), (), s32[]{:S(2)}) async-start(), calls=%async_computation.12 | async-start | bytes 5308416 | tf_op jit(solution)/shard_map/all_gather | solution.py:845
  39.8 23.4 %collective-permute-start = (bf16[320,1536]{1,0:T(8,128)(2,1)S(1)}, bf16[320,1536]{1,0:T(8,128)(2,1)S(1)}, u32[]{:S(2)}, u32[]{:S(2)}) collective-permute-start(bf16[320,1536]{1,0:T(8,128)(2,1)S(1)} %bitcast.133), channel_id=1, source_target_pairs={{0,8},{8,0},{16,24},{24,16},{1,9},{9,1},{17,25},{25,17},{2,10},{10... | collective-permute-start | bytes 2949128 | tf_op jit(solution)/shard_map/ppermute | solution.py:81
  94.1 32.4 %all-to-all-start.2 = ((bf16[4,48,3072]{2,1,0:T(8,128)(2,1)}), bf16[4,48,3072]{2,1,0:T(8,128)(2,1)S(1)}, u32[]{:S(2)}, u32[]{:S(2)}) async-start(bf16[4,48,3072]{2,1,0:T(8,128)(2,1)} %reshape.403), calls=%async_computation.2 | async-start | bytes 2359296 | tf_op jit(solution)/shard_map/all_to_all | solution.py:706
  97.7 186.7 %all-gather.9.cloned.1.call-start = ((), (), s32[]{:S(2)}) async-start(), calls=%async_computation.11 | async-start | bytes 10616832 | tf_op jit(solution)/shard_map/all_gather | solution.py:849
  98.0 26.9 %collective-permute-start.6 = (bf16[160,1536]{1,0:T(8,128)(2,1)S(1)}, bf16[160,1536]{1,0:T(8,128)(2,1)S(1)}, u32[]{:S(2)}, u32[]{:S(2)}) collective-permute-start(bf16[160,1536]{1,0:T(8,128)(2,1)S(1)} %slice.393), channel_id=1, source_target_pairs={{0,8},{8,0},{16,24},{24,16},{1,9},{9,1},{17,25},{25,17},{2,10},{10... | collective-permute-start | bytes 1474568 | tf_op jit(solution)/shard_map/ppermute | solution.py:81
  100.0 24.9 %collective-permute-start.7 = (bf16[160,1536]{1,0:T(8,128)(2,1)S(1)}, bf16[160,1536]{1,0:T(8,128)(2,1)S(1)}, u32[]{:S(2)}, u32[]{:S(2)}) collective-permute-start(bf16[160,1536]{1,0:T(8,128)(2,1)S(1)} %slice.394), channel_id=1, source_target_pairs={{0,16},{8,24},{16,0},{24,8},{1,17},{9,25},{17,1},{25,9},{2,18},{10... | collective-permute-start | bytes 1474568 | tf_op jit(solution)/shard_map/ppermute | solution.py:81
  127.5 270.0 %reduce-scatter.5.cloned.1.call-start = ((), (), s32[]{:S(2)}) async-start(), calls=%async_computation.13 | async-start | bytes 5308416 | tf_op jit(solution)/shard_map/reduce_scatter | solution.py:878
  168.5 23.7 %collective-permute-start.12 = (bf16[320,1536]{1,0:T(8,128)(2,1)}, bf16[320,1536]{1,0:T(8,128)(2,1)}, u32[]{:S(2)}, u32[]{:S(2)}) collective-permute-start(bf16[320,1536]{1,0:T(8,128)(2,1)} %get-tuple-element.275), channel_id=1, source_target_pairs={{0,8},{8,0},{16,24},{24,16},{1,9},{9,1},{17,25},{25,17},{2,10},{10... | collective-permute-start | bytes 2949128 | tf_op jit(solution)/shard_map/ppermute | solution.py:81
  226.8 22.4 %collective-permute-start.17 = (bf16[320,1536]{1,0:T(8,128)(2,1)S(1)}, bf16[320,1536]{1,0:T(8,128)(2,1)S(1)}, u32[]{:S(2)}, u32[]{:S(2)}) collective-permute-start(bf16[320,1536]{1,0:T(8,128)(2,1)S(1)} %pad_maximum_fusion.3), channel_id=1, source_target_pairs={{0,8},{8,0},{16,24},{24,16},{1,9},{9,1},{17,25},{25,17},{2,10},{10... | collective-permute-start | bytes 2949128 | tf_op jit(solution)/shard_map/ppermute | solution.py:81
  332.3 174.0 %reduce-scatter.7.cloned.1.call-start = ((), (), s32[]{:S(2)}) async-start(), calls=%async_computation.14 | async-start | bytes 10616832 | tf_op jit(solution)/shard_map/reduce_scatter | solution.py:886
  397.5 167.6 %reduce-scatter.9.cloned.1.call-start = ((), (), s32[]{:S(2)}) async-start(), calls=%async_computation.15 | async-start | bytes 5750784 | tf_op jit(solution)/shard_map/reduce_scatter | solution.py:913
  445.7 25.0 %collective-permute-start.33 = (bf16[320,1536]{1,0:T(8,128)(2,1)}, bf16[320,1536]{1,0:T(8,128)(2,1)}, u32[]{:S(2)}, u32[]{:S(2)}) collective-permute-start(bf16[320,1536]{1,0:T(8,128)(2,1)} %pad_maximum_fusion.7), channel_id=1, source_target_pairs={{0,8},{8,0},{16,24},{24,16},{1,9},{9,1},{17,25},{25,17},{2,10},{10... | collective-permute-start | bytes 2949128 | tf_op jit(solution)/shard_map/ppermute | solution.py:81
  513.0 37.8 %collective-permute-start.40 = (bf16[160,1536]{1,0:T(8,128)(2,1)}, bf16[160,1536]{1,0:T(8,128)(2,1)}, u32[]{:S(2)}, u32[]{:S(2)}) collective-permute-start(bf16[160,1536]{1,0:T(8,128)(2,1)} %get-tuple-element.278), channel_id=1, source_target_pairs={{0,8},{8,0},{16,24},{24,16},{1,9},{9,1},{17,25},{25,17},{2,10},{10... | collective-permute-start | bytes 1474568 | tf_op jit(solution)/shard_map/ppermute | solution.py:81
  513.7 37.1 %collective-permute-start.41 = (bf16[160,1536]{1,0:T(8,128)(2,1)}, bf16[160,1536]{1,0:T(8,128)(2,1)S(1)}, u32[]{:S(2)}, u32[]{:S(2)}) collective-permute-start(bf16[160,1536]{1,0:T(8,128)(2,1)} %get-tuple-element.281), channel_id=1, source_target_pairs={{0,8},{8,0},{16,24},{24,16},{1,9},{9,1},{17,25},{25,17},{2,10},{10... | collective-permute-start | bytes 1474568 | tf_op jit(solution)/shard_map/ppermute | solution.py:81
  515.0 35.8 %collective-permute-start.42 = (bf16[160,1536]{1,0:T(8,128)(2,1)S(1)}, bf16[160,1536]{1,0:T(8,128)(2,1)S(1)}, u32[]{:S(2)}, u32[]{:S(2)}) collective-permute-start(bf16[160,1536]{1,0:T(8,128)(2,1)S(1)} %get-tuple-element.280), channel_id=1, source_target_pairs={{0,16},{8,24},{16,0},{24,8},{1,17},{9,25},{17,1},{25,9},{2,18},{10... | collective-permute-start | bytes 1474568 | tf_op jit(solution)/shard_map/ppermute | solution.py:81
  515.4 35.4 %collective-permute-start.43 = (bf16[160,1536]{1,0:T(8,128)(2,1)S(1)}, bf16[160,1536]{1,0:T(8,128)(2,1)}, u32[]{:S(2)}, u32[]{:S(2)}) collective-permute-start(bf16[160,1536]{1,0:T(8,128)(2,1)S(1)} %get-tuple-element.279), channel_id=1, source_target_pairs={{0,16},{8,24},{16,0},{24,8},{1,17},{9,25},{17,1},{25,9},{2,18},{10... | collective-permute-start | bytes 1474568 | tf_op jit(solution)/shard_map/ppermute | solution.py:81
  517.0 33.8 %all-to-all-start.3 = ((bf16[4,48,3072]{2,1,0:T(8,128)(2,1)}), bf16[4,48,3072]{2,1,0:T(8,128)(2,1)S(1)}, u32[]{:S(2)}, u32[]{:S(2)}) async-start(bf16[4,48,3072]{2,1,0:T(8,128)(2,1)} %bitcast.165), calls=%async_computation.5 | async-start | bytes 2359296 | tf_op jit(solution)/shard_map/all_to_all | solution.py:706
  520.6 109.9 %reduce-scatter.11.cloned.1.call-start = ((), (), s32[]{:S(2)}) async-start(), calls=%async_computation.16 | async-start | bytes 5750784 | tf_op jit(solution)/shard_map/reduce_scatter | solution.py:926
  582.4 36.8 %collective-permute-start.45 = (bf16[320,1536]{1,0:T(8,128)(2,1)S(1)}, bf16[320,1536]{1,0:T(8,128)(2,1)}, u32[]{:S(2)}, u32[]{:S(2)}) collective-permute-start(bf16[320,1536]{1,0:T(8,128)(2,1)S(1)} %pad_maximum_fusion.9), channel_id=1, source_target_pairs={{0,8},{8,0},{16,24},{24,16},{1,9},{9,1},{17,25},{25,17},{2,10},{10... | collective-permute-start | bytes 2949128 | tf_op jit(solution)/shard_map/ppermute | solution.py:81
  590.4 28.7 %collective-permute-start.47 = (bf16[320,1536]{1,0:T(8,128)(2,1)}, bf16[320,1536]{1,0:T(8,128)(2,1)}, u32[]{:S(2)}, u32[]{:S(2)}) collective-permute-start(bf16[320,1536]{1,0:T(8,128)(2,1)} %pad_maximum_fusion.10), channel_id=1, source_target_pairs={{0,16},{8,24},{16,0},{24,8},{1,17},{9,25},{17,1},{25,9},{2,18},{10... | collective-permute-start | bytes 2949128 | tf_op jit(solution)/shard_map/ppermute | solution.py:81
  592.4 23.5 %collective-permute-start.50 = (bf16[260,768]{1,0:T(8,128)(2,1)}, bf16[260,768]{1,0:T(8,128)(2,1)S(1)}, u32[]{:S(2)}, u32[]{:S(2)}) collective-permute-start(bf16[260,768]{1,0:T(8,128)(2,1)} %get-tuple-element.290), channel_id=1, source_target_pairs={{0,8},{8,0},{16,24},{24,16},{1,9},{9,1},{17,25},{25,17},{2,10},{10... | collective-permute-start | bytes 1198088 | tf_op jit(solution)/shard_map/ppermute | solution.py:81
  594.0 23.0 %collective-permute-start.52 = (bf16[260,768]{1,0:T(8,128)(2,1)}, bf16[260,768]{1,0:T(8,128)(2,1)}, u32[]{:S(2)}, u32[]{:S(2)}) collective-permute-start(bf16[260,768]{1,0:T(8,128)(2,1)} %get-tuple-element.291), channel_id=1, source_target_pairs={{0,16},{8,24},{16,0},{24,8},{1,17},{9,25},{17,1},{25,9},{2,18},{10... | collective-permute-start | bytes 1198088 | tf_op jit(solution)/shard_map/ppermute | solution.py:81
  (118 other events, 1084.2 us)
Sparse Core Ops, SparseCore 0:
  22.8 53.4 all-gather.4
  78.5 50.6 all-gather.6
  130.9 50.5 all-gather.10
  183.5 88.2 all-gather.8
  332.5 53.0 reduce-scatter.4
  397.6 98.7 reduce-scatter.6
  506.5 57.1 reduce-scatter.8
  566.1 57.1 reduce-scatter.10
